TPU v7x, 256 devices: a whole 4x4x8 slice. The times are simulated.
256 devices in a mesh: feat: 4 (over y), rows: 64 (over x, z, core).
Axes of the slice: x: 4, y: 4, z: 8, core: 2. Of those that a mesh axis runs over, the one named last changes fastest.
Arguments:
- features: bfloat16 [16384, 4096], P('rows', 'feat'), may hold values from -16 to 16
- labels: int32 [16384], P('rows'), may hold values from 0 to 639
- inv_gram: float32 [4, 1024, 1024], P('feat'), may hold values from -1 to 1, as said below
Outputs:
- weights: float32 [4096, 640], P(('feat', 'rows'))
- after_block: float32 [4, 16384, 640], P('feat', 'rows')
Inputs may be any that keep to these rules, and one draw needn't show every extreme that they name: Each of the 4 matrices of inv_gram is symmetric.
All inputs are finite; a program needn't handle non-finite values.
Results may differ from a plain program's by a relative error of at most 0.0094.
Values sent between devices are 32-bit elements; how exact they have to be, the bound alone decides.
No kernel may reach another device: no remote copies, remote signals or barrier semaphores. Data moves between devices by JAX's collectives and lax.ppermute only.
A program may use at most 64 MiB of HBM per device.

v0:
```python
import jax
import jax.numpy as jnp
from jax import lax
from jax.sharding import PartitionSpec as P

C = 640
CLS_BLK = 128


def shifted(value, axis, by):
    count = lax.axis_size(axis)
    pairs = [(i, i + by) for i in range(count) if 0 <= i + by < count]
    return lax.ppermute(value, axis, pairs)


def local(features, labels, inv_gram):
    rows_here = features.shape[0]
    block_width = features.shape[1]
    group_total = lax.axis_size("feat")
    shard_total = lax.axis_size("rows")
    feat_index = lax.axis_index("feat")
    shard_index = lax.axis_index("rows")
    row_share = block_width // shard_total
    class_block = CLS_BLK
    wave_total = C // class_block
    class_ids = jnp.arange(C, dtype=jnp.int32)
    onehot = (labels[:, None] == class_ids[None, :]).astype(jnp.float32)
    counts = lax.psum(jnp.sum(onehot, axis=0), "rows")
    count_row = jnp.sum(onehot * counts[None, :], axis=1)
    row_weight = float(rows_here * shard_total) / (C * count_row)
    inverse = inv_gram[0]
    residual = jnp.where(feat_index == 0, onehot, jnp.zeros_like(onehot))
    solved_all = jnp.zeros((row_share, C), jnp.float32)
    own_first = shard_index * row_share
    for segment in range(group_total + wave_total - 1):
        wave_index = segment - feat_index
        active = (wave_index >= 0) & (wave_index < wave_total)
        column_start = jnp.clip(wave_index, 0, wave_total - 1) * class_block
        current = lax.dynamic_slice_in_dim(residual, column_start, class_block, 1)
        scaled = (row_weight[:, None] * current).astype(jnp.bfloat16)
        partial_value = lax.dot_general(
            features, scaled, (((0,), (0,)), ((), ())), preferred_element_type=jnp.float32
        )
        summed = lax.psum(partial_value, "rows")
        solved = jnp.dot(
            inverse, summed, precision=lax.Precision.HIGHEST, preferred_element_type=jnp.float32
        )
        correction = jnp.dot(
            features, solved.astype(jnp.bfloat16), preferred_element_type=jnp.float32
        )
        new_rows = lax.dynamic_slice_in_dim(solved, own_first, row_share, 0)
        updated = current - correction
        residual = jnp.where(
            active, lax.dynamic_update_slice_in_dim(residual, updated, column_start, 1), residual
        )
        solved_all = jnp.where(
            active,
            lax.dynamic_update_slice_in_dim(solved_all, new_rows, column_start, 1),
            solved_all,
        )
        arrived = shifted(updated, "feat", 1)
        incoming = segment - feat_index + 1
        landing = (feat_index >= 1) & (incoming >= 0) & (incoming < wave_total)
        landing_start = jnp.clip(incoming, 0, wave_total - 1) * class_block
        residual = jnp.where(
            landing, lax.dynamic_update_slice_in_dim(residual, arrived, landing_start, 1), residual
        )
    return (solved_all, residual[None])


def solution(mesh):
    in_specs = (P("rows", "feat"), P("rows"), P("feat", None, None))
    out_specs = (P(("feat", "rows"), None), P("feat", "rows", None))
    return jax.shard_map(local, mesh=mesh, in_specs=in_specs, out_specs=out_specs, check_vma=False)
```

profile of v0, /device:TPU:1, one launch (start us, length us, event | category | flops | bytes accessed | tf_op | source)
XLA Modules:
  0.0 1708.1 jit_solution(7271068267111447395)
XLA Ops:
  7.2 0.9 convert_reduce_fusion
  8.1 128.0 %psum.63 = f32[640]{0:T(1024)S(1)} all-reduce(f32[640]{0:T(1024)S(1)} %convert_reduce_fusion), channel_id=1, replica_groups=mesh['feat'=4,'rows'=64] {'rows'}, use_global_device_ids=true, to_apply=%region_1.0 | all-reduce | flops 640 | bytes 5120 | tf_op jit(solution)/shard_map/psum | solution.py:28
  136.1 0.9 select_reduce_fusion
  137.1 1.0 convolution_bitcast_fusion.7
  138.2 179.5 %all-reduce.9.cloned.1.call-done = f32[1024,128]{0,1:T(8,128)} async-done(((f32[1024,128]{0,1:T(8,128)}), f32[1024,128]{0,1:T(8,128)}) %all-reduce.9.cloned.1.call-update) | async-done | bytes 524304 | tf_op jit(solution)/shard_map/psum | solution.py:44
  317.7 6.7 fusion.14
  324.5 0.3 fusion.23
  324.8 3.1 collective-permute-start
  327.9 1.9 collective-permute-done
  329.9 1.0 convolution_bitcast_fusion.6
  331.0 182.4 %all-reduce.11.cloned.1.call-done = f32[1024,128]{0,1:T(8,128)} async-done(((f32[1024,128]{0,1:T(8,128)}), f32[1024,128]{0,1:T(8,128)}) %all-reduce.11.cloned.1.call-update) | async-done | bytes 524304 | tf_op jit(solution)/shard_map/psum | solution.py:44
  513.4 6.7 fusion.12
  520.1 0.3 fusion.22
  520.4 3.1 collective-permute-start.1
  523.6 1.9 collective-permute-done.1
  525.5 1.0 convolution_bitcast_fusion.5
  526.6 0.2 all-reduce.15.cloned.1.call-start
  526.8 182.2 %all-reduce.13.cloned.1.call-done = f32[1024,128]{0,1:T(8,128)} async-done(((f32[1024,128]{0,1:T(8,128)}), f32[1024,128]{0,1:T(8,128)}) %all-reduce.13.cloned.1.call-update) | async-done | bytes 524304 | tf_op jit(solution)/shard_map/psum | solution.py:44
  709.0 6.7 fusion.10
  715.7 0.3 fusion.21
  716.1 3.1 collective-permute-start.2
  719.2 1.9 collective-permute-done.2
  721.1 1.0 convolution_bitcast_fusion.4
  722.2 182.4 %all-reduce.15.cloned.1.call-done = f32[1024,128]{0,1:T(8,128)} async-done(((f32[1024,128]{0,1:T(8,128)}), f32[1024,128]{0,1:T(8,128)}) %all-reduce.15.cloned.1.call-update) | async-done | bytes 524304 | tf_op jit(solution)/shard_map/psum | solution.py:44
  904.6 6.7 fusion.8
  911.4 0.3 fusion.20
  911.7 3.1 collective-permute-start.3
  914.9 1.9 collective-permute-done.3
  916.8 1.0 convolution_bitcast_fusion.3
  917.9 182.4 %all-reduce.17.cloned.1.call-done = f32[1024,128]{0,1:T(8,128)} async-done(((f32[1024,128]{0,1:T(8,128)}), f32[1024,128]{0,1:T(8,128)}) %all-reduce.17.cloned.1.call-update) | async-done | bytes 524304 | tf_op jit(solution)/shard_map/psum | solution.py:44
  1100.3 6.7 fusion.6
  1107.0 0.3 fusion.19
  1107.3 3.1 collective-permute-start.4
  1110.5 1.9 collective-permute-done.4
  1112.4 1.1 convolution_bitcast_fusion.2
  1113.5 0.3 all-reduce.21.cloned.1.call-start
  1113.8 0.1 bitcast_dynamic-update-slice_fusion.1
  1113.9 182.0 %all-reduce.19.cloned.1.call-done = f32[1024,128]{0,1:T(8,128)} async-done(((f32[1024,128]{0,1:T(8,128)}), f32[1024,128]{0,1:T(8,128)}) %all-reduce.19.cloned.1.call-update) | async-done | bytes 524304 | tf_op jit(solution)/shard_map/psum | solution.py:44
  1295.9 6.7 fusion.4
  1302.7 0.3 fusion.18
  1303.0 3.1 collective-permute-start.5
  1306.2 1.9 collective-permute-done.5
  1308.1 1.1 convolution_bitcast_fusion.1
  1309.1 0.0 all-reduce.23.cloned.1.call-start
  1309.2 0.1 fusion.38
  1309.3 0.1 fusion.37
  1309.4 0.9 fusion.36
  1310.3 181.2 %all-reduce.21.cloned.1.call-done = f32[1024,128]{0,1:T(8,128)} async-done(((f32[1024,128]{0,1:T(8,128)}), f32[1024,128]{0,1:T(8,128)}) %all-reduce.21.cloned.1.call-update) | async-done | bytes 524304 | tf_op jit(solution)/shard_map/psum | solution.py:44
  1491.6 6.7 fusion.2
  1498.3 0.3 fusion.17
  1498.6 3.1 collective-permute-start.6
  1501.8 1.9 collective-permute-done.6
  1503.7 1.0 convolution_bitcast_fusion
  1504.8 0.9 fusion.35
  1505.7 0.1 fusion.34
  1505.8 0.1 fusion.33
  1505.9 181.3 %all-reduce.23.cloned.1.call-done = f32[1024,128]{0,1:T(8,128)} async-done(((f32[1024,128]{0,1:T(8,128)}), f32[1024,128]{0,1:T(8,128)}) %all-reduce.23.cloned.1.call-update) | async-done | bytes 524304 | tf_op jit(solution)/shard_map/psum | solution.py:44
  1687.2 6.7 fusion
  1693.9 0.3 fusion.16
  1694.3 0.1 fusion.32
  1694.4 0.8 copy.5
  1695.1 3.1 collective-permute-start.7
  1698.3 1.8 collective-permute-done.7
  1700.2 1.1 copy.6
  (38 shorter events, 0.8 us)
Async XLA Ops:
  7.2 129.9 %copy-start = (bf16[256,1024]{1,0:T(8,128)(2,1)S(1)}, bf16[256,1024]{1,0:T(8,128)(2,1)}, u32[]{:S(2)}) copy-start(bf16[256,1024]{1,0:T(8,128)(2,1)} %param.3) | copy-start | bytes 1572868
  7.2 310.5 %all-reduce.9.cloned.1.call-start = ((), (), s32[]{:S(2)}) async-start(), calls=%async_computation | async-start | bytes 1048576 | tf_op jit(solution)/shard_map/psum | solution.py:44
  138.1 375.3 %all-reduce.11.cloned.1.call-start = ((), (), s32[]{:S(2)}) async-start(), calls=%async_computation.1 | async-start | bytes 1048576 | tf_op jit(solution)/shard_map/psum | solution.py:44
  324.8 5.0 collective-permute-start
  330.9 378.1 %all-reduce.13.cloned.1.call-start = ((), (), s32[]{:S(2)}) async-start(), calls=%async_computation.2 | async-start | bytes 1048576 | tf_op jit(solution)/shard_map/psum | solution.py:44
  520.4 5.0 collective-permute-start.1
  526.6 378.0 %all-reduce.15.cloned.1.call-start = ((), (), s32[]{:S(2)}) async-start(), calls=%async_computation.3 | async-start | bytes 1048576 | tf_op jit(solution)/shard_map/psum | solution.py:44
  716.1 5.0 collective-permute-start.2
  722.2 378.1 %all-reduce.17.cloned.1.call-start = ((), (), s32[]{:S(2)}) async-start(), calls=%async_computation.4 | async-start | bytes 1048576 | tf_op jit(solution)/shard_map/psum | solution.py:44
  911.4 5.4 copy-start.1
  911.7 5.0 collective-permute-start.3
  917.8 378.1 %all-reduce.19.cloned.1.call-start = ((), (), s32[]{:S(2)}) async-start(), calls=%async_computation.5 | async-start | bytes 1048576 | tf_op jit(solution)/shard_map/psum | solution.py:44
  1107.0 5.4 copy-start.2
  1107.3 5.0 collective-permute-start.4
  1113.5 378.1 %all-reduce.21.cloned.1.call-start = ((), (), s32[]{:S(2)}) async-start(), calls=%async_computation.6 | async-start | bytes 1048576 | tf_op jit(solution)/shard_map/psum | solution.py:44
  1303.0 5.0 collective-permute-start.5
  1309.1 378.0 %all-reduce.23.cloned.1.call-start = ((), (), s32[]{:S(2)}) async-start(), calls=%async_computation.7 | async-start | bytes 1048576 | tf_op jit(solution)/shard_map/psum | solution.py:44
  1498.6 5.0 collective-permute-start.6
  1695.1 5.0 collective-permute-start.7
Sparse Core Ops, SparseCore 0:
  138.2 179.4 all-reduce.8
  331.0 182.2 all-reduce.10
  526.7 182.2 all-reduce.12
  722.3 182.2 all-reduce.14
  918.0 182.2 all-reduce.16
  1113.6 182.2 all-reduce.18
  1309.3 182.2 all-reduce.20
  1504.9 182.2 all-reduce.22
where the time goes:
time: 1710 us
  waiting for transfers between devices  1470 us (86%)
  blocking collectives  128 us (7%)
  matrix products  64.7 us (4%)
  starting transfers between devices  25.6 us (1%)
    psum x8, waiting for transfers between devices, local(): summed = lax.psum(partial_value, 'rows')  1450 us
    psum x1, blocking collectives, local(): counts = lax.psum(jnp.sum(onehot, axis=0), 'rows')  128 us
    dot_general x8, matrix products, local(): jnp.dot(inverse, summed, precision=lax.Precision.HIGHEST, preferred_eleme...  53.9 us
  transfers between devices with their start and end apart: 16, of which 16 were waited for; matrix products, arithmetic and copies ran while one was open for 0% of the time, Pallas kernels for 0%

commit v1 on v0

v1 whole, which is shorter than its diff:
```python
import functools

import jax
import jax.numpy as jnp
from jax import lax
from jax.experimental import pallas as pl
from jax.experimental.pallas import tpu as pltpu
from jax.sharding import Mesh, PartitionSpec as P

C = 640
LANES = 128
XZ = ("x", "z")
F32 = jnp.float32
BF16 = jnp.bfloat16
VMEM = pl.BlockSpec(memory_space=pltpu.VMEM)
SMEM = pl.BlockSpec(memory_space=pltpu.SMEM)


def dot(left, right):
    return jnp.dot(left, right, preferred_element_type=F32)


def dot_t(left, right):
    return lax.dot_general(left, right, (((1,), (1,)), ((), ())), preferred_element_type=F32)


def swap_cores(value):
    return lax.ppermute(value, "core", [(0, 1), (1, 0)])


def prepare_kernel(gram_ref, x_ref, zt_ref, xf_ref):
    gram = gram_ref[0]
    high = gram.astype(BF16)
    rest = gram - high.astype(F32)
    mid = rest.astype(BF16)
    low = (rest - mid.astype(F32)).astype(BF16)
    x = x_ref[...]
    zt_ref[...] = (dot_t(low, x) + dot_t(mid, x)) + dot_t(high, x)

    @pl.when(pl.program_id(0) == 0)
    def _():
        xf_ref[...] = x.astype(F32)


def prepare(features, inv_gram, tile=256):
    rows, width = features.shape
    return pl.pallas_call(
        prepare_kernel,
        grid=(width // tile,),
        in_specs=[
            pl.BlockSpec((1, tile, width), lambda i: (0, i, 0)),
            pl.BlockSpec((rows, width), lambda i: (0, 0)),
        ],
        out_specs=[
            pl.BlockSpec((tile, rows), lambda i: (i, 0)),
            pl.BlockSpec((rows, width), lambda i: (0, 0)),
        ],
        out_shape=[
            jax.ShapeDtypeStruct((width, rows), F32),
            jax.ShapeDtypeStruct((rows, width), F32),
        ],
    )(inv_gram, features)


def partial_sum(zt_refs, scaled_halves):
    total = None
    for zt_ref, scaled in zip(zt_refs, scaled_halves):
        zt = zt_ref[0]
        high = zt.astype(BF16)
        low = (zt - high.astype(F32)).astype(BF16)
        part = dot(low, scaled) + dot(high, scaled)
        total = part if total is None else total + part
    return total


def label_parts(lab, slices, width):
    group = jnp.zeros_like(lab)
    for d in range(1, slices):
        group = group + (lab >= d * width).astype(jnp.int32)
    return group, lab - group * width


def first_kernel(slices, slice_ref, lab_ref, labt_ref, za_ref, zb_ref, out_ref):
    width = C // slices
    lab = lab_ref[...]
    rows = lab.shape[0] // 2
    group, low_label = label_parts(lab, slices, width)
    lane = lax.broadcasted_iota(jnp.int32, (lab.shape[0], LANES), 1)
    low_hot = jnp.where(low_label == lane, 1.0, 0.0)
    onehot = jnp.where(group == slice_ref[0], low_hot, 0.0).astype(BF16)
    labt = labt_ref[...]
    first = lax.broadcasted_iota(jnp.int32, (slices, labt.shape[1]), 0) * width
    group_hot = jnp.where((labt >= first) & (labt < first + width), 1.0, 0.0).astype(BF16)
    counts = dot(group_hot, low_hot.astype(BF16))
    total = partial_sum((za_ref, zb_ref), (onehot[:rows], onehot[rows:]))
    chips, deep, _ = out_ref.shape
    out_ref[:, : deep - slices, :] = total.reshape(chips, deep - slices, LANES)
    out_ref[:, deep - slices :, :] = jnp.broadcast_to(counts[None], (chips, slices, LANES))


def middle_kernel(slices, total_rows, slice_ref, in_ref, *out_refs):
    summed = jnp.sum(in_ref[...], axis=0)
    solved_ref, copies_ref = out_refs[0], out_refs[1]
    chunk = solved_ref.shape[0]
    solved = summed[:chunk]
    if len(out_refs) == 3:
        totals = summed[chunk:]
        out_refs[2][...] = totals
        row = lax.broadcasted_iota(jnp.int32, totals.shape, 0)
        mine = jnp.sum(jnp.where(row == slice_ref[0], totals, 0.0), axis=0, keepdims=True)
        scale = jnp.where(mine > 0.0, total_rows / (C * jnp.maximum(mine, 1.0)), 0.0)
        solved = solved * scale.astype(BF16).astype(F32)
    solved_ref[...] = solved
    copies_ref[...] = jnp.broadcast_to(solved[None], copies_ref.shape)


def middle(slices, total_rows, slice_index, arrived, chunk):
    chips, deep, _ = arrived.shape
    shapes = [
        jax.ShapeDtypeStruct((chunk, LANES), F32),
        jax.ShapeDtypeStruct((chips, chunk, LANES), F32),
    ]
    if deep > chunk:
        shapes.append(jax.ShapeDtypeStruct((slices, LANES), F32))
    return pl.pallas_call(
        functools.partial(middle_kernel, slices, total_rows),
        in_specs=[SMEM, VMEM],
        out_specs=[VMEM] * len(shapes),
        out_shape=shapes,
    )(slice_index, arrived)


def update(everyone_ref, xa_ref, xb_ref, residual):
    solved = everyone_ref[...].reshape(-1, LANES).astype(BF16)
    rows = xa_ref.shape[1]
    halves = (
        residual[:rows] - dot(xa_ref[0].astype(BF16), solved),
        residual[rows:] - dot(xb_ref[0].astype(BF16), solved),
    )
    return halves


def second_kernel(
    slices, total_rows, slice_ref, lab_ref, totals_ref, everyone_ref, xa_ref, xb_ref,
    za_ref, zb_ref, residual_ref, weight_ref, out_ref,
):
    width = C // slices
    lab = lab_ref[...]
    group, low_label = label_parts(lab, slices, width)
    lane = lax.broadcasted_iota(jnp.int32, (lab.shape[0], LANES), 1)
    hit = low_label == lane
    spread = jnp.zeros((lab.shape[0], LANES), F32)
    for d in range(slices):
        spread = jnp.where(group == d, totals_ref[d : d + 1, :], spread)
    row_count = jnp.sum(jnp.where(hit, spread, 0.0), axis=1, keepdims=True)
    weight = total_rows / (C * row_count)
    weight_ref[...] = jnp.broadcast_to(weight, weight_ref.shape)
    onehot = jnp.where(hit & (group == slice_ref[0]), 1.0, 0.0)
    halves = update(everyone_ref, xa_ref, xb_ref, onehot)
    rows = xa_ref.shape[1]
    residual_ref[:rows] = halves[0]
    residual_ref[rows:] = halves[1]
    scaled = [
        (weight[k * rows : (k + 1) * rows] * halves[k]).astype(BF16) for k in range(2)
    ]
    total = partial_sum((za_ref, zb_ref), scaled)
    out_ref[...] = total.reshape(out_ref.shape)


def step_kernel(
    everyone_ref, xa_ref, xb_ref, za_ref, zb_ref, old_ref, weight_ref, residual_ref, out_ref
):
    halves = update(everyone_ref, xa_ref, xb_ref, old_ref[...])
    rows = xa_ref.shape[1]
    residual_ref[:rows] = halves[0]
    residual_ref[rows:] = halves[1]
    scaled = [
        (weight_ref[k * rows : (k + 1) * rows] * halves[k]).astype(BF16) for k in range(2)
    ]
    total = partial_sum((za_ref, zb_ref), scaled)
    out_ref[...] = total.reshape(out_ref.shape)


def last_kernel(everyone_ref, xa_ref, xb_ref, old_ref, residual_ref):
    halves = update(everyone_ref, xa_ref, xb_ref, old_ref[...])
    rows = xa_ref.shape[1]
    residual_ref[:rows] = halves[0]
    residual_ref[rows:] = halves[1]


def join_kernel(in_ref, weights_ref, after_ref):
    slices = in_ref.shape[0]
    width = C // slices
    head = weights_ref.shape[0]
    for d in range(slices):
        weights_ref[:, d * width : (d + 1) * width] = in_ref[d, :head, :width]
        after_ref[0, :, d * width : (d + 1) * width] = in_ref[d, head:, :width]


def local(features, labels, inv_gram):
    rows_here, block_width = features.shape
    blocks = lax.axis_size("feat")
    cores = lax.axis_size("core")
    chips = lax.axis_size("x") * lax.axis_size("z")
    slices = blocks * cores
    chunk = block_width // chips
    core = lax.axis_index("core")
    slice_index = (lax.axis_index("feat") * cores + core).astype(jnp.int32)[None]
    total_rows = float(rows_here * chips * cores)
    both = cores * rows_here

    zt_own, x_own = prepare(features, inv_gram)
    zt_mine = lax.all_gather(zt_own, "feat")
    x_mine = lax.all_gather(x_own, "feat")
    zt_other = swap_cores(zt_mine)
    x_other = swap_cores(x_mine)
    lab = jnp.concatenate([labels, swap_cores(labels)])
    lab_column, lab_row = lab[:, None], lab[None, :]

    def z_spec(b):
        return pl.BlockSpec((1, block_width, rows_here), lambda i: (b, 0, 0))

    def x_spec(b):
        return pl.BlockSpec((1, rows_here, block_width), lambda i: (b, 0, 0))

    def whole(*shape):
        return pl.BlockSpec(shape, lambda i: (0,) * len(shape))

    pieces_shape = jax.ShapeDtypeStruct((chips, chunk, LANES), F32)
    rows_shape = jax.ShapeDtypeStruct((both, LANES), F32)
    rows_block = whole(both, LANES)
    pieces_block = whole(chips, chunk, LANES)

    pieces = pl.pallas_call(
        functools.partial(first_kernel, slices),
        grid=(1,),
        in_specs=[SMEM, whole(both, 1), whole(1, both), z_spec(0), z_spec(0)],
        out_specs=whole(chips, chunk + slices, LANES),
        out_shape=jax.ShapeDtypeStruct((chips, chunk + slices, LANES), F32),
    )(slice_index, lab_column, lab_row, zt_mine, zt_other)

    kept_rows = []
    kept_solved = []
    totals = weight = residual = None
    for b in range(blocks):
        arrived = lax.all_to_all(pieces, XZ, 0, 0, tiled=True)
        result = middle(slices, total_rows, slice_index, arrived, chunk)
        kept_solved.append(result[0])
        if b == 0:
            totals = result[2]
        everyone = lax.all_to_all(result[1], XZ, 0, 0, tiled=True)
        if b == 0:
            residual, weight, pieces = pl.pallas_call(
                functools.partial(second_kernel, slices, total_rows),
                grid=(1,),
                in_specs=[SMEM, whole(both, 1), whole(slices, LANES), pieces_block,
                          x_spec(b), x_spec(b), z_spec(b + 1), z_spec(b + 1)],
                out_specs=[rows_block, rows_block, pieces_block],
                out_shape=[rows_shape, rows_shape, pieces_shape],
            )(slice_index, lab_column, totals, everyone, x_mine, x_other, zt_mine, zt_other)
        elif b < blocks - 1:
            residual, pieces = pl.pallas_call(
                step_kernel,
                grid=(1,),
                in_specs=[pieces_block, x_spec(b), x_spec(b), z_spec(b + 1), z_spec(b + 1),
                          rows_block, rows_block],
                out_specs=[rows_block, pieces_block],
                out_shape=[rows_shape, pieces_shape],
            )(everyone, x_mine, x_other, zt_mine, zt_other, residual, weight)
        else:
            residual = pl.pallas_call(
                last_kernel,
                grid=(1,),
                in_specs=[pieces_block, x_spec(b), x_spec(b), rows_block],
                out_specs=rows_block,
                out_shape=rows_shape,
            )(everyone, x_mine, x_other, residual)
        kept_rows.append(residual)

    half = chunk // cores
    sends = []
    for b in range(blocks):
        own = kept_rows[b][:rows_here]
        other = kept_rows[b][rows_here:]
        for k in range(cores):
            sends.append(kept_solved[b][k * half:(k + 1) * half])
            sends.append(jnp.where(core == k, own, other))
    sends = jnp.concatenate(sends, axis=0).reshape(slices, half + rows_here, LANES)
    got = lax.all_to_all(sends, ("feat", "core"), 0, 0, tiled=True)
    return pl.pallas_call(
        join_kernel,
        in_specs=[VMEM],
        out_specs=[VMEM, VMEM],
        out_shape=[
            jax.ShapeDtypeStruct((half, C), F32),
            jax.ShapeDtypeStruct((1, rows_here, C), F32),
        ],
    )(got)


def solution(mesh):
    sizes = dict(mesh.shape)
    fine = Mesh(mesh.devices.reshape(sizes["feat"], 4, 8, 2), ("feat", "x", "z", "core"))
    rows = ("x", "z", "core")
    in_specs = (P(rows, "feat"), P(rows), P("feat", None, None))
    out_specs = (P(("feat",) + rows, None), P("feat", rows, None))
    return jax.shard_map(local, mesh=fine, in_specs=in_specs, out_specs=out_specs, check_vma=False)
```

time: 1710 us -> 375 us (0.22)
  waiting for transfers between devices: 1470 us -> 167 us
  matrix products: 64.7 us -> 0 us
  Pallas kernels: 0 us -> 36 us
    psum x8 -> x0, waiting for transfers between devices: 1450 us -> none  [local(): summed = lax.psum(partial_value, 'rows')]
    psum x1 -> x0, blocking collectives: 128 us -> none  [local(): counts = lax.psum(jnp.sum(onehot, axis=0), 'rows')]
    all_to_all x0 -> x5, blocking collectives: none -> 115 us  [the longest x3 69.9 us: local(): arrived = lax.all_to_all(pieces, XZ, 0, 0, tiled=True)]
    all_gather x0 -> x2, waiting for transfers between devices: none -> 106 us  [the longest x1 53.8 us: local(): zt_mine = lax.all_gather(zt_own, 'feat')]
    dot_general x24 -> x0, matrix products: 64.7 us -> none  [the longest x8 53.9 us: local(): jnp.dot(inverse, summed, precision=lax.Precision.HIGHEST, preferred_eleme...]
    all_to_all x0 -> x4, waiting for transfers between devices: none -> 53 us  [the longest x3 40 us: local(): everyone = lax.all_to_all(result[1], XZ, 0, 0, tiled=True)]
    pallas_call x0 -> x11, Pallas kernels: none -> 36 us  [the longest x2 8.66 us: local(): pl.pallas_call(step_kernel, grid=(1,), in_specs=[pieces_block, x_spec(b),...]
    all_to_all x0 -> x4, starting transfers between devices: none -> 33.8 us  [the longest x3 25.2 us: local(): everyone = lax.all_to_all(result[1], XZ, 0, 0, tiled=True)]
  transfers between devices with their start and end apart: 16 -> 9, of which waited for: 16 -> 7; matrix products, arithmetic and copies ran while one was open for 0% -> 0% of each run, Pallas kernels for 0% -> 1%
where the time goes in v1:
time: 375 us; the launch traced here: 374 us
  waiting for transfers between devices  167 us (45%)
  blocking collectives  115 us (31%)
  Pallas kernels  36 us (10%)
  starting transfers between devices  35.6 us (9%)
  between operations  14.3 us (4%)
  local copies, waits for them, and re-layouts  4.13 us (1%)
    all_to_all x3, blocking collectives, local(): arrived = lax.all_to_all(pieces, XZ, 0, 0, tiled=True)  69.9 us
    all_gather x1, waiting for transfers between devices, local(): zt_mine = lax.all_gather(zt_own, 'feat')  53.8 us
    all_gather x1, waiting for transfers between devices, local(): x_mine = lax.all_gather(x_own, 'feat')  52.1 us
    all_to_all x3, waiting for transfers between devices, local(): everyone = lax.all_to_all(result[1], XZ, 0, 0, tiled=True)  40 us
    all_to_all x3, starting transfers between devices, local(): everyone = lax.all_to_all(result[1], XZ, 0, 0, tiled=True)  25.2 us
    all_to_all x1, blocking collectives, local(): got = lax.all_to_all(sends, ('feat', 'core'), 0, 0, tiled=True)  24.3 us
    all_to_all x1, blocking collectives, local(): everyone = lax.all_to_all(result[1], XZ, 0, 0, tiled=True)  21 us
    all_to_all x1, waiting for transfers between devices, local(): arrived = lax.all_to_all(pieces, XZ, 0, 0, tiled=True)  12.9 us
  transfers between devices with their start and end apart: 9, of which 7 were waited for; matrix products, arithmetic and copies ran while one was open for 0% of the time, Pallas kernels for 1%

profile of v1, /device:TPU:1, one launch (start us, length us, event | category | flops | bytes accessed | tf_op | source)
XLA Modules:
  0.0 373.9 jit_solution(15104877441814801652)
XLA Ops:
  7.2 0.0 all-gather.5.cloned.1.call-start
  7.2 5.8 %shard_map.50 = (f32[1024,256]{1,0:T(8,128)}, f32[256,1024]{1,0:T(8,128)}) custom-call(f32[1,1024,1024]{2,1,0:T(8,128)} %gram_ref.1, bf16[256,1024]{1,0:T(8,128)(2,1)} %x_ref.1), custom_call_target="tpu_custom_call" | custom-call | tf_op jit(solution)/shard_map/pallas_call | solution.py:47
  13.0 0.0 all-gather.5.cloned.1.call-update
  13.1 0.0 all-gather.7.cloned.1.call-start
  13.1 0.7 all-gather.7.cloned.1.call-update
  13.8 53.8 %all-gather.5.cloned.1.call-done = f32[4096,256]{1,0:T(8,128)} async-done(((f32[1024,256]{1,0:T(8,128)}), f32[4096,256]{1,0:T(8,128)}) %all-gather.5.cloned.1.call-update) | async-done | bytes 4194320 | tf_op jit(solution)/shard_map/all_gather | solution.py:213
  67.6 0.8 collective-permute-start.1
  68.5 52.1 %all-gather.7.cloned.1.call-done = f32[1024,1024]{1,0:T(8,128)} async-done(((f32[256,1024]{1,0:T(8,128)}), f32[1024,1024]{1,0:T(8,128)}) %all-gather.7.cloned.1.call-update) | async-done | bytes 4194320 | tf_op jit(solution)/shard_map/all_gather | solution.py:214
  120.6 0.8 collective-permute-start.2
  121.4 0.0 copy-done.12
  121.4 0.0 collective-permute-start
  121.4 7.1 %collective-permute-done = s32[256]{0:T(256)S(1)} collective-permute-done((s32[256]{0:T(256)S(1)}, s32[256]{0:T(256)S(1)}, u32[]{:S(2)}, u32[]{:S(2)}) %collective-permute-start) | collective-permute-done | bytes 1056 | tf_op jit(solution)/shard_map/ppermute | solution.py:28
  128.6 0.0 copy-start.11
  128.6 0.9 copy.5.lab_ref
  129.4 0.0 collective-permute-done.1.zb_ref
  129.4 0.0 copy-done.11
  129.4 3.5 shard_map.51
  132.9 26.5 %all_to_all.45.in_ref = f32[32,40,128]{2,1,0:T(8,128)} all-to-all(f32[32,40,128]{2,1,0:T(8,128)} %shard_map.51), channel_id=1, replica_groups=mesh['feat'=4,'x'=4,'z'=8,'core'=2] {'x','z'}, dimensions={0} | all-to-all | bytes 1310720 | tf_op jit(solution)/shard_map/all_to_all | solution.py:246
  159.5 2.0 shard_map.52
  161.5 8.1 %all-to-all-start.1 = ((f32[32,32,128]{2,1,0:T(8,128)}), f32[32,32,128]{2,1,0:T(8,128)S(1)}, u32[]{:S(2)}, u32[]{:S(2)}) async-start(f32[32,32,128]{2,1,0:T(8,128)} %get-tuple-element.23), calls=%async_computation.1 | async-start | bytes 1048576 | tf_op jit(solution)/shard_map/all_to_all | solution.py:251
  169.6 0.0 collective-permute-done.2.xb_ref
  169.6 14.2 %all-to-all-done.1.everyone_ref = f32[32,32,128]{2,1,0:T(8,128)S(1)} async-done(((f32[32,32,128]{2,1,0:T(8,128)}), f32[32,32,128]{2,1,0:T(8,128)S(1)}, u32[]{:S(2)}, u32[]{:S(2)}) %all-to-all-start.1) | async-done | bytes 524320 | tf_op jit(solution)/shard_map/all_to_all | solution.py:251
  183.8 0.0 copy-start.5
  183.8 0.8 copy-done.5
  184.6 4.9 %shard_map.53 = (f32[512,128]{1,0:T(8,128)}, f32[512,128]{1,0:T(8,128)}, f32[32,32,128]{2,1,0:T(8,128)}) custom-call(s32[1]{0:T(128)} %bitcast.slice_ref, s32[512,1]{1,0:T(8,128)} %copy.5.lab_ref, f32[8,128]{1,0:T(8,128)} %get-tuple-element.22.totals_ref, f32[32,32,128]{2,1,0:T(8,128)} %copy-done.5, f32[4,256,1024]{2,1,0:T(8,128)} %bitcast.7, ...), custom_call_target="tpu_custom_call" | custom-call | tf_op jit(solution)/shard_map/pallas_call | solution.py:253
  189.5 21.8 %all_to_all.46.in_ref = f32[32,32,128]{2,1,0:T(8,128)} all-to-all(f32[32,32,128]{2,1,0:T(8,128)} %get-tuple-element.26), channel_id=1, replica_groups=mesh['feat'=4,'x'=4,'z'=8,'core'=2] {'x','z'}, dimensions={0} | all-to-all | bytes 1048576 | tf_op jit(solution)/shard_map/all_to_all | solution.py:246
  211.3 1.9 shard_map.54
  213.2 21.0 %all_to_all.47.everyone_ref = f32[32,32,128]{2,1,0:T(8,128)} all-to-all(f32[32,32,128]{2,1,0:T(8,128)} %get-tuple-element.28), channel_id=1, replica_groups=mesh['feat'=4,'x'=4,'z'=8,'core'=2] {'x','z'}, dimensions={0} | all-to-all | bytes 1048576 | tf_op jit(solution)/shard_map/all_to_all | solution.py:251
  234.2 4.3 %shard_map.55 = (f32[512,128]{1,0:T(8,128)}, f32[32,32,128]{2,1,0:T(8,128)}) custom-call(f32[32,32,128]{2,1,0:T(8,128)} %all_to_all.47.everyone_ref, f32[4,256,1024]{2,1,0:T(8,128)} %bitcast.8, f32[4,256,1024]{2,1,0:T(8,128)} %collective-permute-done.2.xb_ref, f32[4,1024,256]{2,1,0:T(8,128)} %bitcast.14, f32[4,1024,256]{2,1,0:T(8,128)} %collective-permute-done.1.zb_ref, ...), custom_call_target="tpu_custom_call" | custom-call | tf_op jit(solution)/shard_map/pallas_call | solution.py:262
  238.5 0.0 copy-start.9
  238.5 0.0 copy-start
  238.5 21.6 %all_to_all.48.in_ref = f32[32,32,128]{2,1,0:T(8,128)} all-to-all(f32[32,32,128]{2,1,0:T(8,128)} %get-tuple-element.31), channel_id=1, replica_groups=mesh['feat'=4,'x'=4,'z'=8,'core'=2] {'x','z'}, dimensions={0} | all-to-all | bytes 1048576 | tf_op jit(solution)/shard_map/all_to_all | solution.py:246
  260.1 1.9 shard_map.56
  262.0 8.6 %all-to-all-start.5 = ((f32[32,32,128]{2,1,0:T(8,128)}), f32[32,32,128]{2,1,0:T(8,128)S(1)}, u32[]{:S(2)}, u32[]{:S(2)}) async-start(f32[32,32,128]{2,1,0:T(8,128)} %get-tuple-element.33), calls=%async_computation.5 | async-start | bytes 1048576 | tf_op jit(solution)/shard_map/all_to_all | solution.py:251
  270.7 0.0 copy-done.9
  270.7 0.0 copy-done
  270.7 12.9 %all-to-all-done.5.everyone_ref = f32[32,32,128]{2,1,0:T(8,128)S(1)} async-done(((f32[32,32,128]{2,1,0:T(8,128)}), f32[32,32,128]{2,1,0:T(8,128)S(1)}, u32[]{:S(2)}, u32[]{:S(2)}) %all-to-all-start.5) | async-done | bytes 524320 | tf_op jit(solution)/shard_map/all_to_all | solution.py:251
  283.7 0.0 copy-start.3
  283.7 0.8 copy-done.3
  284.4 4.3 %shard_map.57 = (f32[512,128]{1,0:T(8,128)}, f32[32,32,128]{2,1,0:T(8,128)}) custom-call(f32[32,32,128]{2,1,0:T(8,128)} %copy-done.3, f32[4,256,1024]{2,1,0:T(8,128)} %bitcast.9, f32[4,256,1024]{2,1,0:T(8,128)} %collective-permute-done.2.xb_ref, f32[4,1024,256]{2,1,0:T(8,128)} %bitcast.15, f32[4,1024,256]{2,1,0:T(8,128)} %collective-permute-done.1.zb_ref, ...), custom_call_target="tpu_custom_call" | custom-call | tf_op jit(solution)/shard_map/pallas_call | solution.py:262
  288.8 0.0 copy-start.8
  288.8 0.0 copy-start.1
  288.8 8.6 %all-to-all-start.6 = ((f32[32,32,128]{2,1,0:T(8,128)}), f32[32,32,128]{2,1,0:T(8,128)S(1)}, u32[]{:S(2)}, u32[]{:S(2)}) async-start(f32[32,32,128]{2,1,0:T(8,128)} %get-tuple-element.35), calls=%async_computation.6 | async-start | bytes 1048576 | tf_op jit(solution)/shard_map/all_to_all | solution.py:246
  297.4 0.0 copy-done.8
  297.4 0.0 copy-done.1
  297.5 0.0 copy-start.7
  297.5 0.0 copy-start.2
  297.5 12.9 %all-to-all-done.6.in_ref = f32[32,32,128]{2,1,0:T(8,128)S(1)} async-done(((f32[32,32,128]{2,1,0:T(8,128)}), f32[32,32,128]{2,1,0:T(8,128)S(1)}, u32[]{:S(2)}, u32[]{:S(2)}) %all-to-all-start.6) | async-done | bytes 524320 | tf_op jit(solution)/shard_map/all_to_all | solution.py:246
  310.5 0.0 copy-start.6
  310.5 0.8 copy-done.6
  311.3 2.0 shard_map.58
  313.2 0.0 copy-start.10
  313.2 8.5 %all-to-all-start.7 = ((f32[32,32,128]{2,1,0:T(8,128)}), f32[32,32,128]{2,1,0:T(8,128)S(1)}, u32[]{:S(2)}, u32[]{:S(2)}) async-start(f32[32,32,128]{2,1,0:T(8,128)} %get-tuple-element.37), calls=%async_computation.7 | async-start | bytes 1048576 | tf_op jit(solution)/shard_map/all_to_all | solution.py:251
  321.7 0.0 copy-done.7
  321.7 0.0 copy-done.2
  321.8 0.0 copy-done.10
  321.8 12.9 %all-to-all-done.7.everyone_ref = f32[32,32,128]{2,1,0:T(8,128)S(1)} async-done(((f32[32,32,128]{2,1,0:T(8,128)}), f32[32,32,128]{2,1,0:T(8,128)S(1)}, u32[]{:S(2)}, u32[]{:S(2)}) %all-to-all-start.7) | async-done | bytes 524320 | tf_op jit(solution)/shard_map/all_to_all | solution.py:251
  334.7 0.0 copy-start.4
  334.7 0.8 copy-done.4
  335.5 2.9 shard_map.59
  338.4 1.0 select_dynamic-update-slice_fusion.1
  339.4 1.0 select_dynamic-update-slice_fusion
  340.4 24.3 %all_to_all.49.in_ref = f32[8,272,128]{2,1,0:T(8,128)} all-to-all(f32[8,272,128]{2,1,0:T(8,128)S(1)} %bitcast.16), channel_id=1, replica_groups=mesh['feat'=4,'x'=4,'z'=8,'core'=2] {'feat','core'}, dimensions={0} | all-to-all | bytes 2228224 | tf_op jit(solution)/shard_map/all_to_all | solution.py:289
  364.7 2.4 shard_map.60
  (18 shorter events, 0.2 us)
Async XLA Ops:
  7.2 60.5 %all-gather.5.cloned.1.call-start = ((), (), s32[]{:S(2)}) async-start(), calls=%async_computation.9 | async-start | bytes 5242880 | tf_op jit(solution)/shard_map/all_gather | solution.py:213
  13.0 108.4 %copy-start.12 = (s32[256]{0:T(256)S(1)}, s32[256]{0:T(256)}, u32[]{:S(2)}) copy-start(s32[256]{0:T(256)} %param.4) | copy-start | bytes 3076
  13.1 107.5 %all-gather.7.cloned.1.call-start = ((), (), s32[]{:S(2)}) async-start(), calls=%async_computation.10 | async-start | bytes 5242880 | tf_op jit(solution)/shard_map/all_gather | solution.py:214
  67.6 61.8 %collective-permute-start.1 = (f32[4,1024,256]{2,1,0:T(8,128)}, f32[4,1024,256]{2,1,0:T(8,128)}, u32[]{:S(2)}, u32[]{:S(2)}) collective-permute-start(f32[4,1024,256]{2,1,0:T(8,128)} %bitcast.11), channel_id=1, source_target_pairs={{0,1},{1,0},{2,3},{3,2},{4,5},{5,4},{6,7},{7,6},{8,9},{9,8},{10,11... | collective-permute-start | bytes 12582920 | tf_op jit(solution)/shard_map/ppermute | solution.py:28
  120.6 49.0 %collective-permute-start.2 = (f32[4,256,1024]{2,1,0:T(8,128)}, f32[4,256,1024]{2,1,0:T(8,128)}, u32[]{:S(2)}, u32[]{:S(2)}) collective-permute-start(f32[4,256,1024]{2,1,0:T(8,128)} %bitcast.6), channel_id=1, source_target_pairs={{0,1},{1,0},{2,3},{3,2},{4,5},{5,4},{6,7},{7,6},{8,9},{9,8},{10,11... | collective-permute-start | bytes 12582920 | tf_op jit(solution)/shard_map/ppermute | solution.py:28
  121.4 7.1 %collective-permute-start = (s32[256]{0:T(256)S(1)}, s32[256]{0:T(256)S(1)}, u32[]{:S(2)}, u32[]{:S(2)}) collective-permute-start(s32[256]{0:T(256)S(1)} %copy-done.12), channel_id=1, source_target_pairs={{0,1},{1,0},{2,3},{3,2},{4,5},{5,4},{6,7},{7,6},{8,9},{9,8},{10,11... | collective-permute-start | bytes 3080 | tf_op jit(solution)/shard_map/ppermute | solution.py:28
  128.6 0.9 copy-start.11
  161.5 22.3 %all-to-all-start.1 = ((f32[32,32,128]{2,1,0:T(8,128)}), f32[32,32,128]{2,1,0:T(8,128)S(1)}, u32[]{:S(2)}, u32[]{:S(2)}) async-start(f32[32,32,128]{2,1,0:T(8,128)} %get-tuple-element.23), calls=%async_computation.1 | async-start | bytes 1048576 | tf_op jit(solution)/shard_map/all_to_all | solution.py:251
  183.8 0.8 copy-start.5
  238.5 32.2 %copy-start.9 = (f32[32,128]{1,0:T(8,128)S(1)}, f32[32,128]{1,0:T(8,128)}, u32[]{:S(2)}) copy-start(f32[32,128]{1,0:T(8,128)} %get-tuple-element.21) | copy-start | bytes 49156
  238.5 32.2 %copy-start = (f32[512,128]{1,0:T(8,128)S(1)}, f32[512,128]{1,0:T(8,128)}, u32[]{:S(2)}) copy-start(f32[512,128]{1,0:T(8,128)} %get-tuple-element.25.old_ref) | copy-start | bytes 786436
  262.0 21.6 %all-to-all-start.5 = ((f32[32,32,128]{2,1,0:T(8,128)}), f32[32,32,128]{2,1,0:T(8,128)S(1)}, u32[]{:S(2)}, u32[]{:S(2)}) async-start(f32[32,32,128]{2,1,0:T(8,128)} %get-tuple-element.33), calls=%async_computation.5 | async-start | bytes 1048576 | tf_op jit(solution)/shard_map/all_to_all | solution.py:251
  283.7 0.8 copy-start.3
  288.8 8.7 %copy-start.8 = (f32[32,128]{1,0:T(8,128)S(1)}, f32[32,128]{1,0:T(8,128)}, u32[]{:S(2)}) copy-start(f32[32,128]{1,0:T(8,128)} %get-tuple-element.27) | copy-start | bytes 49156
  288.8 8.7 %copy-start.1 = (f32[512,128]{1,0:T(8,128)S(1)}, f32[512,128]{1,0:T(8,128)}, u32[]{:S(2)}) copy-start(f32[512,128]{1,0:T(8,128)} %get-tuple-element.30.old_ref) | copy-start | bytes 786436
  288.8 21.7 %all-to-all-start.6 = ((f32[32,32,128]{2,1,0:T(8,128)}), f32[32,32,128]{2,1,0:T(8,128)S(1)}, u32[]{:S(2)}, u32[]{:S(2)}) async-start(f32[32,32,128]{2,1,0:T(8,128)} %get-tuple-element.35), calls=%async_computation.6 | async-start | bytes 1048576 | tf_op jit(solution)/shard_map/all_to_all | solution.py:246
  297.5 24.2 %copy-start.7 = (f32[32,128]{1,0:T(8,128)S(1)}, f32[32,128]{1,0:T(8,128)}, u32[]{:S(2)}) copy-start(f32[32,128]{1,0:T(8,128)} %get-tuple-element.32) | copy-start | bytes 49156
  297.5 24.3 %copy-start.2 = (f32[512,128]{1,0:T(8,128)S(1)}, f32[512,128]{1,0:T(8,128)}, u32[]{:S(2)}) copy-start(f32[512,128]{1,0:T(8,128)} %get-tuple-element.34.old_ref) | copy-start | bytes 786436
  310.5 0.8 copy-start.6
  313.2 8.6 %copy-start.10 = (f32[32,128]{1,0:T(8,128)S(1)}, f32[32,128]{1,0:T(8,128)}, u32[]{:S(2)}) copy-start(f32[32,128]{1,0:T(8,128)} %get-tuple-element.36) | copy-start | bytes 49156
  313.2 21.5 %all-to-all-start.7 = ((f32[32,32,128]{2,1,0:T(8,128)}), f32[32,32,128]{2,1,0:T(8,128)S(1)}, u32[]{:S(2)}, u32[]{:S(2)}) async-start(f32[32,32,128]{2,1,0:T(8,128)} %get-tuple-element.37), calls=%async_computation.7 | async-start | bytes 1048576 | tf_op jit(solution)/shard_map/all_to_all | solution.py:251
  334.7 0.8 copy-start.4
Sparse Core Ops, SparseCore 0:
  13.2 54.3 all-gather.4
  69.4 51.1 all-gather.6

commit v2 on v1

v2 whole, which is shorter than its diff:
```python
import functools

import jax
import jax.numpy as jnp
from jax import lax
from jax.experimental import pallas as pl
from jax.experimental.pallas import tpu as pltpu
from jax.sharding import Mesh, PartitionSpec as P

C = 640
LANES = 128
XZ = ("x", "z")
F32 = jnp.float32
BF16 = jnp.bfloat16
VMEM = pl.BlockSpec(memory_space=pltpu.VMEM)
SMEM = pl.BlockSpec(memory_space=pltpu.SMEM)


def room(mib):
    return pltpu.CompilerParams(vmem_limit_bytes=mib << 20)


def dot(left, right):
    return jnp.dot(left, right, preferred_element_type=F32)


def dot_t(left, right):
    return lax.dot_general(left, right, (((1,), (1,)), ((), ())), preferred_element_type=F32)


def swap_cores(value):
    return lax.ppermute(value, "core", [(0, 1), (1, 0)])


def prepare_kernel(gram_ref, x_ref, z0_ref, z1_ref, x0_ref, x1_ref):
    step = pl.program_id(0)
    gram = gram_ref[0]
    high = gram.astype(BF16)
    rest = gram - high.astype(F32)
    mid = rest.astype(BF16)
    low = (rest - mid.astype(F32)).astype(BF16)
    x = x_ref[...]
    zt = (dot_t(low, x) + dot_t(mid, x)) + dot_t(high, x)
    tile = zt.shape[0]
    per_half = z0_ref.shape[0] // tile

    @pl.when(step < per_half)
    def _():
        z0_ref[pl.ds(pl.multiple_of(step * tile, tile), tile), :] = zt

    @pl.when(step >= per_half)
    def _():
        z1_ref[pl.ds(pl.multiple_of((step - per_half) * tile, tile), tile), :] = zt

    @pl.when(step == 0)
    def _():
        half = x0_ref.shape[0]
        x0_ref[...] = x[:half].astype(F32)
        x1_ref[...] = x[half:].astype(F32)


def prepare(features, inv_gram, tile=256):
    rows, width = features.shape
    z_shape = (width // 2, rows)
    x_shape = (rows // 2, width)
    return pl.pallas_call(
        prepare_kernel,
        grid=(width // tile,),
        in_specs=[
            pl.BlockSpec((1, tile, width), lambda i: (0, i, 0)),
            pl.BlockSpec((rows, width), lambda i: (0, 0)),
        ],
        out_specs=[pl.BlockSpec(z_shape, lambda i: (0, 0))] * 2
        + [pl.BlockSpec(x_shape, lambda i: (0, 0))] * 2,
        out_shape=[jax.ShapeDtypeStruct(z_shape, F32)] * 2
        + [jax.ShapeDtypeStruct(x_shape, F32)] * 2,
        compiler_params=room(24),
    )(inv_gram, features)


def held(shape, dtype=F32):
    return pltpu.VMEM(shape, dtype)


def near(value):
    return pltpu.with_memory_space_constraint(value, pltpu.VMEM)


def fetch(slot_ref, refs, landing, sems):
    for slot in range(len(refs) // 4):

        @pl.when(slot_ref[0] == slot)
        def _():
            for q in range(4):
                pltpu.make_async_copy(refs[slot * 4 + q], landing.at[q], sems.at[q]).start()

    for q in range(4):
        pltpu.make_async_copy(refs[q], landing.at[q], sems.at[q]).wait()


def gather_z_kernel(slot_ref, *refs):
    high_ref, low_ref, landing, sems = refs[-4:]
    fetch(slot_ref, refs[:-4], landing, sems)
    half_rows = high_ref.shape[0] // 2
    half_cols = high_ref.shape[1] // 2
    for k in range(2):
        for h in range(2):
            value = landing[k * 2 + h]
            high = value.astype(BF16)
            rows = pl.ds(h * half_rows, half_rows)
            cols = pl.ds(k * half_cols, half_cols)
            high_ref[rows, cols] = high
            low_ref[rows, cols] = (value - high.astype(F32)).astype(BF16)


def gather_x_kernel(slot_ref, *refs):
    out_ref, landing, sems = refs[-3:]
    fetch(slot_ref, refs[:-3], landing, sems)
    piece = out_ref.shape[0] // 4
    for q in range(4):
        out_ref[pl.ds(q * piece, piece), :] = landing[q].astype(BF16)


def gather(kernel, outs, slot, quarters):
    return pl.pallas_call(
        kernel,
        in_specs=[SMEM] + [pl.BlockSpec(memory_space=pl.ANY)] * len(quarters),
        out_specs=[VMEM] * len(outs),
        out_shape=[held(shape, BF16) for shape in outs],
        scratch_shapes=[
            pltpu.VMEM((4,) + quarters[0].shape, F32),
            pltpu.SemaphoreType.DMA((4,)),
        ],
        compiler_params=room(12),
        cost_estimate=pl.CostEstimate(flops=0, bytes_accessed=6 << 20, transcendentals=0),
    )(slot, *quarters)


def partial_sum(high_ref, low_ref, scaled):
    return dot(low_ref[...], scaled) + dot(high_ref[...], scaled)


def label_parts(lab, slices, width):
    group = jnp.zeros_like(lab)
    for d in range(1, slices):
        group = group + (lab >= d * width).astype(jnp.int32)
    return group, lab - group * width


def first_kernel(slices, slice_ref, lab_ref, labt_ref, high_ref, low_ref, out_ref):
    width = C // slices
    lab = lab_ref[...]
    group, low_label = label_parts(lab, slices, width)
    lane = lax.broadcasted_iota(jnp.int32, (lab.shape[0], LANES), 1)
    low_hot = jnp.where(low_label == lane, 1.0, 0.0)
    onehot = jnp.where(group == slice_ref[0], low_hot, 0.0).astype(BF16)
    labt = labt_ref[...]
    first = lax.broadcasted_iota(jnp.int32, (slices, labt.shape[1]), 0) * width
    group_hot = jnp.where((labt >= first) & (labt < first + width), 1.0, 0.0).astype(BF16)
    counts = dot(group_hot, low_hot.astype(BF16))
    total = partial_sum(high_ref, low_ref, onehot)
    chips, deep, _ = out_ref.shape
    out_ref[:, : deep - slices, :] = total.reshape(chips, deep - slices, LANES)
    out_ref[:, deep - slices :, :] = jnp.broadcast_to(counts[None], (chips, slices, LANES))


def middle_kernel(slices, total_rows, slice_ref, in_ref, *out_refs):
    summed = jnp.sum(in_ref[...], axis=0)
    solved_ref, copies_ref = out_refs[0], out_refs[1]
    chunk = solved_ref.shape[0]
    solved = summed[:chunk]
    if len(out_refs) == 3:
        totals = summed[chunk:]
        out_refs[2][...] = totals
        row = lax.broadcasted_iota(jnp.int32, totals.shape, 0)
        mine = jnp.sum(jnp.where(row == slice_ref[0], totals, 0.0), axis=0, keepdims=True)
        scale = jnp.where(mine > 0.0, total_rows / (C * jnp.maximum(mine, 1.0)), 0.0)
        solved = solved * scale.astype(BF16).astype(F32)
    solved_ref[...] = solved
    copies_ref[...] = jnp.broadcast_to(solved[None], copies_ref.shape)


def middle(slices, total_rows, slice_index, arrived, chunk):
    chips, deep, _ = arrived.shape
    shapes = [held((chunk, LANES)), held((chips, chunk, LANES))]
    if deep > chunk:
        shapes.append(held((slices, LANES)))
    return pl.pallas_call(
        functools.partial(middle_kernel, slices, total_rows),
        in_specs=[SMEM, VMEM],
        out_specs=[VMEM] * len(shapes),
        out_shape=shapes,
        compiler_params=room(8),
    )(slice_index, near(arrived))


def update(everyone_ref, x_ref, residual):
    solved = everyone_ref[...].reshape(-1, LANES).astype(BF16)
    return residual - dot(x_ref[...], solved)


def second_kernel(
    slices, total_rows, slice_ref, lab_ref, totals_ref, everyone_ref, x_ref, high_ref,
    low_ref, residual_ref, weight_ref, out_ref,
):
    width = C // slices
    lab = lab_ref[...]
    group, low_label = label_parts(lab, slices, width)
    lane = lax.broadcasted_iota(jnp.int32, (lab.shape[0], LANES), 1)
    hit = low_label == lane
    spread = jnp.zeros((lab.shape[0], LANES), F32)
    for d in range(slices):
        spread = jnp.where(group == d, totals_ref[d : d + 1, :], spread)
    row_count = jnp.sum(jnp.where(hit, spread, 0.0), axis=1, keepdims=True)
    weight = total_rows / (C * row_count)
    weight_ref[...] = jnp.broadcast_to(weight, weight_ref.shape)
    onehot = jnp.where(hit & (group == slice_ref[0]), 1.0, 0.0)
    residual = update(everyone_ref, x_ref, onehot)
    residual_ref[...] = residual
    total = partial_sum(high_ref, low_ref, (weight * residual).astype(BF16))
    out_ref[...] = total.reshape(out_ref.shape)


def step_kernel(
    everyone_ref, x_ref, high_ref, low_ref, old_ref, weight_ref, residual_ref, out_ref
):
    residual = update(everyone_ref, x_ref, old_ref[...])
    residual_ref[...] = residual
    total = partial_sum(high_ref, low_ref, (weight_ref[...] * residual).astype(BF16))
    out_ref[...] = total.reshape(out_ref.shape)


def last_kernel(blocks, core_ref, everyone_ref, x_ref, *refs):
    solved_refs, rows_refs, out_ref = refs[:blocks], refs[blocks:-1], refs[-1]
    rows = rows_refs[0].shape[0] // 2
    half = solved_refs[0].shape[0] // 2
    last = update(everyone_ref, x_ref, rows_refs[-1][...])
    for b in range(blocks):
        for k in range(2):
            out_ref[2 * b + k, :half] = solved_refs[b][k * half : (k + 1) * half]
            if b < blocks - 1:
                begin = jnp.where(core_ref[0] == k, 0, rows)
                begin = pl.multiple_of(begin, rows)
                out_ref[2 * b + k, half:] = rows_refs[b][pl.ds(begin, rows), :]
            else:
                mine = jnp.where(core_ref[0] == k, last[:rows], last[rows:])
                out_ref[2 * b + k, half:] = mine


def join_kernel(in_ref, weights_ref, after_ref):
    slices = in_ref.shape[0]
    width = C // slices
    head = weights_ref.shape[0]
    for d in range(slices):
        weights_ref[:, d * width : (d + 1) * width] = in_ref[d, :head, :width]
        after_ref[0, :, d * width : (d + 1) * width] = in_ref[d, head:, :width]


def shifted(value, by):
    count = lax.axis_size("feat")
    return lax.ppermute(value, "feat", [(i, (i + by) % count) for i in range(count)])


def all_slots(own, forward=None):
    up0, down1, up1, down0 = (
        shifted(own[0], 1), shifted(own[1], -1), shifted(own[1], 1), shifted(own[0], -1)
    )
    if forward is not None:
        up0, down1, up1, down0 = forward(up0, down1, up1, down0)
    far0, far1 = shifted(up0, 1), shifted(down1, -1)
    slots = [own, (up0, up1), (far0, far1), (down0, down1)]
    return slots, (up1, down0)


def with_other_core(slots):
    quarters = []
    for halves in slots:
        quarters += [halves[0], halves[1], swap_cores(halves[0]), swap_cores(halves[1])]
    return quarters


def local(features, labels, inv_gram):
    rows_here, block_width = features.shape
    blocks = lax.axis_size("feat")
    cores = lax.axis_size("core")
    chips = lax.axis_size("x") * lax.axis_size("z")
    slices = blocks * cores
    chunk = block_width // chips
    core = lax.axis_index("core").astype(jnp.int32)
    feat = lax.axis_index("feat").astype(jnp.int32)
    core_index = core[None]
    slice_index = (feat * cores + core)[None]
    total_rows = float(rows_here * chips * cores)
    both = cores * rows_here

    lab = jnp.concatenate([labels, swap_cores(labels)])
    lab_column, lab_row = lab[:, None], lab[None, :]
    z0, z1, x0, x1 = prepare(features, inv_gram)
    z_slots, z_mark = all_slots((z0, z1))
    x0, x1, _ = lax.optimization_barrier((x0, x1, z_mark))
    z_quarters = with_other_core(z_slots)

    def slot(b):
        return lax.rem(feat + (blocks - b), blocks)[None]

    def z_of(b, quarters):
        return gather(gather_z_kernel, [(block_width, both)] * 2, slot(b), quarters)

    def x_of(b, quarters):
        return gather(gather_x_kernel, [(both, block_width)], slot(b), quarters)[0]

    z_now = z_of(0, z_quarters)
    pieces = pl.pallas_call(
        functools.partial(first_kernel, slices),
        in_specs=[SMEM] + [VMEM] * 4,
        out_specs=VMEM,
        out_shape=held((chips, chunk + slices, LANES)),
        compiler_params=room(12),
    )(slice_index, lab_column, lab_row, *map(near, z_now))

    kept_rows = []
    kept_solved = []
    totals = weight = x_quarters = None
    for b in range(blocks):
        arrived = lax.all_to_all(pieces, XZ, 0, 0, tiled=True)
        if b == 0:
            tied = []

            def after_round(*parts):
                held_back = lax.optimization_barrier((*parts, arrived))
                tied.append(held_back[-1])
                return held_back[:-1]

            x_slots, _ = all_slots((x0, x1), after_round)
            arrived = tied[0]
            x_quarters = with_other_core(x_slots)
        result = middle(slices, total_rows, slice_index, arrived, chunk)
        kept_solved.append(result[0])
        if b == 0:
            totals = result[2]
        everyone = lax.all_to_all(result[1], XZ, 0, 0, tiled=True)
        x_now = x_of(b, x_quarters)
        if b < blocks - 1:
            z_now = z_of(b + 1, z_quarters)
        if b == 0:
            residual, weight, pieces = pl.pallas_call(
                functools.partial(second_kernel, slices, total_rows),
                in_specs=[SMEM] + [VMEM] * 6,
                out_specs=[VMEM] * 3,
                out_shape=[held((both, LANES)), held((both, LANES)), held((chips, chunk, LANES))],
                compiler_params=room(12),
            )(slice_index, lab_column, *map(near, (totals, everyone, x_now, *z_now)))
            kept_rows.append(residual)
        elif b < blocks - 1:
            residual, pieces = pl.pallas_call(
                step_kernel,
                in_specs=[VMEM] * 6,
                out_specs=[VMEM] * 2,
                out_shape=[held((both, LANES)), held((chips, chunk, LANES))],
                compiler_params=room(12),
            )(*map(near, (everyone, x_now, *z_now, kept_rows[-1], weight)))
            kept_rows.append(residual)
        else:
            sends = pl.pallas_call(
                functools.partial(last_kernel, blocks),
                in_specs=[SMEM] + [VMEM] * (2 + blocks + len(kept_rows)),
                out_specs=VMEM,
                out_shape=held((slices, chunk // cores + rows_here, LANES)),
                compiler_params=room(12),
            )(core_index, *map(near, (everyone, x_now, *kept_solved, *kept_rows)))

    got = near(lax.all_to_all(sends, ("feat", "core"), 0, 0, tiled=True))
    return pl.pallas_call(
        join_kernel,
        in_specs=[VMEM],
        out_specs=[VMEM, VMEM],
        out_shape=[
            jax.ShapeDtypeStruct((chunk // cores, C), F32),
            jax.ShapeDtypeStruct((1, rows_here, C), F32),
        ],
        compiler_params=room(12),
    )(got)


def solution(mesh):
    sizes = dict(mesh.shape)
    fine = Mesh(mesh.devices.reshape(sizes["feat"], 4, 8, 2), ("feat", "x", "z", "core"))
    rows = ("x", "z", "core")
    in_specs = (P(rows, "feat"), P(rows), P("feat", None, None))
    out_specs = (P(("feat",) + rows, None), P("feat", rows, None))
    return jax.shard_map(local, mesh=fine, in_specs=in_specs, out_specs=out_specs, check_vma=False)
```

time: 375 us -> 309 us (0.82)
  waiting for transfers between devices: 167 us -> 68.2 us
  starting transfers between devices: 35.6 us -> 77.4 us
  local copies, waits for them, and re-layouts: 4.13 us -> 44.1 us
  blocking collectives: 115 us -> 86.9 us
  between operations: 14.3 us -> 1.15 us
  Pallas kernels: 36 us -> 29.2 us
    all_gather x2 -> x0, waiting for transfers between devices: 106 us -> none  [the longest x1 53.8 us: local(): zt_mine = lax.all_gather(zt_own, 'feat')]
    ppermute x0 -> x12, waiting for transfers between devices: none -> 44.5 us  [shifted(): lax.ppermute(value, 'feat', [(i, (i + by) % count) for i in range(count)])]
    unnamed x35 -> x121, local copies, waits for them, and re-layouts: 3.24 us -> 43.9 us
    all_to_all x2 -> x1, blocking collectives: 45.2 us -> 23.5 us  [local(): got = near(lax.all_to_all(sends, ('feat', 'core'), 0, 0, tiled=True))]
    all_to_all x3 -> x4, waiting for transfers between devices: 40 us -> 21.2 us  [local(): everyone = lax.all_to_all(result[1], XZ, 0, 0, tiled=True)]
    ppermute x3 -> x17, starting transfers between devices: 1.68 us -> 17 us  [swap_cores(): return lax.ppermute(value, 'core', [(0, 1), (1, 0)])]
    ppermute x0 -> x12, starting transfers between devices: none -> 14.6 us  [shifted(): lax.ppermute(value, 'feat', [(i, (i + by) % count) for i in range(count)])]
    all_to_all x1, waiting for transfers between devices: 12.9 us -> 0.01 us  [local(): arrived = lax.all_to_all(pieces, XZ, 0, 0, tiled=True)]
  transfers between devices with their start and end apart: 9 -> 34, of which waited for: 7 -> 12; matrix products, arithmetic and copies ran while one was open for 0% -> 0% of each run, Pallas kernels for 1% -> 4%
where the time goes in v2:
time: 309 us; the launch traced here: 307 us
  blocking collectives  86.9 us (28%)
  starting transfers between devices  77.4 us (25%)
  waiting for transfers between devices  68.2 us (22%)
  local copies, waits for them, and re-layouts  44.1 us (14%)
  Pallas kernels  29.2 us (9%)
    all_to_all x3, blocking collectives, local(): arrived = lax.all_to_all(pieces, XZ, 0, 0, tiled=True)  63.4 us
    ppermute x12, waiting for transfers between devices, shifted(): lax.ppermute(value, 'feat', [(i, (i + by) % count) for i in range(count)])  44.5 us
    unnamed x121, local copies, waits for them, and re-layouts  43.9 us
    all_to_all x4, starting transfers between devices, local(): everyone = lax.all_to_all(result[1], XZ, 0, 0, tiled=True)  34.7 us
    all_to_all x1, blocking collectives, local(): got = near(lax.all_to_all(sends, ('feat', 'core'), 0, 0, tiled=True))  23.5 us
    all_to_all x4, waiting for transfers between devices, local(): everyone = lax.all_to_all(result[1], XZ, 0, 0, tiled=True)  21.2 us
    ppermute x17, starting transfers between devices, swap_cores(): return lax.ppermute(value, 'core', [(0, 1), (1, 0)])  17 us
    ppermute x12, starting transfers between devices, shifted(): lax.ppermute(value, 'feat', [(i, (i + by) % count) for i in range(count)])  14.6 us
  transfers between devices with their start and end apart: 34, of which 12 were waited for; matrix products, arithmetic and copies ran while one was open for 0% of the time, Pallas kernels for 4%

profile of v2, /device:TPU:1, one launch (start us, length us, event | category | flops | bytes accessed | tf_op | source)
XLA Modules:
  0.0 307.0 jit_solution(829473124421667397)
XLA Ops:
  0.6 2.2 copy-done.27
  2.8 1.0 copy-done.53
  3.9 2.7 shard_map.50
  6.5 3.6 %collective-permute-start.13 = (f32[512,256]{1,0:T(8,128)S(1)}, f32[512,256]{1,0:T(8,128)S(1)}, u32[]{:S(2)}, u32[]{:S(2)}) collective-permute-start(f32[512,256]{1,0:T(8,128)S(1)} %get-tuple-element.39.refs_1_), channel_id=1, source_target_pairs={{0,192},{64,0},{128,64},{192,128},{1,193},{65,1},{129,65},{193,129... | collective-permute-start | bytes 1572872 | tf_op jit(solution)/shard_map/ppermute | solution.py:261
  13.0 7.7 %collective-permute-done.13.refs_13_ = f32[512,256]{1,0:T(8,128)S(1)} collective-permute-done((f32[512,256]{1,0:T(8,128)S(1)}, f32[512,256]{1,0:T(8,128)S(1)}, u32[]{:S(2)}, u32[]{:S(2)}) %collective-permute-start.13) | collective-permute-done | bytes 524320 | tf_op jit(solution)/shard_map/ppermute | solution.py:261
  20.7 3.4 %collective-permute-start.2 = (f32[512,256]{1,0:T(8,128)S(1)}, f32[512,256]{1,0:T(8,128)}, u32[]{:S(2)}, u32[]{:S(2)}) collective-permute-start(f32[512,256]{1,0:T(8,128)S(1)} %get-tuple-element.40.refs_0_), channel_id=1, source_target_pairs={{0,192},{64,0},{128,64},{192,128},{1,193},{65,1},{129,65},{193,129... | collective-permute-start | bytes 1572872 | tf_op jit(solution)/shard_map/ppermute | solution.py:261
  24.1 1.8 collective-permute-start.18
  26.0 11.2 %collective-permute-done.9.refs_4_ = f32[512,256]{1,0:T(8,128)} collective-permute-done((f32[512,256]{1,0:T(8,128)S(1)}, f32[512,256]{1,0:T(8,128)}, u32[]{:S(2)}, u32[]{:S(2)}) %collective-permute-start.9) | collective-permute-done | bytes 524320 | tf_op jit(solution)/shard_map/ppermute | solution.py:261
  40.2 4.9 %collective-permute-done.14.refs_9_ = f32[512,256]{1,0:T(8,128)} collective-permute-done((f32[512,256]{1,0:T(8,128)S(1)}, f32[512,256]{1,0:T(8,128)}, u32[]{:S(2)}, u32[]{:S(2)}) %collective-permute-start.14) | collective-permute-done | bytes 524320 | tf_op jit(solution)/shard_map/ppermute | solution.py:261
  45.1 2.4 collective-permute-start.16
  47.5 3.8 %collective-permute-done.12.refs_8_ = f32[512,256]{1,0:T(8,128)} collective-permute-done((f32[512,256]{1,0:T(8,128)}, f32[512,256]{1,0:T(8,128)}, u32[]{:S(2)}, u32[]{:S(2)}) %collective-permute-start.12) | collective-permute-done | bytes 524320 | tf_op jit(solution)/shard_map/ppermute | solution.py:261
  51.3 1.7 collective-permute-start.15
  53.2 1.6 collective-permute-done.15.refs_10_
  54.9 1.0 copy-done.1
  55.9 1.0 copy-done.6
  59.4 11.2 %all-to-all-start = ((f32[32,40,128]{2,1,0:T(8,128)}), f32[32,40,128]{2,1,0:T(8,128)}, u32[]{:S(2)}, u32[]{:S(2)}) async-start(f32[32,40,128]{2,1,0:T(8,128)} %copy-done.32), calls=%async_computation | async-start | bytes 1310720 | tf_op jit(solution)/shard_map/all_to_all | solution.py:325
  71.1 1.1 collective-permute-start.3
  72.4 2.5 collective-permute-start.4
  74.9 1.8 collective-permute-start.19
  76.7 7.0 %collective-permute-done.6.refs_12_ = f32[128,1024]{1,0:T(8,128)S(1)} collective-permute-done((f32[128,1024]{1,0:T(8,128)S(1)}, f32[128,1024]{1,0:T(8,128)S(1)}, u32[]{:S(2)}, u32[]{:S(2)}) %collective-permute-start.6) | collective-permute-done | bytes 524320 | tf_op jit(solution)/shard_map/ppermute | solution.py:261
  83.7 2.5 collective-permute-start.20
  86.2 9.8 %collective-permute-done.5.refs_5_ = f32[128,1024]{1,0:T(8,128)S(1)} collective-permute-done((f32[128,1024]{1,0:T(8,128)S(1)}, f32[128,1024]{1,0:T(8,128)S(1)}, u32[]{:S(2)}, u32[]{:S(2)}) %collective-permute-start.5) | collective-permute-done | bytes 524320 | tf_op jit(solution)/shard_map/ppermute | solution.py:261
  96.9 1.8 collective-permute-start.22
  98.7 2.7 collective-permute-start.24
  101.4 1.2 shard_map.53
  103.3 9.3 %all-to-all-start.1 = ((f32[32,32,128]{2,1,0:T(8,128)}), f32[32,32,128]{2,1,0:T(8,128)}, u32[]{:S(2)}, u32[]{:S(2)}) async-start(f32[32,32,128]{2,1,0:T(8,128)} %copy-done.54), calls=%async_computation.1 | async-start | bytes 1048576 | tf_op jit(solution)/shard_map/all_to_all | solution.py:341
  114.7 1.0 copy-done.2
  115.7 1.0 copy-done.7
  116.8 1.7 shard_map.55
  120.5 1.4 shard_map.54.x_ref
  122.9 4.1 %all-to-all-done.1.everyone_ref = f32[32,32,128]{2,1,0:T(8,128)} async-done(((f32[32,32,128]{2,1,0:T(8,128)}), f32[32,32,128]{2,1,0:T(8,128)}, u32[]{:S(2)}, u32[]{:S(2)}) %all-to-all-start.1) | async-done | bytes 524320 | tf_op jit(solution)/shard_map/all_to_all | solution.py:341
  127.1 1.2 copy-done.26
  128.3 1.2 copy-done.34
  129.5 1.2 copy-done.36
  130.7 2.8 shard_map.56
  133.6 21.0 %all_to_all.45.in_ref = f32[32,32,128]{2,1,0:T(8,128)S(1)} all-to-all(f32[32,32,128]{2,1,0:T(8,128)S(1)} %get-tuple-element.54), channel_id=1, replica_groups=mesh['feat'=4,'x'=4,'z'=8,'core'=2] {'x','z'}, dimensions={0} | all-to-all | bytes 1048576 | tf_op jit(solution)/shard_map/all_to_all | solution.py:325
  155.4 8.2 %all-to-all-start.3 = ((f32[32,32,128]{2,1,0:T(8,128)}), f32[32,32,128]{2,1,0:T(8,128)}, u32[]{:S(2)}, u32[]{:S(2)}) async-start(f32[32,32,128]{2,1,0:T(8,128)} %copy-done.56), calls=%async_computation.3 | async-start | bytes 1048576 | tf_op jit(solution)/shard_map/all_to_all | solution.py:341
  164.7 1.0 copy-done.8
  165.8 2.0 shard_map.59
  169.8 1.6 shard_map.58.x_ref
  172.4 4.5 %all-to-all-done.3.everyone_ref = f32[32,32,128]{2,1,0:T(8,128)} async-done(((f32[32,32,128]{2,1,0:T(8,128)}), f32[32,32,128]{2,1,0:T(8,128)}, u32[]{:S(2)}, u32[]{:S(2)}) %all-to-all-start.3) | async-done | bytes 524320 | tf_op jit(solution)/shard_map/all_to_all | solution.py:341
  176.8 1.2 copy-done.31
  178.1 1.2 copy-done.44
  179.3 1.2 copy-done.46
  181.5 2.7 shard_map.60
  184.1 21.1 %all_to_all.46.in_ref = f32[32,32,128]{2,1,0:T(8,128)S(1)} all-to-all(f32[32,32,128]{2,1,0:T(8,128)S(1)} %get-tuple-element.60), channel_id=1, replica_groups=mesh['feat'=4,'x'=4,'z'=8,'core'=2] {'x','z'}, dimensions={0} | all-to-all | bytes 1048576 | tf_op jit(solution)/shard_map/all_to_all | solution.py:325
  206.2 8.8 %all-to-all-start.5 = ((f32[32,32,128]{2,1,0:T(8,128)}), f32[32,32,128]{2,1,0:T(8,128)}, u32[]{:S(2)}, u32[]{:S(2)}) async-start(f32[32,32,128]{2,1,0:T(8,128)} %copy-done.55), calls=%async_computation.5 | async-start | bytes 1048576 | tf_op jit(solution)/shard_map/all_to_all | solution.py:341
  216.0 1.0 copy-done.9
  217.0 2.0 shard_map.63
  221.0 1.7 shard_map.62.x_ref
  222.7 5.2 %all-to-all-done.5.everyone_ref = f32[32,32,128]{2,1,0:T(8,128)} async-done(((f32[32,32,128]{2,1,0:T(8,128)}), f32[32,32,128]{2,1,0:T(8,128)}, u32[]{:S(2)}, u32[]{:S(2)}) %all-to-all-start.5) | async-done | bytes 524320 | tf_op jit(solution)/shard_map/all_to_all | solution.py:341
  227.9 1.2 copy-done.40
  229.1 1.2 copy-done.42
  231.3 2.7 shard_map.64
  234.0 21.3 %all_to_all.47.in_ref = f32[32,32,128]{2,1,0:T(8,128)S(1)} all-to-all(f32[32,32,128]{2,1,0:T(8,128)S(1)} %get-tuple-element.65), channel_id=1, replica_groups=mesh['feat'=4,'x'=4,'z'=8,'core'=2] {'x','z'}, dimensions={0} | all-to-all | bytes 1048576 | tf_op jit(solution)/shard_map/all_to_all | solution.py:325
  256.2 8.5 %all-to-all-start.7 = ((f32[32,32,128]{2,1,0:T(8,128)}), f32[32,32,128]{2,1,0:T(8,128)}, u32[]{:S(2)}, u32[]{:S(2)}) async-start(f32[32,32,128]{2,1,0:T(8,128)} %get-tuple-element.66), calls=%async_computation.7 | async-start | bytes 1048576 | tf_op jit(solution)/shard_map/all_to_all | solution.py:341
  265.7 1.0 copy-done.19
  266.8 1.0 copy-done.24
  267.8 1.4 shard_map.66.x_ref
  270.2 7.5 %all-to-all-done.7.everyone_ref = f32[32,32,128]{2,1,0:T(8,128)} async-done(((f32[32,32,128]{2,1,0:T(8,128)}), f32[32,32,128]{2,1,0:T(8,128)}, u32[]{:S(2)}, u32[]{:S(2)}) %all-to-all-start.7) | async-done | bytes 524320 | tf_op jit(solution)/shard_map/all_to_all | solution.py:341
  277.7 1.2 copy-done.29
  280.8 1.5 shard_map.67
  282.4 23.5 %all_to_all.48.in_ref = f32[8,272,128]{2,1,0:T(8,128)S(1)} all-to-all(f32[8,272,128]{2,1,0:T(8,128)S(1)} %shard_map.67), channel_id=1, replica_groups=mesh['feat'=4,'x'=4,'z'=8,'core'=2] {'feat','core'}, dimensions={0} | all-to-all | bytes 2228224 | tf_op jit(solution)/shard_map/all_to_all | solution.py:372
  305.9 1.2 shard_map.68
  (151 shorter events, 31.2 us)
Async XLA Ops:
  0.6 2.2 copy-start.27
  3.9 7.7 %copy-start.59 = (s32[256]{0:T(256)S(1)}, s32[256]{0:T(256)}, u32[]{:S(2)}) copy-start(s32[256]{0:T(256)} %param.4) | copy-start | bytes 3076
  6.5 14.2 %collective-permute-start.13 = (f32[512,256]{1,0:T(8,128)S(1)}, f32[512,256]{1,0:T(8,128)S(1)}, u32[]{:S(2)}, u32[]{:S(2)}) collective-permute-start(f32[512,256]{1,0:T(8,128)S(1)} %get-tuple-element.39.refs_1_), channel_id=1, source_target_pairs={{0,192},{64,0},{128,64},{192,128},{1,193},{65,1},{129,65},{193,129... | collective-permute-start | bytes 1572872 | tf_op jit(solution)/shard_map/ppermute | solution.py:261
  10.1 14.0 %collective-permute-start.8 = (f32[512,256]{1,0:T(8,128)S(1)}, f32[512,256]{1,0:T(8,128)S(1)}, u32[]{:S(2)}, u32[]{:S(2)}) collective-permute-start(f32[512,256]{1,0:T(8,128)S(1)} %get-tuple-element.39.refs_1_), channel_id=1, source_target_pairs={{0,1},{1,0},{2,3},{3,2},{4,5},{5,4},{6,7},{7,6},{8,9},{9,8},{10,11... | collective-permute-start | bytes 1572872 | tf_op jit(solution)/shard_map/ppermute | solution.py:32
  11.1 14.9 %collective-permute-start.1 = (f32[512,256]{1,0:T(8,128)S(1)}, f32[512,256]{1,0:T(8,128)}, u32[]{:S(2)}, u32[]{:S(2)}) collective-permute-start(f32[512,256]{1,0:T(8,128)S(1)} %get-tuple-element.39.refs_1_), channel_id=1, source_target_pairs={{0,64},{64,128},{128,192},{192,0},{1,65},{65,129},{129,193},{193,1... | collective-permute-start | bytes 1572872 | tf_op jit(solution)/shard_map/ppermute | solution.py:261
  11.5 25.6 %collective-permute-start.9 = (f32[512,256]{1,0:T(8,128)S(1)}, f32[512,256]{1,0:T(8,128)}, u32[]{:S(2)}, u32[]{:S(2)}) collective-permute-start(f32[512,256]{1,0:T(8,128)S(1)} %get-tuple-element.40.refs_0_), channel_id=1, source_target_pairs={{0,64},{64,128},{128,192},{192,0},{1,65},{65,129},{129,193},{193,1... | collective-permute-start | bytes 1572872 | tf_op jit(solution)/shard_map/ppermute | solution.py:261
  11.6 1.2 collective-permute-start
  12.7 24.4 %collective-permute-start.7 = (f32[512,256]{1,0:T(8,128)S(1)}, f32[512,256]{1,0:T(8,128)S(1)}, u32[]{:S(2)}, u32[]{:S(2)}) collective-permute-start(f32[512,256]{1,0:T(8,128)S(1)} %get-tuple-element.40.refs_0_), channel_id=1, source_target_pairs={{0,1},{1,0},{2,3},{3,2},{4,5},{5,4},{6,7},{7,6},{8,9},{9,8},{10,11... | collective-permute-start | bytes 1572872 | tf_op jit(solution)/shard_map/ppermute | solution.py:32
  20.7 18.1 %collective-permute-start.2 = (f32[512,256]{1,0:T(8,128)S(1)}, f32[512,256]{1,0:T(8,128)}, u32[]{:S(2)}, u32[]{:S(2)}) collective-permute-start(f32[512,256]{1,0:T(8,128)S(1)} %get-tuple-element.40.refs_0_), channel_id=1, source_target_pairs={{0,192},{64,0},{128,64},{192,128},{1,193},{65,1},{129,65},{193,129... | collective-permute-start | bytes 1572872 | tf_op jit(solution)/shard_map/ppermute | solution.py:261
  24.1 14.7 %collective-permute-start.18 = (f32[512,256]{1,0:T(8,128)S(1)}, f32[512,256]{1,0:T(8,128)S(1)}, u32[]{:S(2)}, u32[]{:S(2)}) collective-permute-start(f32[512,256]{1,0:T(8,128)S(1)} %collective-permute-done.13.refs_13_), channel_id=1, source_target_pairs={{0,1},{1,0},{2,3},{3,2},{4,5},{5,4},{6,7},{7,6},{8,9},{9,8},{10,11... | collective-permute-start | bytes 1572872 | tf_op jit(solution)/shard_map/ppermute | solution.py:32
  26.0 19.1 %collective-permute-start.14 = (f32[512,256]{1,0:T(8,128)S(1)}, f32[512,256]{1,0:T(8,128)}, u32[]{:S(2)}, u32[]{:S(2)}) collective-permute-start(f32[512,256]{1,0:T(8,128)S(1)} %collective-permute-done.13.refs_13_), channel_id=1, source_target_pairs={{0,192},{64,0},{128,64},{192,128},{1,193},{65,1},{129,65},{193,129... | collective-permute-start | bytes 1572872 | tf_op jit(solution)/shard_map/ppermute | solution.py:261
  37.1 14.1 %collective-permute-start.12 = (f32[512,256]{1,0:T(8,128)}, f32[512,256]{1,0:T(8,128)}, u32[]{:S(2)}, u32[]{:S(2)}) collective-permute-start(f32[512,256]{1,0:T(8,128)} %collective-permute-done.9.refs_4_), channel_id=1, source_target_pairs={{0,64},{64,128},{128,192},{192,0},{1,65},{65,129},{129,193},{193,1... | collective-permute-start | bytes 1572872 | tf_op jit(solution)/shard_map/ppermute | solution.py:261
  38.0 15.3 %collective-permute-start.10 = (f32[512,256]{1,0:T(8,128)}, f32[512,256]{1,0:T(8,128)}, u32[]{:S(2)}, u32[]{:S(2)}) collective-permute-start(f32[512,256]{1,0:T(8,128)} %collective-permute-done.9.refs_4_), channel_id=1, source_target_pairs={{0,1},{1,0},{2,3},{3,2},{4,5},{5,4},{6,7},{7,6},{8,9},{9,8},{10,11... | collective-permute-start | bytes 1572872 | tf_op jit(solution)/shard_map/ppermute | solution.py:32
  38.8 14.4 %collective-permute-start.11 = (f32[512,256]{1,0:T(8,128)}, f32[512,256]{1,0:T(8,128)}, u32[]{:S(2)}, u32[]{:S(2)}) collective-permute-start(f32[512,256]{1,0:T(8,128)} %collective-permute-done.1.refs_5_), channel_id=1, source_target_pairs={{0,1},{1,0},{2,3},{3,2},{4,5},{5,4},{6,7},{7,6},{8,9},{9,8},{10,11... | collective-permute-start | bytes 1572872 | tf_op jit(solution)/shard_map/ppermute | solution.py:32
  39.7 13.6 %collective-permute-start.17 = (f32[512,256]{1,0:T(8,128)}, f32[512,256]{1,0:T(8,128)}, u32[]{:S(2)}, u32[]{:S(2)}) collective-permute-start(f32[512,256]{1,0:T(8,128)} %collective-permute-done.2.refs_12_), channel_id=1, source_target_pairs={{0,1},{1,0},{2,3},{3,2},{4,5},{5,4},{6,7},{7,6},{8,9},{9,8},{10,11... | collective-permute-start | bytes 1572872 | tf_op jit(solution)/shard_map/ppermute | solution.py:32
  45.1 8.1 %collective-permute-start.16 = (f32[512,256]{1,0:T(8,128)}, f32[512,256]{1,0:T(8,128)}, u32[]{:S(2)}, u32[]{:S(2)}) collective-permute-start(f32[512,256]{1,0:T(8,128)} %collective-permute-done.14.refs_9_), channel_id=1, source_target_pairs={{0,1},{1,0},{2,3},{3,2},{4,5},{5,4},{6,7},{7,6},{8,9},{9,8},{10,11... | collective-permute-start | bytes 1572872 | tf_op jit(solution)/shard_map/ppermute | solution.py:32
  51.3 3.6 %collective-permute-start.15 = (f32[512,256]{1,0:T(8,128)}, f32[512,256]{1,0:T(8,128)}, u32[]{:S(2)}, u32[]{:S(2)}) collective-permute-start(f32[512,256]{1,0:T(8,128)} %collective-permute-done.12.refs_8_), channel_id=1, source_target_pairs={{0,1},{1,0},{2,3},{3,2},{4,5},{5,4},{6,7},{7,6},{8,9},{9,8},{10,11... | collective-permute-start | bytes 1572872 | tf_op jit(solution)/shard_map/ppermute | solution.py:32
  59.4 37.5 %all-to-all-start = ((f32[32,40,128]{2,1,0:T(8,128)}), f32[32,40,128]{2,1,0:T(8,128)}, u32[]{:S(2)}, u32[]{:S(2)}) async-start(f32[32,40,128]{2,1,0:T(8,128)} %copy-done.32), calls=%async_computation | async-start | bytes 1310720 | tf_op jit(solution)/shard_map/all_to_all | solution.py:325
  70.5 13.2 %collective-permute-start.6 = (f32[128,1024]{1,0:T(8,128)S(1)}, f32[128,1024]{1,0:T(8,128)S(1)}, u32[]{:S(2)}, u32[]{:S(2)}) collective-permute-start(f32[128,1024]{1,0:T(8,128)S(1)} %get-tuple-element.41.refs_0_), channel_id=1, source_target_pairs={{0,192},{64,0},{128,64},{192,128},{1,193},{65,1},{129,65},{193,129... | collective-permute-start | bytes 1572872 | tf_op jit(solution)/shard_map/ppermute | solution.py:261
  71.1 15.1 %collective-permute-start.3 = (f32[128,1024]{1,0:T(8,128)S(1)}, f32[128,1024]{1,0:T(8,128)S(1)}, u32[]{:S(2)}, u32[]{:S(2)}) collective-permute-start(f32[128,1024]{1,0:T(8,128)S(1)} %get-tuple-element.41.refs_0_), channel_id=1, source_target_pairs={{0,64},{64,128},{128,192},{192,0},{1,65},{65,129},{129,193},{193,1... | collective-permute-start | bytes 1572872 | tf_op jit(solution)/shard_map/ppermute | solution.py:261
  72.2 23.8 %collective-permute-start.5 = (f32[128,1024]{1,0:T(8,128)S(1)}, f32[128,1024]{1,0:T(8,128)S(1)}, u32[]{:S(2)}, u32[]{:S(2)}) collective-permute-start(f32[128,1024]{1,0:T(8,128)S(1)} %get-tuple-element.42.refs_1_), channel_id=1, source_target_pairs={{0,64},{64,128},{128,192},{192,0},{1,65},{65,129},{129,193},{193,1... | collective-permute-start | bytes 1572872 | tf_op jit(solution)/shard_map/ppermute | solution.py:261
  72.4 24.5 %collective-permute-start.4 = (f32[128,1024]{1,0:T(8,128)S(1)}, f32[128,1024]{1,0:T(8,128)}, u32[]{:S(2)}, u32[]{:S(2)}) collective-permute-start(f32[128,1024]{1,0:T(8,128)S(1)} %get-tuple-element.42.refs_1_), channel_id=1, source_target_pairs={{0,192},{64,0},{128,64},{192,128},{1,193},{65,1},{129,65},{193,129... | collective-permute-start | bytes 1572872 | tf_op jit(solution)/shard_map/ppermute | solution.py:261
  74.9 37.7 %collective-permute-start.19 = (f32[128,1024]{1,0:T(8,128)S(1)}, f32[128,1024]{1,0:T(8,128)}, u32[]{:S(2)}, u32[]{:S(2)}) collective-permute-start(f32[128,1024]{1,0:T(8,128)S(1)} %get-tuple-element.41.refs_0_), channel_id=1, source_target_pairs={{0,1},{1,0},{2,3},{3,2},{4,5},{5,4},{6,7},{7,6},{8,9},{9,8},{10,11... | collective-permute-start | bytes 1572872 | tf_op jit(solution)/shard_map/ppermute | solution.py:32
  83.7 12.4 %copy-start.10 = (f32[128,1024]{1,0:T(8,128)}, f32[128,1024]{1,0:T(8,128)S(1)}, u32[]{:S(2)}) copy-start(f32[128,1024]{1,0:T(8,128)S(1)} %collective-permute-done.6.refs_12_) | copy-start | bytes 1572868
  83.7 30.0 %collective-permute-start.20 = (f32[128,1024]{1,0:T(8,128)S(1)}, f32[128,1024]{1,0:T(8,128)}, u32[]{:S(2)}, u32[]{:S(2)}) collective-permute-start(f32[128,1024]{1,0:T(8,128)S(1)} %get-tuple-element.42.refs_1_), channel_id=1, source_target_pairs={{0,1},{1,0},{2,3},{3,2},{4,5},{5,4},{6,7},{7,6},{8,9},{9,8},{10,11... | collective-permute-start | bytes 1572872 | tf_op jit(solution)/shard_map/ppermute | solution.py:32
  86.2 9.9 %copy-start.15 = (f32[128,1024]{1,0:T(8,128)}, f32[128,1024]{1,0:T(8,128)S(1)}, u32[]{:S(2)}) copy-start(f32[128,1024]{1,0:T(8,128)S(1)} %collective-permute-done.3.refs_4_) | copy-start | bytes 1572868
  96.9 16.9 %collective-permute-start.22 = (f32[128,1024]{1,0:T(8,128)}, f32[128,1024]{1,0:T(8,128)}, u32[]{:S(2)}, u32[]{:S(2)}) collective-permute-start(f32[128,1024]{1,0:T(8,128)} %copy-done.20), channel_id=1, source_target_pairs={{0,1},{1,0},{2,3},{3,2},{4,5},{5,4},{6,7},{7,6},{8,9},{9,8},{10,11... | collective-permute-start | bytes 1572872 | tf_op jit(solution)/shard_map/ppermute | solution.py:32
  98.7 15.5 %collective-permute-start.23 = (f32[128,1024]{1,0:T(8,128)}, f32[128,1024]{1,0:T(8,128)}, u32[]{:S(2)}, u32[]{:S(2)}) collective-permute-start(f32[128,1024]{1,0:T(8,128)} %copy-done.15), channel_id=1, source_target_pairs={{0,64},{64,128},{128,192},{192,0},{1,65},{65,129},{129,193},{193,1... | collective-permute-start | bytes 1572872 | tf_op jit(solution)/shard_map/ppermute | solution.py:261
  98.7 15.9 %collective-permute-start.24 = (f32[128,1024]{1,0:T(8,128)}, f32[128,1024]{1,0:T(8,128)}, u32[]{:S(2)}, u32[]{:S(2)}) collective-permute-start(f32[128,1024]{1,0:T(8,128)} %collective-permute-done.4.refs_13_), channel_id=1, source_target_pairs={{0,192},{64,0},{128,64},{192,128},{1,193},{65,1},{129,65},{193,129... | collective-permute-start | bytes 1572872 | tf_op jit(solution)/shard_map/ppermute | solution.py:261
  103.3 23.7 %all-to-all-start.1 = ((f32[32,32,128]{2,1,0:T(8,128)}), f32[32,32,128]{2,1,0:T(8,128)}, u32[]{:S(2)}, u32[]{:S(2)}) async-start(f32[32,32,128]{2,1,0:T(8,128)} %copy-done.54), calls=%async_computation.1 | async-start | bytes 1048576 | tf_op jit(solution)/shard_map/all_to_all | solution.py:341
  112.6 7.8 %collective-permute-start.21 = (f32[128,1024]{1,0:T(8,128)}, f32[128,1024]{1,0:T(8,128)}, u32[]{:S(2)}, u32[]{:S(2)}) collective-permute-start(f32[128,1024]{1,0:T(8,128)} %copy-done.15), channel_id=1, source_target_pairs={{0,1},{1,0},{2,3},{3,2},{4,5},{5,4},{6,7},{7,6},{8,9},{9,8},{10,11... | collective-permute-start | bytes 1572872 | tf_op jit(solution)/shard_map/ppermute | solution.py:32
  113.7 6.8 %collective-permute-start.28 = (f32[128,1024]{1,0:T(8,128)}, f32[128,1024]{1,0:T(8,128)}, u32[]{:S(2)}, u32[]{:S(2)}) collective-permute-start(f32[128,1024]{1,0:T(8,128)} %collective-permute-done.4.refs_13_), channel_id=1, source_target_pairs={{0,1},{1,0},{2,3},{3,2},{4,5},{5,4},{6,7},{7,6},{8,9},{9,8},{10,11... | collective-permute-start | bytes 1572872 | tf_op jit(solution)/shard_map/ppermute | solution.py:32
  113.8 6.7 %collective-permute-start.27 = (f32[128,1024]{1,0:T(8,128)}, f32[128,1024]{1,0:T(8,128)}, u32[]{:S(2)}, u32[]{:S(2)}) collective-permute-start(f32[128,1024]{1,0:T(8,128)} %copy-done.10), channel_id=1, source_target_pairs={{0,1},{1,0},{2,3},{3,2},{4,5},{5,4},{6,7},{7,6},{8,9},{9,8},{10,11... | collective-permute-start | bytes 1572872 | tf_op jit(solution)/shard_map/ppermute | solution.py:32
  114.2 6.3 %collective-permute-start.25 = (f32[128,1024]{1,0:T(8,128)}, f32[128,1024]{1,0:T(8,128)}, u32[]{:S(2)}, u32[]{:S(2)}) collective-permute-start(f32[128,1024]{1,0:T(8,128)} %collective-permute-done.23.refs_8_), channel_id=1, source_target_pairs={{0,1},{1,0},{2,3},{3,2},{4,5},{5,4},{6,7},{7,6},{8,9},{9,8},{10,11... | collective-permute-start | bytes 1572872 | tf_op jit(solution)/shard_map/ppermute | solution.py:32
  114.6 5.9 %collective-permute-start.26 = (f32[128,1024]{1,0:T(8,128)}, f32[128,1024]{1,0:T(8,128)}, u32[]{:S(2)}, u32[]{:S(2)}) collective-permute-start(f32[128,1024]{1,0:T(8,128)} %collective-permute-done.24.refs_9_), channel_id=1, source_target_pairs={{0,1},{1,0},{2,3},{3,2},{4,5},{5,4},{6,7},{7,6},{8,9},{9,8},{10,11... | collective-permute-start | bytes 1572872 | tf_op jit(solution)/shard_map/ppermute | solution.py:32
  116.8 3.7 %copy-start.11 = (f32[128,1024]{1,0:T(8,128)S(1)}, f32[128,1024]{1,0:T(8,128)}, u32[]{:S(2)}) copy-start(f32[128,1024]{1,0:T(8,128)} %copy-done.10) | copy-start | bytes 1572868
  116.8 3.7 %copy-start.16 = (f32[128,1024]{1,0:T(8,128)S(1)}, f32[128,1024]{1,0:T(8,128)}, u32[]{:S(2)}) copy-start(f32[128,1024]{1,0:T(8,128)} %copy-done.15) | copy-start | bytes 1572868
  116.8 3.7 %copy-start.21 = (f32[128,1024]{1,0:T(8,128)S(1)}, f32[128,1024]{1,0:T(8,128)}, u32[]{:S(2)}) copy-start(f32[128,1024]{1,0:T(8,128)} %copy-done.20) | copy-start | bytes 1572868
  127.1 1.2 copy-start.26
  128.3 1.2 copy-start.34
  129.5 1.2 copy-start.36
  133.6 21.1 %copy-start.37 = (f32[512,128]{1,0:T(8,128)}, f32[512,128]{1,0:T(8,128)S(1)}, u32[]{:S(2)}) copy-start(f32[512,128]{1,0:T(8,128)S(1)} %get-tuple-element.59.weight_ref) | copy-start | bytes 786436
  133.6 21.1 %copy-start.47 = (f32[512,128]{1,0:T(8,128)}, f32[512,128]{1,0:T(8,128)S(1)}, u32[]{:S(2)}) copy-start(f32[512,128]{1,0:T(8,128)S(1)} %get-tuple-element.58.old_ref.refs_4_) | copy-start | bytes 786436
  155.4 21.4 %all-to-all-start.3 = ((f32[32,32,128]{2,1,0:T(8,128)}), f32[32,32,128]{2,1,0:T(8,128)}, u32[]{:S(2)}, u32[]{:S(2)}) async-start(f32[32,32,128]{2,1,0:T(8,128)} %copy-done.56), calls=%async_computation.3 | async-start | bytes 1048576 | tf_op jit(solution)/shard_map/all_to_all | solution.py:341
  163.7 1.0 copy-start.3
  165.8 4.0 %copy-start.12 = (f32[128,1024]{1,0:T(8,128)S(1)}, f32[128,1024]{1,0:T(8,128)}, u32[]{:S(2)}) copy-start(f32[128,1024]{1,0:T(8,128)} %copy-done.10) | copy-start | bytes 1572868
  165.8 4.0 %copy-start.17 = (f32[128,1024]{1,0:T(8,128)S(1)}, f32[128,1024]{1,0:T(8,128)}, u32[]{:S(2)}) copy-start(f32[128,1024]{1,0:T(8,128)} %copy-done.15) | copy-start | bytes 1572868
  165.8 4.0 %copy-start.22 = (f32[128,1024]{1,0:T(8,128)S(1)}, f32[128,1024]{1,0:T(8,128)}, u32[]{:S(2)}) copy-start(f32[128,1024]{1,0:T(8,128)} %copy-done.20) | copy-start | bytes 1572868
  169.8 7.1 %copy-start.38 = (f32[512,128]{1,0:T(8,128)S(1)}, f32[512,128]{1,0:T(8,128)}, u32[]{:S(2)}) copy-start(f32[512,128]{1,0:T(8,128)} %copy-done.37) | copy-start | bytes 786436
  176.8 1.2 copy-start.31
  178.1 1.2 copy-start.44
  179.3 1.2 copy-start.46
  184.1 21.3 %copy-start.50 = (f32[512,128]{1,0:T(8,128)}, f32[512,128]{1,0:T(8,128)S(1)}, u32[]{:S(2)}) copy-start(f32[512,128]{1,0:T(8,128)S(1)} %get-tuple-element.64.old_ref.refs_5_) | copy-start | bytes 786436
  206.2 21.7 %all-to-all-start.5 = ((f32[32,32,128]{2,1,0:T(8,128)}), f32[32,32,128]{2,1,0:T(8,128)}, u32[]{:S(2)}, u32[]{:S(2)}) async-start(f32[32,32,128]{2,1,0:T(8,128)} %copy-done.55), calls=%async_computation.5 | async-start | bytes 1048576 | tf_op jit(solution)/shard_map/all_to_all | solution.py:341
  217.0 4.0 %copy-start.13 = (f32[128,1024]{1,0:T(8,128)S(1)}, f32[128,1024]{1,0:T(8,128)}, u32[]{:S(2)}) copy-start(f32[128,1024]{1,0:T(8,128)} %copy-done.10) | copy-start | bytes 1572868
  217.0 4.0 %copy-start.18 = (f32[128,1024]{1,0:T(8,128)S(1)}, f32[128,1024]{1,0:T(8,128)}, u32[]{:S(2)}) copy-start(f32[128,1024]{1,0:T(8,128)} %copy-done.15) | copy-start | bytes 1572868
  217.0 4.0 %copy-start.23 = (f32[128,1024]{1,0:T(8,128)S(1)}, f32[128,1024]{1,0:T(8,128)}, u32[]{:S(2)}) copy-start(f32[128,1024]{1,0:T(8,128)} %copy-done.20) | copy-start | bytes 1572868
  227.9 1.2 copy-start.40
  229.1 1.2 copy-start.42
  234.0 22.2 %copy-start.57 = (f32[512,128]{1,0:T(8,128)}, f32[512,128]{1,0:T(8,128)S(1)}, u32[]{:S(2)}) copy-start(f32[512,128]{1,0:T(8,128)S(1)} %get-tuple-element.71.refs_6_) | copy-start | bytes 786436
  256.2 21.5 %all-to-all-start.7 = ((f32[32,32,128]{2,1,0:T(8,128)}), f32[32,32,128]{2,1,0:T(8,128)}, u32[]{:S(2)}, u32[]{:S(2)}) async-start(f32[32,32,128]{2,1,0:T(8,128)} %get-tuple-element.66), calls=%async_computation.7 | async-start | bytes 1048576 | tf_op jit(solution)/shard_map/all_to_all | solution.py:341
  264.7 1.0 copy-start.14
  267.8 9.9 %copy-start.49 = (f32[512,128]{1,0:T(8,128)S(1)}, f32[512,128]{1,0:T(8,128)}, u32[]{:S(2)}) copy-start(f32[512,128]{1,0:T(8,128)} %copy-done.47) | copy-start | bytes 786436
  277.7 1.2 copy-start.29
  (30 other events, 28.7 us)

commit v3 on v2

v3 whole, which is shorter than its diff:
```python
import functools

import jax
import jax.numpy as jnp
from jax import lax
from jax.experimental import pallas as pl
from jax.experimental.pallas import tpu as pltpu
from jax.sharding import Mesh, PartitionSpec as P


C = 640
LANES = 128
XZ = ("x", "z")
F32 = jnp.float32
BF16 = jnp.bfloat16
VMEM = pl.BlockSpec(memory_space=pltpu.VMEM)
SMEM = pl.BlockSpec(memory_space=pltpu.SMEM)


def room(mib):
    return pltpu.CompilerParams(vmem_limit_bytes=mib << 20)


def dot(left, right):
    return jnp.dot(left, right, preferred_element_type=F32)


def dot_t(left, right):
    return lax.dot_general(left, right, (((1,), (1,)), ((), ())), preferred_element_type=F32)


def swap_cores(value):
    return lax.ppermute(value, "core", [(0, 1), (1, 0)])


def prepare_kernel(gram_ref, x_ref, z0_ref, z1_ref, x0_ref, x1_ref):
    step = pl.program_id(0)
    gram = gram_ref[0]
    high = gram.astype(BF16)
    rest = gram - high.astype(F32)
    mid = rest.astype(BF16)
    low = (rest - mid.astype(F32)).astype(BF16)
    x = x_ref[...]
    zt = (dot_t(low, x) + dot_t(mid, x)) + dot_t(high, x)
    tile = zt.shape[0]
    per_half = z0_ref.shape[0] // tile

    @pl.when(step < per_half)
    def _():
        z0_ref[pl.ds(pl.multiple_of(step * tile, tile), tile), :] = zt

    @pl.when(step >= per_half)
    def _():
        z1_ref[pl.ds(pl.multiple_of((step - per_half) * tile, tile), tile), :] = zt

    @pl.when(step == 0)
    def _():
        half = x0_ref.shape[0]
        x0_ref[...] = x[:half].astype(F32)
        x1_ref[...] = x[half:].astype(F32)


def prepare(features, inv_gram, tile=256):
    rows, width = features.shape
    z_shape = (width // 2, rows)
    x_shape = (rows // 2, width)
    return pl.pallas_call(
        prepare_kernel,
        grid=(width // tile,),
        in_specs=[
            pl.BlockSpec((1, tile, width), lambda i: (0, i, 0)),
            pl.BlockSpec((rows, width), lambda i: (0, 0)),
        ],
        out_specs=[pl.BlockSpec(z_shape, lambda i: (0, 0))] * 2
        + [pl.BlockSpec(x_shape, lambda i: (0, 0))] * 2,
        out_shape=[jax.ShapeDtypeStruct(z_shape, F32)] * 2
        + [jax.ShapeDtypeStruct(x_shape, F32)] * 2,
        compiler_params=room(24),
    )(inv_gram, features)


def held(shape, dtype=F32):
    return pltpu.VMEM(shape, dtype)


def near(value):
    return pltpu.with_memory_space_constraint(value, pltpu.VMEM)


def far(value):
    return pltpu.with_memory_space_constraint(value, pltpu.HBM)


ANY = pl.BlockSpec(memory_space=pl.ANY)


def start_fetch(slot_ref, refs, landing, sems):
    for slot in range(len(refs) // 4):

        @pl.when(slot_ref[0] == slot)
        def _():
            for q in range(4):
                pltpu.make_async_copy(refs[slot * 4 + q], landing.at[q], sems.at[q]).start()


def wait_fetch(refs, landing, sems):
    for q in range(4):
        pltpu.make_async_copy(refs[q], landing.at[q], sems.at[q]).wait()


def landing_of(quarters):
    return [pltpu.VMEM((4,) + quarters[0].shape, F32), pltpu.SemaphoreType.DMA((4,))]


def partial_sum(landing, scaled):
    half = scaled.shape[0] // 2
    parts = []
    for h in range(2):
        total = None
        for k in range(2):
            value = landing[k * 2 + h]
            high = value.astype(BF16)
            low = (value - high.astype(F32)).astype(BF16)
            right = scaled[k * half : (k + 1) * half]
            part = dot(low, right) + dot(high, right)
            total = part if total is None else total + part
        parts.append(total)
    return parts


def put_pieces(out_ref, parts, chunk):
    for h, part in enumerate(parts):
        count = part.shape[0] // chunk
        out_ref[h * count : (h + 1) * count, :chunk, :] = part.reshape(count, chunk, LANES)


def label_parts(lab, slices, width):
    group = jnp.zeros_like(lab)
    for d in range(1, slices):
        group = group + (lab >= d * width).astype(jnp.int32)
    return group, lab - group * width


def first_kernel(slices, slice_ref, slot_ref, lab_ref, labt_ref, *refs):
    z_refs, (out_ref, landing, sems) = refs[:-3], refs[-3:]
    start_fetch(slot_ref, z_refs, landing, sems)
    width = C // slices
    lab = lab_ref[...]
    group, low_label = label_parts(lab, slices, width)
    lane = lax.broadcasted_iota(jnp.int32, (lab.shape[0], LANES), 1)
    low_hot = jnp.where(low_label == lane, 1.0, 0.0)
    onehot = jnp.where(group == slice_ref[0], low_hot, 0.0).astype(BF16)
    labt = labt_ref[...]
    first = lax.broadcasted_iota(jnp.int32, (slices, labt.shape[1]), 0) * width
    group_hot = jnp.where((labt >= first) & (labt < first + width), 1.0, 0.0).astype(BF16)
    counts = dot(group_hot, low_hot.astype(BF16))
    chips, deep, _ = out_ref.shape
    out_ref[:, deep - slices :, :] = jnp.broadcast_to(counts[None], (chips, slices, LANES))
    wait_fetch(z_refs, landing, sems)
    put_pieces(out_ref, partial_sum(landing, onehot), deep - slices)


def middle_kernel(total_rows, slice_ref, in_ref, *out_refs):
    summed = jnp.sum(in_ref[...], axis=0)
    solved_ref, copies_ref = out_refs[0], out_refs[1]
    chunk = solved_ref.shape[0]
    solved = summed[:chunk]
    if len(out_refs) == 3:
        totals = summed[chunk:]
        out_refs[2][...] = totals
        row = lax.broadcasted_iota(jnp.int32, totals.shape, 0)
        mine = jnp.sum(jnp.where(row == slice_ref[0], totals, 0.0), axis=0, keepdims=True)
        scale = jnp.where(mine > 0.0, total_rows / (C * jnp.maximum(mine, 1.0)), 0.0)
        solved = solved * scale.astype(BF16).astype(F32)
    solved_ref[...] = solved
    copies_ref[...] = jnp.broadcast_to(solved[None], copies_ref.shape)


def middle(slices, total_rows, slice_index, arrived, chunk):
    chips, deep, _ = arrived.shape
    shapes = [held((chunk, LANES)), held((chips, chunk, LANES))]
    if deep > chunk:
        shapes.append(held((slices, LANES)))
    return pl.pallas_call(
        functools.partial(middle_kernel, total_rows),
        in_specs=[SMEM, VMEM],
        out_specs=[VMEM] * len(shapes),
        out_shape=shapes,
        compiler_params=room(8),
    )(slice_index, near(arrived))


def update(everyone_ref, landing, residual):
    solved = everyone_ref[...].reshape(-1, LANES).astype(BF16)
    product = dot(landing[...].reshape(-1, landing.shape[2]).astype(BF16), solved)
    return residual - product


def second_kernel(
    slices, total_rows, count, slice_ref, x_slot_ref, z_slot_ref, lab_ref, totals_ref,
    everyone_ref, *refs,
):
    x_refs, z_refs = refs[:count], refs[count : 2 * count]
    residual_ref, weight_ref, out_ref, x_land, x_sems, z_land, z_sems = refs[2 * count :]
    start_fetch(x_slot_ref, x_refs, x_land, x_sems)
    start_fetch(z_slot_ref, z_refs, z_land, z_sems)
    width = C // slices
    lab = lab_ref[...]
    group, low_label = label_parts(lab, slices, width)
    lane = lax.broadcasted_iota(jnp.int32, (lab.shape[0], LANES), 1)
    hit = low_label == lane
    spread = jnp.zeros((lab.shape[0], LANES), F32)
    for d in range(slices):
        spread = jnp.where(group == d, totals_ref[d : d + 1, :], spread)
    row_count = jnp.sum(jnp.where(hit, spread, 0.0), axis=1, keepdims=True)
    weight = total_rows / (C * row_count)
    weight_ref[...] = jnp.broadcast_to(weight, weight_ref.shape)
    onehot = jnp.where(hit & (group == slice_ref[0]), 1.0, 0.0)
    wait_fetch(x_refs, x_land, x_sems)
    residual = update(everyone_ref, x_land, onehot)
    residual_ref[...] = residual
    wait_fetch(z_refs, z_land, z_sems)
    put_pieces(out_ref, partial_sum(z_land, (weight * residual).astype(BF16)), out_ref.shape[1])


def step_kernel(count, x_slot_ref, z_slot_ref, everyone_ref, old_ref, weight_ref, *refs):
    x_refs, z_refs = refs[:count], refs[count : 2 * count]
    residual_ref, out_ref, x_land, x_sems, z_land, z_sems = refs[2 * count :]
    start_fetch(x_slot_ref, x_refs, x_land, x_sems)
    start_fetch(z_slot_ref, z_refs, z_land, z_sems)
    wait_fetch(x_refs, x_land, x_sems)
    residual = update(everyone_ref, x_land, old_ref[...])
    residual_ref[...] = residual
    scaled = (weight_ref[...] * residual).astype(BF16)
    wait_fetch(z_refs, z_land, z_sems)
    put_pieces(out_ref, partial_sum(z_land, scaled), out_ref.shape[1])


def last_kernel(blocks, count, core_ref, x_slot_ref, everyone_ref, *refs):
    solved_refs, refs = refs[:blocks], refs[blocks:]
    rows_refs, refs = refs[: blocks - 1], refs[blocks - 1 :]
    x_refs, (out_ref, x_land, x_sems) = refs[:count], refs[count:]
    start_fetch(x_slot_ref, x_refs, x_land, x_sems)
    rows = rows_refs[0].shape[0] // 2
    half = solved_refs[0].shape[0] // 2
    for b in range(blocks):
        for k in range(2):
            out_ref[2 * b + k, :half] = solved_refs[b][k * half : (k + 1) * half]
            if b < blocks - 1:
                begin = pl.multiple_of(jnp.where(core_ref[0] == k, 0, rows), rows)
                out_ref[2 * b + k, half:] = rows_refs[b][pl.ds(begin, rows), :]
    wait_fetch(x_refs, x_land, x_sems)
    last = update(everyone_ref, x_land, rows_refs[-1][...])
    for k in range(2):
        mine = jnp.where(core_ref[0] == k, last[:rows], last[rows:])
        out_ref[2 * blocks - 2 + k, half:] = mine


def join_kernel(in_ref, weights_ref, after_ref):
    slices = in_ref.shape[0]
    width = C // slices
    head = weights_ref.shape[0]
    for d in range(slices):
        weights_ref[:, d * width : (d + 1) * width] = in_ref[d, :head, :width]
        after_ref[0, :, d * width : (d + 1) * width] = in_ref[d, head:, :width]


def shifted(value, by):
    count = lax.axis_size("feat")
    return lax.ppermute(value, "feat", [(i, (i + by) % count) for i in range(count)])


def exchange(value):
    return lax.all_to_all(value, XZ, 0, 0, tiled=True)


def tie(values, *others):
    return lax.optimization_barrier((*values, *others))[: len(values)]


def local(features, labels, inv_gram):
    rows_here, block_width = features.shape
    blocks = lax.axis_size("feat")
    cores = lax.axis_size("core")
    chips = lax.axis_size("x") * lax.axis_size("z")
    slices = blocks * cores
    chunk = block_width // chips
    core = lax.axis_index("core").astype(jnp.int32)
    feat = lax.axis_index("feat").astype(jnp.int32)
    core_index = core[None]
    slice_index = (feat * cores + core)[None]
    total_rows = float(rows_here * chips * cores)
    both = cores * rows_here

    def slot(b):
        return lax.rem(feat + (blocks - b), blocks)[None]

    z0, z1, x0, x1 = prepare(features, inv_gram)
    lab_other = swap_cores(labels)
    lab = jnp.concatenate([labels, lab_other])
    lab_column, lab_row = lab[:, None], lab[None, :]

    z_up0, z_down1 = shifted(z0, 1), shifted(z1, -1)
    z0s, z1s = swap_cores(z0), swap_cores(z1)
    z0_late, z1_late = tie((z0, z1), z0s, z1s)
    z_up1, z_down0 = shifted(z1_late, 1), shifted(z0_late, -1)
    z_far0, z_far1 = shifted(z_up0, 1), shifted(z_down1, -1)
    x0, x1 = tie((x0, x1), z_up0, z_down1)
    z_all = [
        z0, z1, z0s, z1s,
        z_up0, z_up1, swap_cores(z_up0), swap_cores(z_up1),
        z_far0, z_far1, swap_cores(z_far0), swap_cores(z_far1),
        z_down0, z_down1, swap_cores(z_down0), swap_cores(z_down1),
    ]
    z_all = [far(z) for z in z_all]
    x0s, x1s = swap_cores(x0), swap_cores(x1)
    x_up0, x_down1 = shifted(x0, 1), shifted(x1, -1)
    x0_late, x1_late = tie((x0, x1), x0s, x1s)
    x_up1 = shifted(x1_late, 1)
    x_down0 = shifted(x0_late, -1)

    pieces = pl.pallas_call(
        functools.partial(first_kernel, slices),
        in_specs=[SMEM, SMEM, VMEM, VMEM] + [ANY] * len(z_all),
        out_specs=VMEM,
        out_shape=held((chips, chunk + slices, LANES)),
        scratch_shapes=landing_of(z_all),
        compiler_params=room(12),
    )(slice_index, slot(0), lab_column, lab_row, *z_all)

    kept_rows = []
    kept_solved = []
    totals = weight = x_all = None
    for b in range(blocks):
        arrived = exchange(pieces)
        if b == 0:
            arrived, x_up0, x_down1, x_up1, x_down0 = lax.optimization_barrier(
                (arrived, x_up0, x_down1, x_up1, x_down0)
            )
            x_far0, x_far1 = shifted(x_up0, 1), shifted(x_down1, -1)
            x_near = [x_up0, x_up1, swap_cores(x_up0), swap_cores(x_up1)]
            x_next = [x_down0, x_down1, swap_cores(x_down0), swap_cores(x_down1)]
        result = middle(slices, total_rows, slice_index, arrived, chunk)
        kept_solved.append(result[0])
        if b == 0:
            totals = result[2]
        everyone = exchange(result[1])
        if b == 0:
            everyone, x_far0, x_far1, *x_others = lax.optimization_barrier(
                (everyone, x_far0, x_far1, *x_near, *x_next)
            )
            x_all = [x0, x1, x0s, x1s, *x_others[:4]]
            x_all += [x_far0, x_far1, swap_cores(x_far0), swap_cores(x_far1), *x_others[4:]]
            x_all = [far(x) for x in x_all]
        count = len(x_all)
        if b == 0:
            residual, weight, pieces = pl.pallas_call(
                functools.partial(second_kernel, slices, total_rows, count),
                in_specs=[SMEM] * 3 + [VMEM] * 3 + [ANY] * 2 * count,
                out_specs=[VMEM] * 3,
                out_shape=[held((both, LANES)), held((both, LANES)), held((chips, chunk, LANES))],
                scratch_shapes=landing_of(x_all) + landing_of(z_all),
                compiler_params=room(16),
            )(slice_index, slot(b), slot(b + 1), lab_column, near(totals), near(everyone),
              *x_all, *z_all)
            kept_rows.append(residual)
        elif b < blocks - 1:
            residual, pieces = pl.pallas_call(
                functools.partial(step_kernel, count),
                in_specs=[SMEM] * 2 + [VMEM] * 3 + [ANY] * 2 * count,
                out_specs=[VMEM] * 2,
                out_shape=[held((both, LANES)), held((chips, chunk, LANES))],
                scratch_shapes=landing_of(x_all) + landing_of(z_all),
                compiler_params=room(16),
            )(slot(b), slot(b + 1), near(everyone), near(kept_rows[-1]), near(weight),
              *x_all, *z_all)
            kept_rows.append(residual)
        else:
            sends = pl.pallas_call(
                functools.partial(last_kernel, blocks, count),
                in_specs=[SMEM] * 2 + [VMEM] * (1 + blocks + len(kept_rows)) + [ANY] * count,
                out_specs=VMEM,
                out_shape=held((slices, chunk // cores + rows_here, LANES)),
                scratch_shapes=landing_of(x_all),
                compiler_params=room(12),
            )(core_index, slot(b), *map(near, (everyone, *kept_solved, *kept_rows)), *x_all)

    got = near(lax.all_to_all(sends, ("feat", "core"), 0, 0, tiled=True))
    return pl.pallas_call(
        join_kernel,
        in_specs=[VMEM],
        out_specs=[VMEM, VMEM],
        out_shape=[
            jax.ShapeDtypeStruct((chunk // cores, C), F32),
            jax.ShapeDtypeStruct((1, rows_here, C), F32),
        ],
        compiler_params=room(12),
    )(got)


def solution(mesh):
    sizes = dict(mesh.shape)
    fine = Mesh(mesh.devices.reshape(sizes["feat"], 4, 8, 2), ("feat", "x", "z", "core"))
    rows = ("x", "z", "core")
    in_specs = (P(rows, "feat"), P(rows), P("feat", None, None))
    out_specs = (P(("feat",) + rows, None), P("feat", rows, None))

    return jax.shard_map(local, mesh=fine, in_specs=in_specs, out_specs=out_specs, check_vma=False)
```

time: 309 us -> 299 us (0.968)
  local copies, waits for them, and re-layouts: 44.1 us -> 5.87 us
  blocking collectives: 86.9 us -> 112 us
  waiting for transfers between devices: 68.2 us -> 87.6 us
  starting transfers between devices: 77.4 us -> 69.5 us
  Pallas kernels: 29.2 us -> 22.3 us
    unnamed x121 -> x45, local copies, waits for them, and re-layouts: 43.9 us -> 5.7 us
    all_to_all x3 -> x4, blocking collectives: 63.4 us -> 86.9 us  [exchange(): return lax.all_to_all(value, XZ, 0, 0, tiled=True)]
    ppermute x12, waiting for transfers between devices: 44.5 us -> 55.8 us  [shifted(): lax.ppermute(value, 'feat', [(i, (i + by) % count) for i in range(count)])]
    all_to_all x5 -> x4, starting transfers between devices: 45.9 us -> 35 us  [exchange(): return lax.all_to_all(value, XZ, 0, 0, tiled=True)]
    pallas_call x17 -> x9, Pallas kernels: 25.4 us -> 18.5 us  [the longest x2 6.76 us: local(): pl.pallas_call(functools.partial(step_kernel, count), in_specs=[SMEM] * 2...]
    all_to_all x5 -> x4, waiting for transfers between devices: 21.2 us -> 27.5 us  [exchange(): return lax.all_to_all(value, XZ, 0, 0, tiled=True)]
  transfers between devices with their start and end apart: 34 -> 33, of which waited for: 12 -> 13; matrix products, arithmetic and copies ran while one was open for 0% -> 0% of each run, Pallas kernels for 4% -> 0%
where the time goes in v3:
time: 299 us; the launch traced here: 298 us
  blocking collectives  112 us (37%)
  waiting for transfers between devices  87.6 us (29%)
  starting transfers between devices  69.5 us (23%)
  Pallas kernels  22.3 us (7%)
  local copies, waits for them, and re-layouts  5.87 us (2%)
    all_to_all x4, blocking collectives, exchange(): return lax.all_to_all(value, XZ, 0, 0, tiled=True)  86.9 us
    ppermute x12, waiting for transfers between devices, shifted(): lax.ppermute(value, 'feat', [(i, (i + by) % count) for i in range(count)])  55.8 us
    all_to_all x4, starting transfers between devices, exchange(): return lax.all_to_all(value, XZ, 0, 0, tiled=True)  35 us
    all_to_all x4, waiting for transfers between devices, exchange(): return lax.all_to_all(value, XZ, 0, 0, tiled=True)  27.5 us
    all_to_all x1, blocking collectives, local(): got = near(lax.all_to_all(sends, ('feat', 'core'), 0, 0, tiled=True))  24.8 us
    ppermute x12, starting transfers between devices, shifted(): lax.ppermute(value, 'feat', [(i, (i + by) % count) for i in range(count)])  17.4 us
    ppermute x17, starting transfers between devices, swap_cores(): return lax.ppermute(value, 'core', [(0, 1), (1, 0)])  17.2 us
    pallas_call x2, Pallas kernels, local(): pl.pallas_call(functools.partial(step_kernel, count), in_specs=[SMEM] * 2...  6.76 us
  transfers between devices with their start and end apart: 33, of which 13 were waited for; matrix products, arithmetic and copies ran while one was open for 0% of the time, Pallas kernels for 0%

profile of v3, /device:TPU:1, one launch (start us, length us, event | category | flops | bytes accessed | tf_op | source)
XLA Modules:
  0.0 297.9 jit_solution(9988284694888741036)
XLA Ops:
  0.6 2.2 copy-done.4
  2.8 1.0 copy-done.5
  3.9 2.7 shard_map.50
  6.6 3.3 %collective-permute-start.1 = (f32[512,256]{1,0:T(8,128)S(1)}, f32[512,256]{1,0:T(8,128)S(1)}, u32[]{:S(2)}, u32[]{:S(2)}) collective-permute-start(f32[512,256]{1,0:T(8,128)S(1)} %get-tuple-element.47.refs_0_.refs_16_), channel_id=1, source_target_pairs={{0,1},{1,0},{2,3},{3,2},{4,5},{5,4},{6,7},{7,6},{8,9},{9,8},{10,11... | collective-permute-start | bytes 1572872 | tf_op jit(solution)/shard_map/ppermute | solution.py:33
  9.8 0.1 collective-permute-start.2
  10.0 2.7 collective-permute-start.8
  12.6 1.0 collective-permute-start
  13.6 10.6 %collective-permute-done.3.refs_4_.refs_20_ = f32[512,256]{1,0:T(8,128)S(1)} collective-permute-done((f32[512,256]{1,0:T(8,128)S(1)}, f32[512,256]{1,0:T(8,128)S(1)}, u32[]{:S(2)}, u32[]{:S(2)}) %collective-permute-start.3) | collective-permute-done | bytes 524320 | tf_op jit(solution)/shard_map/ppermute | solution.py:270
  24.2 1.3 collective-permute-start.5
  25.5 3.0 collective-permute-start.9
  28.5 2.7 collective-permute-start.12
  31.1 6.6 %collective-permute-done.7.refs_8_.refs_24_ = f32[512,256]{1,0:T(8,128)} collective-permute-done((f32[512,256]{1,0:T(8,128)S(1)}, f32[512,256]{1,0:T(8,128)}, u32[]{:S(2)}, u32[]{:S(2)}) %collective-permute-start.7) | collective-permute-done | bytes 524320 | tf_op jit(solution)/shard_map/ppermute | solution.py:270
  37.8 3.8 %collective-permute-start.14 = (f32[512,256]{1,0:T(8,128)}, f32[512,256]{1,0:T(8,128)}, u32[]{:S(2)}, u32[]{:S(2)}) collective-permute-start(f32[512,256]{1,0:T(8,128)} %collective-permute-done.8.refs_13_.refs_29_), channel_id=1, source_target_pairs={{0,1},{1,0},{2,3},{3,2},{4,5},{5,4},{6,7},{7,6},{8,9},{9,8},{10,11... | collective-permute-start | bytes 1572872 | tf_op jit(solution)/shard_map/ppermute | solution.py:33
  41.6 0.1 collective-permute-start.10
  41.7 0.4 collective-permute-start.11
  42.1 6.9 %collective-permute-done.4.refs_5_.refs_21_ = f32[512,256]{1,0:T(8,128)} collective-permute-done((f32[512,256]{1,0:T(8,128)S(1)}, f32[512,256]{1,0:T(8,128)}, u32[]{:S(2)}, u32[]{:S(2)}) %collective-permute-start.4) | collective-permute-done | bytes 524320 | tf_op jit(solution)/shard_map/ppermute | solution.py:270
  49.0 2.1 collective-permute-start.6
  51.1 0.1 collective-permute-done.12.refs_12_.refs_28_
  51.2 0.9 collective-permute-start.13
  52.1 0.1 copy.6.lab_ref
  52.3 0.7 collective-permute-done.6.refs_7_.refs_23_
  53.0 0.9 collective-permute-done.13.refs_14_.refs_30_
  53.9 3.2 %shard_map.51 = f32[32,40,128]{2,1,0:T(8,128)} custom-call(s32[1]{0:T(128)} %bitcast.2.slice_ref, s32[1]{0:T(128)} %bitcast.5.slot_ref.x_slot_ref, s32[512,1]{1,0:T(8,128)S(1)} %copy.6.lab_ref, s32[1,512]{1,0:T(1,128)S(1)} %bitcast.9, f32[512,256]{1,0:T(8,128)} %copy-done.2, f32[512,256]{1,0:T(8,128)} %copy-done.3, f32[512,256]{1,0:T(8,128)} %copy-done.17, ...), custom_call_target="tpu_custom_call" | custom-call | tf_op jit(solution)/shard_map/pallas_call | solution.py:322
  57.1 9.4 %all-to-all-start = ((f32[32,40,128]{2,1,0:T(8,128)}), f32[32,40,128]{2,1,0:T(8,128)S(1)}, u32[]{:S(2)}, u32[]{:S(2)}) async-start(f32[32,40,128]{2,1,0:T(8,128)} %shard_map.51), calls=%async_computation | async-start | bytes 1310720 | tf_op jit(solution)/shard_map/all_to_all | solution.py:274
  66.5 0.9 collective-permute-start.17
  67.5 0.1 collective-permute-start.18
  67.6 1.1 collective-permute-start.15
  68.6 2.6 collective-permute-start.16
  71.2 0.1 collective-permute-start.19
  71.3 2.7 collective-permute-start.20
  74.0 9.1 %collective-permute-done.15.refs_4_.refs_11_ = f32[128,1024]{1,0:T(8,128)S(1)} collective-permute-done((f32[128,1024]{1,0:T(8,128)S(1)}, f32[128,1024]{1,0:T(8,128)S(1)}, u32[]{:S(2)}, u32[]{:S(2)}) %collective-permute-start.15) | collective-permute-done | bytes 524320 | tf_op jit(solution)/shard_map/ppermute | solution.py:270
  83.1 11.2 %collective-permute-done.19.refs_5_.refs_12_ = f32[128,1024]{1,0:T(8,128)S(1)} collective-permute-done((f32[128,1024]{1,0:T(8,128)S(1)}, f32[128,1024]{1,0:T(8,128)S(1)}, u32[]{:S(2)}, u32[]{:S(2)}) %collective-permute-start.19) | collective-permute-done | bytes 524320 | tf_op jit(solution)/shard_map/ppermute | solution.py:270
  94.3 0.8 copy-done.11
  95.2 1.1 collective-permute-start.24
  96.2 0.9 shard_map.52
  97.2 9.5 %all-to-all-start.1 = ((f32[32,32,128]{2,1,0:T(8,128)}), f32[32,32,128]{2,1,0:T(8,128)S(1)}, u32[]{:S(2)}, u32[]{:S(2)}) async-start(f32[32,32,128]{2,1,0:T(8,128)} %get-tuple-element.56), calls=%async_computation.1 | async-start | bytes 1048576 | tf_op jit(solution)/shard_map/all_to_all | solution.py:274
  106.7 0.4 collective-permute-start.23
  107.1 0.0 collective-permute-start.21
  107.1 0.5 collective-permute-start.25
  107.6 0.0 collective-permute-start.26
  107.6 2.6 collective-permute-start.22
  110.3 11.3 %collective-permute-done.21.refs_8_.refs_15_ = f32[128,1024]{1,0:T(8,128)S(1)} collective-permute-done((f32[128,1024]{1,0:T(8,128)S(1)}, f32[128,1024]{1,0:T(8,128)S(1)}, u32[]{:S(2)}, u32[]{:S(2)}) %collective-permute-start.21) | collective-permute-done | bytes 524320 | tf_op jit(solution)/shard_map/ppermute | solution.py:270
  121.6 0.8 copy-done.13
  122.3 0.8 copy-done.15
  123.1 1.2 collective-permute-start.27
  124.4 1.7 collective-permute-done.27.refs_10_.refs_17_
  126.1 0.9 collective-permute-done.28.refs_11_.refs_18_
  127.0 3.8 %shard_map.53 = (f32[512,128]{1,0:T(8,128)S(1)}, f32[512,128]{1,0:T(8,128)S(1)}, f32[32,32,128]{2,1,0:T(8,128)S(1)}) custom-call(s32[1]{0:T(128)} %bitcast.2.slice_ref, s32[1]{0:T(128)} %bitcast.5.slot_ref.x_slot_ref, s32[1]{0:T(128)} %bitcast.4.z_slot_ref.x_slot_ref, s32[512,1]{1,0:T(8,128)S(1)} %copy.6.lab_ref, f32[8,128]{1,0:T(8,128)S(1)} %get-tuple-element.55.totals_ref, ...), custom_call_target="tpu_custom_call" | custom-call | tf_op jit(solution)/shard_map/pallas_call | solution.py:357
  130.8 23.4 %all_to_all.45.in_ref = f32[32,32,128]{2,1,0:T(8,128)S(1)} all-to-all(f32[32,32,128]{2,1,0:T(8,128)S(1)} %get-tuple-element.72), channel_id=1, replica_groups=mesh['feat'=4,'x'=4,'z'=8,'core'=2] {'x','z'}, dimensions={0} | all-to-all | bytes 1048576 | tf_op jit(solution)/shard_map/all_to_all | solution.py:274
  154.2 0.9 shard_map.54
  155.1 8.3 %all-to-all-start.3 = ((f32[32,32,128]{2,1,0:T(8,128)}), f32[32,32,128]{2,1,0:T(8,128)S(1)}, u32[]{:S(2)}, u32[]{:S(2)}) async-start(f32[32,32,128]{2,1,0:T(8,128)} %get-tuple-element.73), calls=%async_computation.3 | async-start | bytes 1048576 | tf_op jit(solution)/shard_map/all_to_all | solution.py:274
  163.4 14.3 %all-to-all-done.3.everyone_ref = f32[32,32,128]{2,1,0:T(8,128)S(1)} async-done(((f32[32,32,128]{2,1,0:T(8,128)}), f32[32,32,128]{2,1,0:T(8,128)S(1)}, u32[]{:S(2)}, u32[]{:S(2)}) %all-to-all-start.3) | async-done | bytes 524320 | tf_op jit(solution)/shard_map/all_to_all | solution.py:274
  177.7 3.4 %shard_map.55 = (f32[512,128]{1,0:T(8,128)S(1)}, f32[32,32,128]{2,1,0:T(8,128)S(1)}) custom-call(s32[1]{0:T(128)} %bitcast.4.z_slot_ref.x_slot_ref, s32[1]{0:T(128)} %bitcast.3.z_slot_ref.x_slot_ref, f32[32,32,128]{2,1,0:T(8,128)S(1)} %all-to-all-done.3.everyone_ref, f32[512,128]{1,0:T(8,128)S(1)} %get-tuple-element.74.old_ref.refs_4_, ...), custom_call_target="tpu_custom_call" | custom-call | tf_op jit(solution)/shard_map/pallas_call | solution.py:368
  181.1 21.0 %all_to_all.46.in_ref = f32[32,32,128]{2,1,0:T(8,128)S(1)} all-to-all(f32[32,32,128]{2,1,0:T(8,128)S(1)} %get-tuple-element.76), channel_id=1, replica_groups=mesh['feat'=4,'x'=4,'z'=8,'core'=2] {'x','z'}, dimensions={0} | all-to-all | bytes 1048576 | tf_op jit(solution)/shard_map/all_to_all | solution.py:274
  202.1 0.9 shard_map.56
  203.0 7.8 %all-to-all-start.5 = ((f32[32,32,128]{2,1,0:T(8,128)}), f32[32,32,128]{2,1,0:T(8,128)S(1)}, u32[]{:S(2)}, u32[]{:S(2)}) async-start(f32[32,32,128]{2,1,0:T(8,128)} %get-tuple-element.77), calls=%async_computation.5 | async-start | bytes 1048576 | tf_op jit(solution)/shard_map/all_to_all | solution.py:274
  210.8 13.2 %all-to-all-done.5.everyone_ref = f32[32,32,128]{2,1,0:T(8,128)S(1)} async-done(((f32[32,32,128]{2,1,0:T(8,128)}), f32[32,32,128]{2,1,0:T(8,128)S(1)}, u32[]{:S(2)}, u32[]{:S(2)}) %all-to-all-start.5) | async-done | bytes 524320 | tf_op jit(solution)/shard_map/all_to_all | solution.py:274
  223.9 3.4 %shard_map.57 = (f32[512,128]{1,0:T(8,128)S(1)}, f32[32,32,128]{2,1,0:T(8,128)S(1)}) custom-call(s32[1]{0:T(128)} %bitcast.3.z_slot_ref.x_slot_ref, s32[1]{0:T(128)} %bitcast.1.z_slot_ref.x_slot_ref, f32[32,32,128]{2,1,0:T(8,128)S(1)} %all-to-all-done.5.everyone_ref, f32[512,128]{1,0:T(8,128)S(1)} %get-tuple-element.78.old_ref.refs_5_, ...), custom_call_target="tpu_custom_call" | custom-call | tf_op jit(solution)/shard_map/pallas_call | solution.py:368
  227.3 21.2 %all_to_all.47.in_ref = f32[32,32,128]{2,1,0:T(8,128)S(1)} all-to-all(f32[32,32,128]{2,1,0:T(8,128)S(1)} %get-tuple-element.79), channel_id=1, replica_groups=mesh['feat'=4,'x'=4,'z'=8,'core'=2] {'x','z'}, dimensions={0} | all-to-all | bytes 1048576 | tf_op jit(solution)/shard_map/all_to_all | solution.py:274
  248.5 0.1 shard_map.58
  248.6 21.4 %all_to_all.48.everyone_ref = f32[32,32,128]{2,1,0:T(8,128)S(1)} all-to-all(f32[32,32,128]{2,1,0:T(8,128)S(1)} %get-tuple-element.80), channel_id=1, replica_groups=mesh['feat'=4,'x'=4,'z'=8,'core'=2] {'x','z'}, dimensions={0} | all-to-all | bytes 1048576 | tf_op jit(solution)/shard_map/all_to_all | solution.py:274
  270.0 2.0 shard_map.59
  272.0 24.8 %all_to_all.49.in_ref = f32[8,272,128]{2,1,0:T(8,128)S(1)} all-to-all(f32[8,272,128]{2,1,0:T(8,128)S(1)} %shard_map.59), channel_id=1, replica_groups=mesh['feat'=4,'x'=4,'z'=8,'core'=2] {'feat','core'}, dimensions={0} | all-to-all | bytes 2228224 | tf_op jit(solution)/shard_map/all_to_all | solution.py:388
  296.8 1.2 shard_map.60
  (66 shorter events, 0.2 us)
Async XLA Ops:
  0.6 2.2 copy-start.4
  2.8 1.0 copy-start.5
  3.9 8.8 %copy-start.21 = (s32[256]{0:T(256)S(1)}, s32[256]{0:T(256)}, u32[]{:S(2)}) copy-start(s32[256]{0:T(256)} %param.4) | copy-start | bytes 3076
  6.5 47.4 %copy-start.2 = (f32[512,256]{1,0:T(8,128)}, f32[512,256]{1,0:T(8,128)S(1)}, u32[]{:S(2)}) copy-start(f32[512,256]{1,0:T(8,128)S(1)} %get-tuple-element.47.refs_0_.refs_16_) | copy-start | bytes 1572868
  6.5 47.4 %copy-start.3 = (f32[512,256]{1,0:T(8,128)}, f32[512,256]{1,0:T(8,128)S(1)}, u32[]{:S(2)}) copy-start(f32[512,256]{1,0:T(8,128)S(1)} %get-tuple-element.46.refs_1_.refs_17_) | copy-start | bytes 1572868
  6.5 64.7 %copy-start.1 = (f32[128,1024]{1,0:T(8,128)}, f32[128,1024]{1,0:T(8,128)S(1)}, u32[]{:S(2)}) copy-start(f32[128,1024]{1,0:T(8,128)S(1)} %get-tuple-element.52.refs_1_.refs_8_) | copy-start | bytes 1572868
  6.6 64.8 %copy-start = (f32[128,1024]{1,0:T(8,128)}, f32[128,1024]{1,0:T(8,128)S(1)}, u32[]{:S(2)}) copy-start(f32[128,1024]{1,0:T(8,128)S(1)} %get-tuple-element.53.refs_0_.refs_7_) | copy-start | bytes 1572868
  6.6 7.0 %collective-permute-start.1 = (f32[512,256]{1,0:T(8,128)S(1)}, f32[512,256]{1,0:T(8,128)S(1)}, u32[]{:S(2)}, u32[]{:S(2)}) collective-permute-start(f32[512,256]{1,0:T(8,128)S(1)} %get-tuple-element.47.refs_0_.refs_16_), channel_id=1, source_target_pairs={{0,1},{1,0},{2,3},{3,2},{4,5},{5,4},{6,7},{7,6},{8,9},{9,8},{10,11... | collective-permute-start | bytes 1572872 | tf_op jit(solution)/shard_map/ppermute | solution.py:33
  9.8 3.8 %collective-permute-start.2 = (f32[512,256]{1,0:T(8,128)S(1)}, f32[512,256]{1,0:T(8,128)S(1)}, u32[]{:S(2)}, u32[]{:S(2)}) collective-permute-start(f32[512,256]{1,0:T(8,128)S(1)} %get-tuple-element.46.refs_1_.refs_17_), channel_id=1, source_target_pairs={{0,1},{1,0},{2,3},{3,2},{4,5},{5,4},{6,7},{7,6},{8,9},{9,8},{10,11... | collective-permute-start | bytes 1572872 | tf_op jit(solution)/shard_map/ppermute | solution.py:33
  10.0 14.3 %collective-permute-start.3 = (f32[512,256]{1,0:T(8,128)S(1)}, f32[512,256]{1,0:T(8,128)S(1)}, u32[]{:S(2)}, u32[]{:S(2)}) collective-permute-start(f32[512,256]{1,0:T(8,128)S(1)} %get-tuple-element.47.refs_0_.refs_16_), channel_id=1, source_target_pairs={{0,64},{64,128},{128,192},{192,0},{1,65},{65,129},{129,193},{193,1... | collective-permute-start | bytes 1572872 | tf_op jit(solution)/shard_map/ppermute | solution.py:270
  10.0 15.6 %collective-permute-start.8 = (f32[512,256]{1,0:T(8,128)S(1)}, f32[512,256]{1,0:T(8,128)}, u32[]{:S(2)}, u32[]{:S(2)}) collective-permute-start(f32[512,256]{1,0:T(8,128)S(1)} %get-tuple-element.46.refs_1_.refs_17_), channel_id=1, source_target_pairs={{0,192},{64,0},{128,64},{192,128},{1,193},{65,1},{129,65},{193,129... | collective-permute-start | bytes 1572872 | tf_op jit(solution)/shard_map/ppermute | solution.py:270
  12.6 15.8 %collective-permute-start = (s32[256]{0:T(256)S(1)}, s32[256]{0:T(256)S(1)}, u32[]{:S(2)}, u32[]{:S(2)}) collective-permute-start(s32[256]{0:T(256)S(1)} %copy-done.21), channel_id=1, source_target_pairs={{0,1},{1,0},{2,3},{3,2},{4,5},{5,4},{6,7},{7,6},{8,9},{9,8},{10,11... | collective-permute-start | bytes 3080 | tf_op jit(solution)/shard_map/ppermute | solution.py:33
  13.6 40.3 %copy-start.17 = (f32[512,256]{1,0:T(8,128)}, f32[512,256]{1,0:T(8,128)S(1)}, u32[]{:S(2)}) copy-start(f32[512,256]{1,0:T(8,128)S(1)} %collective-permute-done.1.refs_2_.refs_18_) | copy-start | bytes 1572868
  13.6 40.3 %copy-start.18 = (f32[512,256]{1,0:T(8,128)}, f32[512,256]{1,0:T(8,128)S(1)}, u32[]{:S(2)}) copy-start(f32[512,256]{1,0:T(8,128)S(1)} %collective-permute-done.2.refs_3_.refs_19_) | copy-start | bytes 1572868
  24.2 27.8 %copy-start.19 = (f32[512,256]{1,0:T(8,128)}, f32[512,256]{1,0:T(8,128)S(1)}, u32[]{:S(2)}) copy-start(f32[512,256]{1,0:T(8,128)S(1)} %collective-permute-done.3.refs_4_.refs_20_) | copy-start | bytes 1572868
  24.2 13.5 %collective-permute-start.7 = (f32[512,256]{1,0:T(8,128)S(1)}, f32[512,256]{1,0:T(8,128)}, u32[]{:S(2)}, u32[]{:S(2)}) collective-permute-start(f32[512,256]{1,0:T(8,128)S(1)} %collective-permute-done.3.refs_4_.refs_20_), channel_id=1, source_target_pairs={{0,64},{64,128},{128,192},{192,0},{1,65},{65,129},{129,193},{193,1... | collective-permute-start | bytes 1572872 | tf_op jit(solution)/shard_map/ppermute | solution.py:270
  24.2 17.4 %collective-permute-start.5 = (f32[512,256]{1,0:T(8,128)S(1)}, f32[512,256]{1,0:T(8,128)S(1)}, u32[]{:S(2)}, u32[]{:S(2)}) collective-permute-start(f32[512,256]{1,0:T(8,128)S(1)} %collective-permute-done.3.refs_4_.refs_20_), channel_id=1, source_target_pairs={{0,1},{1,0},{2,3},{3,2},{4,5},{5,4},{6,7},{7,6},{8,9},{9,8},{10,11... | collective-permute-start | bytes 1572872 | tf_op jit(solution)/shard_map/ppermute | solution.py:33
  25.5 16.2 %collective-permute-start.9 = (f32[512,256]{1,0:T(8,128)}, f32[512,256]{1,0:T(8,128)}, u32[]{:S(2)}, u32[]{:S(2)}) collective-permute-start(f32[512,256]{1,0:T(8,128)} %collective-permute-done.8.refs_13_.refs_29_), channel_id=1, source_target_pairs={{0,192},{64,0},{128,64},{192,128},{1,193},{65,1},{129,65},{193,129... | collective-permute-start | bytes 1572872 | tf_op jit(solution)/shard_map/ppermute | solution.py:270
  28.5 20.5 %collective-permute-start.4 = (f32[512,256]{1,0:T(8,128)S(1)}, f32[512,256]{1,0:T(8,128)}, u32[]{:S(2)}, u32[]{:S(2)}) collective-permute-start(f32[512,256]{1,0:T(8,128)S(1)} %get-tuple-element.46.refs_1_.refs_17_), channel_id=1, source_target_pairs={{0,64},{64,128},{128,192},{192,0},{1,65},{65,129},{129,193},{193,1... | collective-permute-start | bytes 1572872 | tf_op jit(solution)/shard_map/ppermute | solution.py:270
  28.5 22.7 %collective-permute-start.12 = (f32[512,256]{1,0:T(8,128)S(1)}, f32[512,256]{1,0:T(8,128)}, u32[]{:S(2)}, u32[]{:S(2)}) collective-permute-start(f32[512,256]{1,0:T(8,128)S(1)} %get-tuple-element.47.refs_0_.refs_16_), channel_id=1, source_target_pairs={{0,192},{64,0},{128,64},{192,128},{1,193},{65,1},{129,65},{193,129... | collective-permute-start | bytes 1572872 | tf_op jit(solution)/shard_map/ppermute | solution.py:270
  37.8 14.5 %collective-permute-start.14 = (f32[512,256]{1,0:T(8,128)}, f32[512,256]{1,0:T(8,128)}, u32[]{:S(2)}, u32[]{:S(2)}) collective-permute-start(f32[512,256]{1,0:T(8,128)} %collective-permute-done.8.refs_13_.refs_29_), channel_id=1, source_target_pairs={{0,1},{1,0},{2,3},{3,2},{4,5},{5,4},{6,7},{7,6},{8,9},{9,8},{10,11... | collective-permute-start | bytes 1572872 | tf_op jit(solution)/shard_map/ppermute | solution.py:33
  41.6 10.4 %copy-start.20 = (f32[512,256]{1,0:T(8,128)}, f32[512,256]{1,0:T(8,128)S(1)}, u32[]{:S(2)}) copy-start(f32[512,256]{1,0:T(8,128)S(1)} %collective-permute-done.5.refs_6_.refs_22_) | copy-start | bytes 1572868
  41.6 10.6 %collective-permute-start.10 = (f32[512,256]{1,0:T(8,128)}, f32[512,256]{1,0:T(8,128)}, u32[]{:S(2)}, u32[]{:S(2)}) collective-permute-start(f32[512,256]{1,0:T(8,128)} %collective-permute-done.7.refs_8_.refs_24_), channel_id=1, source_target_pairs={{0,1},{1,0},{2,3},{3,2},{4,5},{5,4},{6,7},{7,6},{8,9},{9,8},{10,11... | collective-permute-start | bytes 1572872 | tf_op jit(solution)/shard_map/ppermute | solution.py:33
  41.7 10.6 %collective-permute-start.11 = (f32[512,256]{1,0:T(8,128)}, f32[512,256]{1,0:T(8,128)}, u32[]{:S(2)}, u32[]{:S(2)}) collective-permute-start(f32[512,256]{1,0:T(8,128)} %collective-permute-done.9.refs_9_.refs_25_), channel_id=1, source_target_pairs={{0,1},{1,0},{2,3},{3,2},{4,5},{5,4},{6,7},{7,6},{8,9},{9,8},{10,11... | collective-permute-start | bytes 1572872 | tf_op jit(solution)/shard_map/ppermute | solution.py:33
  49.0 4.0 %collective-permute-start.6 = (f32[512,256]{1,0:T(8,128)}, f32[512,256]{1,0:T(8,128)}, u32[]{:S(2)}, u32[]{:S(2)}) collective-permute-start(f32[512,256]{1,0:T(8,128)} %collective-permute-done.4.refs_5_.refs_21_), channel_id=1, source_target_pairs={{0,1},{1,0},{2,3},{3,2},{4,5},{5,4},{6,7},{7,6},{8,9},{9,8},{10,11... | collective-permute-start | bytes 1572872 | tf_op jit(solution)/shard_map/ppermute | solution.py:33
  51.2 2.7 collective-permute-start.13
  57.1 38.1 %all-to-all-start = ((f32[32,40,128]{2,1,0:T(8,128)}), f32[32,40,128]{2,1,0:T(8,128)S(1)}, u32[]{:S(2)}, u32[]{:S(2)}) async-start(f32[32,40,128]{2,1,0:T(8,128)} %shard_map.51), calls=%async_computation | async-start | bytes 1310720 | tf_op jit(solution)/shard_map/all_to_all | solution.py:274
  66.5 4.7 %collective-permute-start.17 = (f32[128,1024]{1,0:T(8,128)S(1)}, f32[128,1024]{1,0:T(8,128)S(1)}, u32[]{:S(2)}, u32[]{:S(2)}) collective-permute-start(f32[128,1024]{1,0:T(8,128)S(1)} %get-tuple-element.53.refs_0_.refs_7_), channel_id=1, source_target_pairs={{0,1},{1,0},{2,3},{3,2},{4,5},{5,4},{6,7},{7,6},{8,9},{9,8},{10,11... | collective-permute-start | bytes 1572872 | tf_op jit(solution)/shard_map/ppermute | solution.py:33
  67.5 3.8 %collective-permute-start.18 = (f32[128,1024]{1,0:T(8,128)S(1)}, f32[128,1024]{1,0:T(8,128)S(1)}, u32[]{:S(2)}, u32[]{:S(2)}) collective-permute-start(f32[128,1024]{1,0:T(8,128)S(1)} %get-tuple-element.52.refs_1_.refs_8_), channel_id=1, source_target_pairs={{0,1},{1,0},{2,3},{3,2},{4,5},{5,4},{6,7},{7,6},{8,9},{9,8},{10,11... | collective-permute-start | bytes 1572872 | tf_op jit(solution)/shard_map/ppermute | solution.py:33
  67.6 15.5 %collective-permute-start.15 = (f32[128,1024]{1,0:T(8,128)S(1)}, f32[128,1024]{1,0:T(8,128)S(1)}, u32[]{:S(2)}, u32[]{:S(2)}) collective-permute-start(f32[128,1024]{1,0:T(8,128)S(1)} %get-tuple-element.53.refs_0_.refs_7_), channel_id=1, source_target_pairs={{0,64},{64,128},{128,192},{192,0},{1,65},{65,129},{129,193},{193,1... | collective-permute-start | bytes 1572872 | tf_op jit(solution)/shard_map/ppermute | solution.py:270
  68.6 14.5 %collective-permute-start.16 = (f32[128,1024]{1,0:T(8,128)S(1)}, f32[128,1024]{1,0:T(8,128)S(1)}, u32[]{:S(2)}, u32[]{:S(2)}) collective-permute-start(f32[128,1024]{1,0:T(8,128)S(1)} %get-tuple-element.52.refs_1_.refs_8_), channel_id=1, source_target_pairs={{0,192},{64,0},{128,64},{192,128},{1,193},{65,1},{129,65},{193,129... | collective-permute-start | bytes 1572872 | tf_op jit(solution)/shard_map/ppermute | solution.py:270
  71.2 55.8 %copy-start.6 = (f32[128,1024]{1,0:T(8,128)}, f32[128,1024]{1,0:T(8,128)S(1)}, u32[]{:S(2)}) copy-start(f32[128,1024]{1,0:T(8,128)S(1)} %collective-permute-done.17.refs_2_.refs_9_) | copy-start | bytes 1572868
  71.2 55.8 %copy-start.7 = (f32[128,1024]{1,0:T(8,128)}, f32[128,1024]{1,0:T(8,128)S(1)}, u32[]{:S(2)}) copy-start(f32[128,1024]{1,0:T(8,128)S(1)} %collective-permute-done.18.refs_3_.refs_10_) | copy-start | bytes 1572868
  71.2 23.1 %collective-permute-start.19 = (f32[128,1024]{1,0:T(8,128)S(1)}, f32[128,1024]{1,0:T(8,128)S(1)}, u32[]{:S(2)}, u32[]{:S(2)}) collective-permute-start(f32[128,1024]{1,0:T(8,128)S(1)} %get-tuple-element.52.refs_1_.refs_8_), channel_id=1, source_target_pairs={{0,64},{64,128},{128,192},{192,0},{1,65},{65,129},{129,193},{193,1... | collective-permute-start | bytes 1572872 | tf_op jit(solution)/shard_map/ppermute | solution.py:270
  71.3 23.8 %collective-permute-start.20 = (f32[128,1024]{1,0:T(8,128)S(1)}, f32[128,1024]{1,0:T(8,128)}, u32[]{:S(2)}, u32[]{:S(2)}) collective-permute-start(f32[128,1024]{1,0:T(8,128)S(1)} %get-tuple-element.53.refs_0_.refs_7_), channel_id=1, source_target_pairs={{0,192},{64,0},{128,64},{192,128},{1,193},{65,1},{129,65},{193,129... | collective-permute-start | bytes 1572872 | tf_op jit(solution)/shard_map/ppermute | solution.py:270
  83.1 11.2 %copy-start.8 = (f32[128,1024]{1,0:T(8,128)}, f32[128,1024]{1,0:T(8,128)S(1)}, u32[]{:S(2)}) copy-start(f32[128,1024]{1,0:T(8,128)S(1)} %collective-permute-done.15.refs_4_.refs_11_) | copy-start | bytes 1572868
  83.1 43.9 %copy-start.10 = (f32[128,1024]{1,0:T(8,128)}, f32[128,1024]{1,0:T(8,128)S(1)}, u32[]{:S(2)}) copy-start(f32[128,1024]{1,0:T(8,128)S(1)} %collective-permute-done.16.refs_13_.refs_20_) | copy-start | bytes 1572868
  94.3 0.8 copy-start.11
  95.2 11.5 %copy-start.9 = (f32[128,1024]{1,0:T(8,128)S(1)}, f32[128,1024]{1,0:T(8,128)}, u32[]{:S(2)}) copy-start(f32[128,1024]{1,0:T(8,128)} %copy-done.8) | copy-start | bytes 1572868
  95.2 12.4 %collective-permute-start.24 = (f32[128,1024]{1,0:T(8,128)}, f32[128,1024]{1,0:T(8,128)}, u32[]{:S(2)}, u32[]{:S(2)}) collective-permute-start(f32[128,1024]{1,0:T(8,128)} %copy-done.11), channel_id=1, source_target_pairs={{0,1},{1,0},{2,3},{3,2},{4,5},{5,4},{6,7},{7,6},{8,9},{9,8},{10,11... | collective-permute-start | bytes 1572872 | tf_op jit(solution)/shard_map/ppermute | solution.py:33
  97.2 26.0 %all-to-all-start.1 = ((f32[32,32,128]{2,1,0:T(8,128)}), f32[32,32,128]{2,1,0:T(8,128)S(1)}, u32[]{:S(2)}, u32[]{:S(2)}) async-start(f32[32,32,128]{2,1,0:T(8,128)} %get-tuple-element.56), calls=%async_computation.1 | async-start | bytes 1048576 | tf_op jit(solution)/shard_map/all_to_all | solution.py:274
  106.7 3.6 %collective-permute-start.23 = (f32[128,1024]{1,0:T(8,128)S(1)}, f32[128,1024]{1,0:T(8,128)S(1)}, u32[]{:S(2)}, u32[]{:S(2)}) collective-permute-start(f32[128,1024]{1,0:T(8,128)S(1)} %copy-done.9), channel_id=1, source_target_pairs={{0,1},{1,0},{2,3},{3,2},{4,5},{5,4},{6,7},{7,6},{8,9},{9,8},{10,11... | collective-permute-start | bytes 1572872 | tf_op jit(solution)/shard_map/ppermute | solution.py:33
  107.1 14.5 %collective-permute-start.21 = (f32[128,1024]{1,0:T(8,128)S(1)}, f32[128,1024]{1,0:T(8,128)S(1)}, u32[]{:S(2)}, u32[]{:S(2)}) collective-permute-start(f32[128,1024]{1,0:T(8,128)S(1)} %copy-done.9), channel_id=1, source_target_pairs={{0,64},{64,128},{128,192},{192,0},{1,65},{65,129},{129,193},{193,1... | collective-permute-start | bytes 1572872 | tf_op jit(solution)/shard_map/ppermute | solution.py:270
  107.1 3.2 %collective-permute-start.25 = (f32[128,1024]{1,0:T(8,128)}, f32[128,1024]{1,0:T(8,128)S(1)}, u32[]{:S(2)}, u32[]{:S(2)}) collective-permute-start(f32[128,1024]{1,0:T(8,128)} %collective-permute-done.20.refs_12_.refs_19_), channel_id=1, source_target_pairs={{0,1},{1,0},{2,3},{3,2},{4,5},{5,4},{6,7},{7,6},{8,9},{9,8},{10,11... | collective-permute-start | bytes 1572872 | tf_op jit(solution)/shard_map/ppermute | solution.py:33
  107.6 13.9 %collective-permute-start.26 = (f32[128,1024]{1,0:T(8,128)S(1)}, f32[128,1024]{1,0:T(8,128)S(1)}, u32[]{:S(2)}, u32[]{:S(2)}) collective-permute-start(f32[128,1024]{1,0:T(8,128)S(1)} %collective-permute-done.16.refs_13_.refs_20_), channel_id=1, source_target_pairs={{0,1},{1,0},{2,3},{3,2},{4,5},{5,4},{6,7},{7,6},{8,9},{9,8},{10,11... | collective-permute-start | bytes 1572872 | tf_op jit(solution)/shard_map/ppermute | solution.py:33
  107.6 15.5 %collective-permute-start.22 = (f32[128,1024]{1,0:T(8,128)S(1)}, f32[128,1024]{1,0:T(8,128)}, u32[]{:S(2)}, u32[]{:S(2)}) collective-permute-start(f32[128,1024]{1,0:T(8,128)S(1)} %collective-permute-done.16.refs_13_.refs_20_), channel_id=1, source_target_pairs={{0,192},{64,0},{128,64},{192,128},{1,193},{65,1},{129,65},{193,129... | collective-permute-start | bytes 1572872 | tf_op jit(solution)/shard_map/ppermute | solution.py:270
  110.3 11.3 %copy-start.14 = (f32[128,1024]{1,0:T(8,128)}, f32[128,1024]{1,0:T(8,128)S(1)}, u32[]{:S(2)}) copy-start(f32[128,1024]{1,0:T(8,128)S(1)} %collective-permute-done.25.refs_14_.refs_21_) | copy-start | bytes 1572868
  110.3 11.3 %copy-start.12 = (f32[128,1024]{1,0:T(8,128)}, f32[128,1024]{1,0:T(8,128)S(1)}, u32[]{:S(2)}) copy-start(f32[128,1024]{1,0:T(8,128)S(1)} %collective-permute-done.23.refs_6_.refs_13_) | copy-start | bytes 1572868
  121.5 0.8 copy-start.13
  122.3 0.8 copy-start.15
  123.1 3.0 collective-permute-start.27
  124.4 2.6 collective-permute-start.28
  126.1 0.9 copy-start.16
  155.1 22.6 %all-to-all-start.3 = ((f32[32,32,128]{2,1,0:T(8,128)}), f32[32,32,128]{2,1,0:T(8,128)S(1)}, u32[]{:S(2)}, u32[]{:S(2)}) async-start(f32[32,32,128]{2,1,0:T(8,128)} %get-tuple-element.73), calls=%async_computation.3 | async-start | bytes 1048576 | tf_op jit(solution)/shard_map/all_to_all | solution.py:274
  203.0 21.0 %all-to-all-start.5 = ((f32[32,32,128]{2,1,0:T(8,128)}), f32[32,32,128]{2,1,0:T(8,128)S(1)}, u32[]{:S(2)}, u32[]{:S(2)}) async-start(f32[32,32,128]{2,1,0:T(8,128)} %get-tuple-element.77), calls=%async_computation.5 | async-start | bytes 1048576 | tf_op jit(solution)/shard_map/all_to_all | solution.py:274

commit v4 on v3

v4 whole, which is shorter than its diff:
```python
import functools

import jax
import jax.numpy as jnp
from jax import lax
from jax.experimental import pallas as pl
from jax.experimental.pallas import tpu as pltpu
from jax.sharding import Mesh, PartitionSpec as P


C = 640
LANES = 128
ROW_TILE = 8
XZ = ("x", "z")
F32 = jnp.float32
BF16 = jnp.bfloat16
VMEM = pl.BlockSpec(memory_space=pltpu.VMEM)
SMEM = pl.BlockSpec(memory_space=pltpu.SMEM)
ANY = pl.BlockSpec(memory_space=pl.ANY)


def room(mib):
    return pltpu.CompilerParams(vmem_limit_bytes=mib << 20)


def dot_t(left, right):
    return lax.dot_general(left, right, (((1,), (1,)), ((), ())), preferred_element_type=F32)


def swap_cores(value):
    return lax.ppermute(value, "core", [(0, 1), (1, 0)])


def prepare_kernel(gram_ref, x_ref, z_ref, xf_ref):
    gram = gram_ref[0]
    high = gram.astype(BF16)
    rest = gram - high.astype(F32)
    mid = rest.astype(BF16)
    low = (rest - mid.astype(F32)).astype(BF16)
    x = x_ref[...]
    z_ref[...] = (dot_t(low, x) + dot_t(mid, x)) + dot_t(high, x)

    @pl.when(pl.program_id(0) == 0)
    def _():
        xf_ref[...] = x.astype(F32)


def prepare(features, inv_gram, tile=256):
    rows, width = features.shape
    return pl.pallas_call(
        prepare_kernel,
        grid=(width // tile,),
        in_specs=[
            pl.BlockSpec((1, tile, width), lambda i: (0, i, 0)),
            pl.BlockSpec((rows, width), lambda i: (0, 0)),
        ],
        out_specs=[
            pl.BlockSpec((tile, rows), lambda i: (i, 0)),
            pl.BlockSpec((rows, width), lambda i: (0, 0)),
        ],
        out_shape=[
            jax.ShapeDtypeStruct((width, rows), F32),
            jax.ShapeDtypeStruct((rows, width), F32),
        ],
        compiler_params=room(24),
    )(inv_gram, features)


def held(shape, dtype=F32):
    return pltpu.VMEM(shape, dtype)


def near(value):
    return pltpu.with_memory_space_constraint(value, pltpu.VMEM)


def far(value):
    return pltpu.with_memory_space_constraint(value, pltpu.HBM)


HELD_BLOCKS = 10


def fetch(slot_ref, refs, landing, sems):
    half = landing.shape[1] // 2
    for slot, first in ((0, 0), (1, 2), (3, 4)):

        @pl.when(slot_ref[0] == slot)
        def _():
            for k in range(2):
                pltpu.make_async_copy(refs[first + k], landing.at[k], sems.at[k]).start()

    @pl.when(slot_ref[0] == 2)
    def _():
        for k in range(2):
            for h in range(2):
                target = landing.at[k, pl.ds(h * half, half)]
                pltpu.make_async_copy(refs[6 + 2 * k + h], target, sems.at[k]).start()


def wait_fetch(refs, landing, sems):
    for k in range(2):
        pltpu.make_async_copy(refs[k], landing.at[k], sems.at[k]).wait()


def landing_of(blocks):
    return [pltpu.VMEM((2,) + blocks[0].shape, F32), pltpu.SemaphoreType.DMA((2,))]


def partial_sum(landing, scaled):
    half = scaled.shape[1] // 2
    total = None
    for k in range(2):
        value = landing[k]
        high = value.astype(BF16)
        low = (value - high.astype(F32)).astype(BF16)
        left = scaled[:, k * half : (k + 1) * half]
        part = dot_t(left, low) + dot_t(left, high)
        total = part if total is None else total + part
    return total


def put_pieces(out_ref, total, chunk):
    tiles = total.shape[1] // LANES
    for g in range(total.shape[0] // chunk):
        for t in range(tiles):
            out_ref[g * tiles + t, :chunk, :] = total[
                g * chunk : (g + 1) * chunk, t * LANES : (t + 1) * LANES
            ]


def take_copies(everyone_ref, groups):
    tiles = everyone_ref.shape[0] // groups
    rows = []
    for g in range(groups):
        rows.append(
            jnp.concatenate([everyone_ref[g * tiles + t] for t in range(tiles)], axis=1)
        )
    return jnp.concatenate(rows, axis=0)


def label_parts(lab, slices, width):
    group = jnp.zeros_like(lab)
    for d in range(1, slices):
        group = group + (lab >= d * width).astype(jnp.int32)
    return group, lab - group * width


def first_kernel(slices, padded, slice_ref, slot_ref, lab_ref, *refs):
    z_refs, (out_ref, landing, sems) = refs[:-3], refs[-3:]
    fetch(slot_ref, z_refs, landing, sems)
    lab = lab_ref[...]
    group, low_label = label_parts(lab, slices, C // slices)
    row = lax.broadcasted_iota(jnp.int32, (LANES, lab.shape[1]), 0)
    low_hot = jnp.where(low_label == row, 1.0, 0.0)
    onehot = jnp.where(group == slice_ref[0], low_hot, 0.0)[:padded].astype(BF16)
    group_row = lax.broadcasted_iota(jnp.int32, (slices, lab.shape[1]), 0)
    group_hot = jnp.where(group == group_row, 1.0, 0.0).astype(BF16)
    counts = dot_t(group_hot, low_hot.astype(BF16))
    chips, deep, _ = out_ref.shape
    chunk = deep - slices
    out_ref[:, chunk:, :] = jnp.broadcast_to(counts[None], (chips, slices, LANES))
    wait_fetch(z_refs, landing, sems)
    put_pieces(out_ref, partial_sum(landing, onehot), chunk)


def middle_kernel(total_rows, slice_ref, part_ref, in_ref, *out_refs):
    summed = jnp.sum(in_ref[...], axis=0)
    copies_ref = out_refs[0]
    chunk = copies_ref.shape[1]
    solved = summed[:chunk]
    if len(out_refs) == 2:
        totals = summed[chunk:]
        out_refs[1][...] = totals
        row = lax.broadcasted_iota(jnp.int32, totals.shape, 0)
        mine = jnp.sum(jnp.where(row == slice_ref[0], totals, 0.0), axis=0, keepdims=True)
        scale = jnp.where(mine > 0.0, total_rows / (C * jnp.maximum(mine, 1.0)), 0.0)
        scale = scale.astype(BF16).astype(F32)
        lane = lax.broadcasted_iota(jnp.int32, (chunk, LANES), 1)
        here = lax.broadcasted_iota(jnp.int32, (chunk, LANES), 0) + part_ref[0] * chunk
        solved = solved * jnp.sum(jnp.where(lane == here, scale, 0.0), axis=1, keepdims=True)
    copies_ref[...] = jnp.broadcast_to(solved[None], copies_ref.shape)


def middle(slices, total_rows, slice_index, part_index, arrived, chunk):
    chips, deep, _ = arrived.shape
    shapes = [held((chips, chunk, LANES))]
    if deep > chunk:
        shapes.append(held((slices, LANES)))
    return pl.pallas_call(
        functools.partial(middle_kernel, total_rows),
        in_specs=[SMEM, SMEM, VMEM],
        out_specs=[VMEM] * len(shapes),
        out_shape=shapes,
        compiler_params=room(8),
    )(slice_index, part_index, near(arrived))


def update(solved, landing, residual):
    rows = landing.shape[1]
    solved = solved.astype(BF16)
    parts = [
        residual[:, k * rows : (k + 1) * rows] - dot_t(solved, landing[k].astype(BF16))
        for k in range(2)
    ]
    return jnp.concatenate(parts, axis=1)


def second_kernel(
    slices, total_rows, groups, slice_ref, x_slot_ref, z_slot_ref, lab_ref, totals_ref,
    everyone_ref, *refs,
):
    x_refs, z_refs = refs[:HELD_BLOCKS], refs[HELD_BLOCKS : 2 * HELD_BLOCKS]
    solved_ref, residual_ref, weight_ref, out_ref = refs[2 * HELD_BLOCKS : 2 * HELD_BLOCKS + 4]
    x_land, x_sems, z_land, z_sems = refs[2 * HELD_BLOCKS + 4 :]
    fetch(x_slot_ref, x_refs, x_land, x_sems)
    fetch(z_slot_ref, z_refs, z_land, z_sems)
    lab = lab_ref[...]
    group, low_label = label_parts(lab, slices, C // slices)
    solved = take_copies(everyone_ref, groups)
    solved_ref[...] = solved
    padded = solved.shape[0]
    row = lax.broadcasted_iota(jnp.int32, (padded, lab.shape[1]), 0)
    hit = low_label == row
    columns = totals_ref[...].T
    spread = jnp.zeros((padded, lab.shape[1]), F32)
    for d in range(slices):
        spread = jnp.where(group == d, columns[:padded, d : d + 1], spread)
    row_count = jnp.sum(jnp.where(hit, spread, 0.0), axis=0, keepdims=True)
    weight = total_rows / (C * row_count)
    weight_ref[...] = jnp.broadcast_to(weight, weight_ref.shape)
    onehot = jnp.where(hit & (group == slice_ref[0]), 1.0, 0.0)
    wait_fetch(x_refs, x_land, x_sems)
    residual = update(solved, x_land, onehot)
    residual_ref[...] = residual
    wait_fetch(z_refs, z_land, z_sems)
    put_pieces(out_ref, partial_sum(z_land, (weight * residual).astype(BF16)), out_ref.shape[1])


def step_kernel(groups, x_slot_ref, z_slot_ref, everyone_ref, old_ref, weight_ref, *refs):
    x_refs, z_refs = refs[:HELD_BLOCKS], refs[HELD_BLOCKS : 2 * HELD_BLOCKS]
    solved_ref, residual_ref, out_ref = refs[2 * HELD_BLOCKS : 2 * HELD_BLOCKS + 3]
    x_land, x_sems, z_land, z_sems = refs[2 * HELD_BLOCKS + 3 :]
    fetch(x_slot_ref, x_refs, x_land, x_sems)
    fetch(z_slot_ref, z_refs, z_land, z_sems)
    solved = take_copies(everyone_ref, groups)
    solved_ref[...] = solved
    wait_fetch(x_refs, x_land, x_sems)
    residual = update(solved, x_land, old_ref[...])
    residual_ref[...] = residual
    scaled = (weight_ref[0:1, :] * residual).astype(BF16)
    wait_fetch(z_refs, z_land, z_sems)
    put_pieces(out_ref, partial_sum(z_land, scaled), out_ref.shape[1])


def last_kernel(
    blocks, groups, width, place_ref, x_slot_ref, everyone_ref, *refs,
):
    solved_refs, refs = refs[: blocks - 1], refs[blocks - 1 :]
    rows_refs, refs = refs[: blocks - 1], refs[blocks - 1 :]
    x_refs, (out_ref, x_land, x_sems, turned) = refs[:HELD_BLOCKS], refs[HELD_BLOCKS:]
    fetch(x_slot_ref, x_refs, x_land, x_sems)
    last_solved = take_copies(everyone_ref, groups)
    rows = x_land.shape[1]
    head = out_ref.shape[1] - width
    share = 2 * head
    for b in range(blocks):
        solved = last_solved if b == blocks - 1 else solved_refs[b][...]
        tile = jnp.zeros((solved.shape[0], LANES), F32)
        for t in range(solved.shape[1] // LANES):
            tile = jnp.where(place_ref[1] == t, solved[:, t * LANES : (t + 1) * LANES], tile)
        empty = jnp.zeros((LANES - tile.shape[0], LANES), F32)
        turned[...] = jnp.concatenate([tile, empty], axis=0).T
        for k in range(2):
            begin = place_ref[2] * (2 * share) + k * share
            begin = pl.multiple_of(begin, ROW_TILE)
            for h in range(2):
                out_ref[2 * b + k, :head, h * LANES : (h + 1) * LANES] = turned[
                    pl.ds(pl.multiple_of(begin + h * head, ROW_TILE), head), :
                ]
    wait_fetch(x_refs, x_land, x_sems)
    last = update(last_solved, x_land, rows_refs[-1][...])
    for b in range(blocks):
        value = last if b == blocks - 1 else rows_refs[b][...]
        for k in range(2):
            mine = jnp.where(place_ref[0] == k, value[:width, :rows], value[:width, rows:])
            out_ref[2 * b + k, head:, :] = mine


def join_kernel(in_ref, weights_ref, after_ref):
    slices, deep, _ = in_ref.shape
    width = C // slices
    head = deep - width
    for d in range(slices):
        for h in range(2):
            weights_ref[h * head : (h + 1) * head, d * width : (d + 1) * width] = in_ref[
                d, :head, h * LANES : h * LANES + width
            ]
    joined = jnp.concatenate([in_ref[d, head:, :] for d in range(slices)], axis=0)
    after_ref[0] = joined.T


def shifted(value, by):
    count = lax.axis_size("feat")
    return lax.ppermute(value, "feat", [(i, (i + by) % count) for i in range(count)])


def exchange(value):
    return lax.all_to_all(value, XZ, 0, 0, tiled=True)


def halves(value):
    middle_row = value.shape[0] // 2
    return value[:middle_row], value[middle_row:]


def local(features, labels, inv_gram):
    rows_here, block_width = features.shape
    blocks = lax.axis_size("feat")
    cores = lax.axis_size("core")
    groups = lax.axis_size("x")
    depth = lax.axis_size("z")
    chips = groups * depth
    slices = blocks * cores
    width = C // slices
    tile_rows = groups * ROW_TILE
    padded = -(-width // tile_rows) * tile_rows
    chunk = padded // groups
    core = lax.axis_index("core").astype(jnp.int32)
    feat = lax.axis_index("feat").astype(jnp.int32)
    x_index = lax.axis_index("x").astype(jnp.int32)
    chip = x_index * depth + lax.axis_index("z").astype(jnp.int32)
    per_tile = LANES * chips // block_width
    place = jnp.stack([core, chip // per_tile, chip % per_tile])
    slice_index = (feat * cores + core)[None]
    part_index = x_index[None]
    total_rows = float(rows_here * chips * cores)
    both = cores * rows_here

    def slot(b):
        return lax.rem(feat + (blocks - b), blocks)[None]

    z_own, x_own = prepare(features, inv_gram)
    lab = jnp.concatenate([labels, swap_cores(labels)])[None, :]

    z_up, z_down = shifted(z_own, 1), shifted(z_own, -1)
    z_pair = [z_own, swap_cores(z_own)]
    z_far0 = shifted(halves(z_up)[0], 1)
    z_far1 = shifted(halves(z_down)[1], -1)
    x_own, _, _ = lax.optimization_barrier((x_own, z_up, z_down))
    z_all = z_pair + [z_up, swap_cores(z_up), z_down, swap_cores(z_down)]
    z_all += [z_far0, z_far1, swap_cores(z_far0), swap_cores(z_far1)]
    z_all = [far(z) for z in z_all]
    x_up, x_down = shifted(x_own, 1), shifted(x_own, -1)

    pieces = pl.pallas_call(
        functools.partial(first_kernel, slices, padded),
        in_specs=[SMEM, SMEM, VMEM] + [ANY] * HELD_BLOCKS,
        out_specs=VMEM,
        out_shape=held((chips, chunk + slices, LANES)),
        scratch_shapes=landing_of(z_all),
        compiler_params=room(12),
    )(slice_index, slot(0), lab, *z_all)

    rows_shape = held((padded, both))
    solved_shape = held((padded, block_width))
    pieces_shape = held((chips, chunk, LANES))
    kept_rows = []
    kept_solved = []
    totals = weight = x_all = x_near = None
    for b in range(blocks):
        arrived = exchange(pieces)
        if b == 0:
            arrived, x_up, x_down, x_own = lax.optimization_barrier(
                (arrived, x_up, x_down, x_own)
            )
            x_far0 = shifted(halves(x_up)[0], 1)
            x_far1 = shifted(halves(x_down)[1], -1)
            x_near = [x_own, swap_cores(x_own), x_up, swap_cores(x_up)]
            x_near += [x_down, swap_cores(x_down)]
        result = middle(slices, total_rows, slice_index, part_index, arrived, chunk)
        if b == 0:
            totals = result[1]
        everyone = exchange(result[0])
        if b == 0:
            everyone, x_far0, x_far1, *x_near = lax.optimization_barrier(
                (everyone, x_far0, x_far1, *x_near)
            )
            x_all = x_near + [x_far0, x_far1, swap_cores(x_far0), swap_cores(x_far1)]
            x_all = [far(x) for x in x_all]
            solved, residual, weight, pieces = pl.pallas_call(
                functools.partial(second_kernel, slices, total_rows, groups),
                in_specs=[SMEM] * 3 + [VMEM] * 3 + [ANY] * 2 * HELD_BLOCKS,
                out_specs=[VMEM] * 4,
                out_shape=[solved_shape, rows_shape, held((ROW_TILE, both)), pieces_shape],
                scratch_shapes=landing_of(x_all) + landing_of(z_all),
                compiler_params=room(16),
            )(slice_index, slot(b), slot(b + 1), lab, near(totals), near(everyone),
              *x_all, *z_all)
        elif b < blocks - 1:
            solved, residual, pieces = pl.pallas_call(
                functools.partial(step_kernel, groups),
                in_specs=[SMEM] * 2 + [VMEM] * 3 + [ANY] * 2 * HELD_BLOCKS,
                out_specs=[VMEM] * 3,
                out_shape=[solved_shape, rows_shape, pieces_shape],
                scratch_shapes=landing_of(x_all) + landing_of(z_all),
                compiler_params=room(16),
            )(slot(b), slot(b + 1), near(everyone), near(kept_rows[-1]), near(weight),
              *x_all, *z_all)
        else:
            head = block_width // (chips * cores) // 2
            sends = pl.pallas_call(
                functools.partial(last_kernel, blocks, groups, width),
                in_specs=[SMEM] * 2 + [VMEM] * (2 * blocks - 1) + [ANY] * HELD_BLOCKS,
                out_specs=VMEM,
                out_shape=held((slices, head + width, rows_here)),
                scratch_shapes=landing_of(x_all) + [pltpu.VMEM((LANES, LANES), F32)],
                compiler_params=room(14),
            )(place, slot(b), *map(near, (everyone, *kept_solved, *kept_rows)), *x_all)
        if b < blocks - 1:
            kept_solved.append(solved)
            kept_rows.append(residual)

    got = near(lax.all_to_all(sends, ("feat", "core"), 0, 0, tiled=True))
    return pl.pallas_call(
        join_kernel,
        in_specs=[VMEM],
        out_specs=[VMEM, VMEM],
        out_shape=[
            jax.ShapeDtypeStruct((block_width // (chips * cores), C), F32),
            jax.ShapeDtypeStruct((1, rows_here, C), F32),
        ],
        compiler_params=room(12),
    )(got)


def solution(mesh):
    sizes = dict(mesh.shape)
    fine = Mesh(mesh.devices.reshape(sizes["feat"], 4, 8, 2), ("feat", "x", "z", "core"))
    rows = ("x", "z", "core")
    in_specs = (P(rows, "feat"), P(rows), P("feat", None, None))
    out_specs = (P(("feat",) + rows, None), P("feat", rows, None))

    return jax.shard_map(local, mesh=fine, in_specs=in_specs, out_specs=out_specs, check_vma=False)
```

time: 299 us -> 264 us (0.88)
  blocking collectives: 112 us -> 76.8 us
  starting transfers between devices: 69.5 us -> 61.4 us
  waiting for transfers between devices: 87.6 us -> 94.1 us
    all_to_all x4 -> x3, blocking collectives: 86.9 us -> 56.3 us  [exchange(): return lax.all_to_all(value, XZ, 0, 0, tiled=True)]
    all_to_all x4 -> x5, waiting for transfers between devices: 27.5 us -> 35.6 us  [exchange(): return lax.all_to_all(value, XZ, 0, 0, tiled=True)]
    ppermute x12 -> x8, starting transfers between devices: 17.4 us -> 10.5 us  [shifted(): lax.ppermute(value, 'feat', [(i, (i + by) % count) for i in range(count)])]
    all_to_all x1, blocking collectives: 24.8 us -> 20.5 us  [local(): got = near(lax.all_to_all(sends, ('feat', 'core'), 0, 0, tiled=True))]
    ppermute x17 -> x11, starting transfers between devices: 17.2 us -> 12.9 us  [swap_cores(): return lax.ppermute(value, 'core', [(0, 1), (1, 0)])]
    slice x0 -> x4, local copies, waits for them, and re-layouts: none -> 3.26 us  [halves(): return (value[:middle_row], value[middle_row:])]
    all_to_all x4 -> x5, starting transfers between devices: 35 us -> 38 us  [exchange(): return lax.all_to_all(value, XZ, 0, 0, tiled=True)]
    ppermute x12 -> x8, waiting for transfers between devices: 55.8 us -> 55.7 us  [shifted(): lax.ppermute(value, 'feat', [(i, (i + by) % count) for i in range(count)])]
  transfers between devices with their start and end apart: 33 -> 24, of which waited for: 13 -> 14; matrix products, arithmetic and copies ran while one was open for 0% -> 1% of each run, Pallas kernels for 0% -> 2%
where the time goes in v4:
time: 264 us; the launch traced here: 263 us
  waiting for transfers between devices  94.1 us (36%)
  blocking collectives  76.8 us (29%)
  starting transfers between devices  61.4 us (23%)
  Pallas kernels  22.2 us (8%)
  local copies, waits for them, and re-layouts  7.3 us (3%)
    all_to_all x3, blocking collectives, exchange(): return lax.all_to_all(value, XZ, 0, 0, tiled=True)  56.3 us
    ppermute x8, waiting for transfers between devices, shifted(): lax.ppermute(value, 'feat', [(i, (i + by) % count) for i in range(count)])  55.7 us
    all_to_all x5, starting transfers between devices, exchange(): return lax.all_to_all(value, XZ, 0, 0, tiled=True)  38 us
    all_to_all x5, waiting for transfers between devices, exchange(): return lax.all_to_all(value, XZ, 0, 0, tiled=True)  35.6 us
    all_to_all x1, blocking collectives, local(): got = near(lax.all_to_all(sends, ('feat', 'core'), 0, 0, tiled=True))  20.5 us
    ppermute x11, starting transfers between devices, swap_cores(): return lax.ppermute(value, 'core', [(0, 1), (1, 0)])  12.9 us
    ppermute x8, starting transfers between devices, shifted(): lax.ppermute(value, 'feat', [(i, (i + by) % count) for i in range(count)])  10.5 us
    pallas_call x2, Pallas kernels, local(): pl.pallas_call(functools.partial(step_kernel, groups), in_specs=[SMEM] *...  6.41 us
  transfers between devices with their start and end apart: 24, of which 14 were waited for; matrix products, arithmetic and copies ran while one was open for 1% of the time, Pallas kernels for 2%

profile of v4, /device:TPU:1, one launch (start us, length us, event | category | flops | bytes accessed | tf_op | source)
XLA Modules:
  0.0 262.8 jit_solution(12094700065669470888)
XLA Ops:
  0.6 2.2 copy-done.2
  2.8 1.0 copy-done.3
  3.9 2.6 shard_map.50
  6.5 3.6 %collective-permute-start.4 = (f32[1024,256]{1,0:T(8,128)S(1)}, f32[1024,256]{1,0:T(8,128)}, u32[]{:S(2)}, u32[]{:S(2)}) collective-permute-start(f32[1024,256]{1,0:T(8,128)S(1)} %get-tuple-element.30.refs_0_.refs_10_), channel_id=1, source_target_pairs={{0,192},{64,0},{128,64},{192,128},{1,193},{65,1},{129,65},{193,129... | collective-permute-start | bytes 3145736 | tf_op jit(solution)/shard_map/ppermute | solution.py:305
  10.1 0.0 collective-permute-start.2
  10.1 1.7 collective-permute-start.1
  11.8 20.2 %collective-permute-done.4.refs_4_.refs_14_ = f32[1024,256]{1,0:T(8,128)} collective-permute-done((f32[1024,256]{1,0:T(8,128)S(1)}, f32[1024,256]{1,0:T(8,128)}, u32[]{:S(2)}, u32[]{:S(2)}) %collective-permute-start.4) | collective-permute-done | bytes 1048608 | tf_op jit(solution)/shard_map/ppermute | solution.py:305
  31.9 1.1 slice.17
  33.0 3.6 %collective-permute-start.7 = (f32[512,256]{1,0:T(8,128)S(1)}, f32[512,256]{1,0:T(8,128)}, u32[]{:S(2)}, u32[]{:S(2)}) collective-permute-start(f32[512,256]{1,0:T(8,128)S(1)} %slice.17), channel_id=1, source_target_pairs={{0,192},{64,0},{128,64},{192,128},{1,193},{65,1},{129,65},{193,129... | collective-permute-start | bytes 1572872 | tf_op jit(solution)/shard_map/ppermute | solution.py:305
  36.6 1.8 collective-permute-start
  38.4 0.0 collective-permute-done.2.refs_2_.refs_12_
  38.4 1.1 slice.16
  39.5 0.1 collective-permute-start.6
  39.6 0.1 collective-permute-start.5
  39.7 0.5 collective-permute-start.3
  40.2 6.2 %collective-permute-done.7.refs_7_.refs_17_ = f32[512,256]{1,0:T(8,128)} collective-permute-done((f32[512,256]{1,0:T(8,128)S(1)}, f32[512,256]{1,0:T(8,128)}, u32[]{:S(2)}, u32[]{:S(2)}) %collective-permute-start.7) | collective-permute-done | bytes 524320 | tf_op jit(solution)/shard_map/ppermute | solution.py:305
  46.4 2.4 collective-permute-start.9
  48.7 5.6 %collective-permute-done.6.refs_6_.refs_16_ = f32[512,256]{1,0:T(8,128)} collective-permute-done((f32[512,256]{1,0:T(8,128)S(1)}, f32[512,256]{1,0:T(8,128)}, u32[]{:S(2)}, u32[]{:S(2)}) %collective-permute-start.6) | collective-permute-done | bytes 524320 | tf_op jit(solution)/shard_map/ppermute | solution.py:305
  54.4 0.9 collective-permute-start.8
  55.2 0.0 collective-permute-start.11
  55.2 0.0 collective-permute-done.9.refs_9_.refs_19_
  55.2 1.5 collective-permute-start.10
  56.7 0.4 collective-permute-done.8.refs_8_.refs_18_
  57.1 0.0 collective-permute-done.3.refs_3_.refs_13_
  57.1 3.1 %shard_map.51 = f32[32,32,128]{2,1,0:T(8,128)} custom-call(s32[1]{0:T(128)} %bitcast.4.slice_ref, s32[1]{0:T(128)} %bitcast.8.slot_ref.x_slot_ref, s32[1,512]{1,0:T(1,128)S(1)} %bitcast.10, f32[1024,256]{1,0:T(8,128)} %copy-done.1, f32[1024,256]{1,0:T(8,128)} %collective-permute-done.1.refs_1_.refs_11_, f32[1024,256]{1,0:T(8,128)} %collective-permute-done.2.refs_2_.refs_12_, ...), custom_call_target="tpu_custom_call" | custom-call | tf_op jit(solution)/shard_map/pallas_call | solution.py:356
  60.3 11.0 %all-to-all-start = ((f32[32,32,128]{2,1,0:T(8,128)}), f32[32,32,128]{2,1,0:T(8,128)S(1)}, u32[]{:S(2)}, u32[]{:S(2)}) async-start(f32[32,32,128]{2,1,0:T(8,128)} %shard_map.51), calls=%async_computation | async-start | bytes 1048576 | tf_op jit(solution)/shard_map/all_to_all | solution.py:309
  71.3 8.7 %collective-permute-done.11.refs_4_.refs_10_ = f32[256,1024]{1,0:T(8,128)S(1)} collective-permute-done((f32[256,1024]{1,0:T(8,128)S(1)}, f32[256,1024]{1,0:T(8,128)S(1)}, u32[]{:S(2)}, u32[]{:S(2)}) %collective-permute-start.11) | collective-permute-done | bytes 1048608 | tf_op jit(solution)/shard_map/ppermute | solution.py:305
  80.1 1.3 collective-permute-done.10.refs_2_.refs_8_
  81.3 4.2 %all-to-all-done.in_ref = f32[32,32,128]{2,1,0:T(8,128)S(1)} async-done(((f32[32,32,128]{2,1,0:T(8,128)}), f32[32,32,128]{2,1,0:T(8,128)S(1)}, u32[]{:S(2)}, u32[]{:S(2)}) %all-to-all-start) | async-done | bytes 524320 | tf_op jit(solution)/shard_map/all_to_all | solution.py:309
  85.5 3.5 %collective-permute-start.14 = (f32[256,1024]{1,0:T(8,128)S(1)}, f32[256,1024]{1,0:T(8,128)}, u32[]{:S(2)}, u32[]{:S(2)}) collective-permute-start(f32[256,1024]{1,0:T(8,128)S(1)} %get-tuple-element.40.refs_0_.refs_6_), channel_id=1, source_target_pairs={{0,1},{1,0},{2,3},{3,2},{4,5},{5,4},{6,7},{7,6},{8,9},{9,8},{10,11... | collective-permute-start | bytes 3145736 | tf_op jit(solution)/shard_map/ppermute | solution.py:31
  89.0 0.0 collective-permute-start.15
  89.0 0.5 collective-permute-start.16
  89.5 0.9 shard_map.52
  90.4 5.5 %all-to-all-start.1 = ((f32[32,24,128]{2,1,0:T(8,128)}), f32[32,24,128]{2,1,0:T(8,128)S(1)}, u32[]{:S(2)}, u32[]{:S(2)}) async-start(f32[32,24,128]{2,1,0:T(8,128)} %get-tuple-element.35), calls=%async_computation.1 | async-start | bytes 786432 | tf_op jit(solution)/shard_map/all_to_all | solution.py:309
  95.9 1.1 slice.14
  97.0 1.2 collective-permute-start.13
  98.2 0.5 collective-permute-start.12
  98.7 11.8 %collective-permute-done.13.refs_7_.refs_13_ = f32[128,1024]{1,0:T(8,128)S(1)} collective-permute-done((f32[128,1024]{1,0:T(8,128)S(1)}, f32[128,1024]{1,0:T(8,128)S(1)}, u32[]{:S(2)}, u32[]{:S(2)}) %collective-permute-start.13) | collective-permute-done | bytes 524320 | tf_op jit(solution)/shard_map/ppermute | solution.py:305
  110.6 1.9 collective-permute-done.12.refs_6_.refs_12_
  112.5 1.5 collective-permute-start.17
  114.0 0.1 collective-permute-start.18
  114.1 1.6 collective-permute-done.17.refs_8_.refs_14_
  115.7 0.7 collective-permute-done.18.refs_9_.refs_15_
  116.5 0.1 copy-done.6
  116.5 0.7 copy-done.7
  117.3 3.0 %shard_map.53 = (f32[96,1024]{1,0:T(8,128)S(1)}, f32[96,512]{1,0:T(8,128)S(1)}, f32[8,512]{1,0:T(8,128)S(1)}, f32[32,24,128]{2,1,0:T(8,128)S(1)}) custom-call(s32[1]{0:T(128)} %bitcast.4.slice_ref, s32[1]{0:T(128)} %bitcast.8.slot_ref.x_slot_ref, s32[1]{0:T(128)} %bitcast.7.z_slot_ref.x_slot_ref, s32[1,512]{1,0:T(1,128)S(1)} %bitcast.11, ...), custom_call_target="tpu_custom_call" | custom-call | tf_op jit(solution)/shard_map/pallas_call | solution.py:391
  120.3 20.9 %all_to_all.45.in_ref = f32[32,24,128]{2,1,0:T(8,128)S(1)} all-to-all(f32[32,24,128]{2,1,0:T(8,128)S(1)} %get-tuple-element.48), channel_id=1, replica_groups=mesh['feat'=4,'x'=4,'z'=8,'core'=2] {'x','z'}, dimensions={0} | all-to-all | bytes 786432 | tf_op jit(solution)/shard_map/all_to_all | solution.py:309
  141.2 0.8 shard_map.54
  142.0 7.5 %all-to-all-start.3 = ((f32[32,24,128]{2,1,0:T(8,128)}), f32[32,24,128]{2,1,0:T(8,128)S(1)}, u32[]{:S(2)}, u32[]{:S(2)}) async-start(f32[32,24,128]{2,1,0:T(8,128)} %shard_map.54), calls=%async_computation.3 | async-start | bytes 786432 | tf_op jit(solution)/shard_map/all_to_all | solution.py:309
  149.5 10.9 %all-to-all-done.3.everyone_ref = f32[32,24,128]{2,1,0:T(8,128)S(1)} async-done(((f32[32,24,128]{2,1,0:T(8,128)}), f32[32,24,128]{2,1,0:T(8,128)S(1)}, u32[]{:S(2)}, u32[]{:S(2)}) %all-to-all-start.3) | async-done | bytes 393248 | tf_op jit(solution)/shard_map/all_to_all | solution.py:309
  160.5 3.0 %shard_map.55 = (f32[96,1024]{1,0:T(8,128)S(1)}, f32[96,512]{1,0:T(8,128)S(1)}, f32[32,24,128]{2,1,0:T(8,128)S(1)}) custom-call(s32[1]{0:T(128)} %bitcast.7.z_slot_ref.x_slot_ref, s32[1]{0:T(128)} %bitcast.6.z_slot_ref.x_slot_ref, f32[32,24,128]{2,1,0:T(8,128)S(1)} %all-to-all-done.3.everyone_ref, f32[96,512]{1,0:T(8,128)S(1)} %get-tuple-element.49.old_ref.refs_3_, ...), custom_call_target="tpu_custom_call" | custom-call | tf_op jit(solution)/shard_map/pallas_call | solution.py:401
  163.4 18.1 %all_to_all.46.in_ref = f32[32,24,128]{2,1,0:T(8,128)S(1)} all-to-all(f32[32,24,128]{2,1,0:T(8,128)S(1)} %get-tuple-element.51), channel_id=1, replica_groups=mesh['feat'=4,'x'=4,'z'=8,'core'=2] {'x','z'}, dimensions={0} | all-to-all | bytes 786432 | tf_op jit(solution)/shard_map/all_to_all | solution.py:309
  181.6 0.8 shard_map.56
  182.4 7.4 %all-to-all-start.5 = ((f32[32,24,128]{2,1,0:T(8,128)}), f32[32,24,128]{2,1,0:T(8,128)S(1)}, u32[]{:S(2)}, u32[]{:S(2)}) async-start(f32[32,24,128]{2,1,0:T(8,128)} %shard_map.56), calls=%async_computation.5 | async-start | bytes 786432 | tf_op jit(solution)/shard_map/all_to_all | solution.py:309
  189.8 10.2 %all-to-all-done.5.everyone_ref = f32[32,24,128]{2,1,0:T(8,128)S(1)} async-done(((f32[32,24,128]{2,1,0:T(8,128)}), f32[32,24,128]{2,1,0:T(8,128)S(1)}, u32[]{:S(2)}, u32[]{:S(2)}) %all-to-all-start.5) | async-done | bytes 393248 | tf_op jit(solution)/shard_map/all_to_all | solution.py:309
  200.0 3.4 %shard_map.57 = (f32[96,1024]{1,0:T(8,128)S(1)}, f32[96,512]{1,0:T(8,128)S(1)}, f32[32,24,128]{2,1,0:T(8,128)S(1)}) custom-call(s32[1]{0:T(128)} %bitcast.6.z_slot_ref.x_slot_ref, s32[1]{0:T(128)} %bitcast.3.z_slot_ref.x_slot_ref, f32[32,24,128]{2,1,0:T(8,128)S(1)} %all-to-all-done.5.everyone_ref, f32[96,512]{1,0:T(8,128)S(1)} %get-tuple-element.52.old_ref.refs_4_, ...), custom_call_target="tpu_custom_call" | custom-call | tf_op jit(solution)/shard_map/pallas_call | solution.py:401
  203.5 17.3 %all_to_all.47.in_ref = f32[32,24,128]{2,1,0:T(8,128)S(1)} all-to-all(f32[32,24,128]{2,1,0:T(8,128)S(1)} %get-tuple-element.53), channel_id=1, replica_groups=mesh['feat'=4,'x'=4,'z'=8,'core'=2] {'x','z'}, dimensions={0} | all-to-all | bytes 786432 | tf_op jit(solution)/shard_map/all_to_all | solution.py:309
  220.8 0.8 shard_map.58
  221.6 6.5 %all-to-all-start.7 = ((f32[32,24,128]{2,1,0:T(8,128)}), f32[32,24,128]{2,1,0:T(8,128)S(1)}, u32[]{:S(2)}, u32[]{:S(2)}) async-start(f32[32,24,128]{2,1,0:T(8,128)} %shard_map.58), calls=%async_computation.7 | async-start | bytes 786432 | tf_op jit(solution)/shard_map/all_to_all | solution.py:309
  228.2 0.1 pad_add_fusion.1.place_ref
  228.3 10.3 %all-to-all-done.7.everyone_ref = f32[32,24,128]{2,1,0:T(8,128)S(1)} async-done(((f32[32,24,128]{2,1,0:T(8,128)}), f32[32,24,128]{2,1,0:T(8,128)S(1)}, u32[]{:S(2)}, u32[]{:S(2)}) %all-to-all-start.7) | async-done | bytes 393248 | tf_op jit(solution)/shard_map/all_to_all | solution.py:309
  238.5 2.7 %shard_map.59 = f32[8,88,256]{2,1,0:T(8,128)S(1)} custom-call(s32[3]{0:T(128)S(1)} %pad_add_fusion.1.place_ref, s32[1]{0:T(128)} %bitcast.3.z_slot_ref.x_slot_ref, f32[32,24,128]{2,1,0:T(8,128)S(1)} %all-to-all-done.7.everyone_ref, f32[96,1024]{1,0:T(8,128)S(1)} %get-tuple-element.54.refs_0_, f32[96,1024]{1,0:T(8,128)S(1)} %get-tuple-element.55.refs_1_, ...), custom_call_target="tpu_custom_call" | custom-call | tf_op jit(solution)/shard_map/pallas_call | solution.py:412
  241.2 20.5 %all_to_all.48.in_ref = f32[8,88,256]{2,1,0:T(8,128)S(1)} all-to-all(f32[8,88,256]{2,1,0:T(8,128)S(1)} %shard_map.59), channel_id=1, replica_groups=mesh['feat'=4,'x'=4,'z'=8,'core'=2] {'feat','core'}, dimensions={0} | all-to-all | bytes 1441792 | tf_op jit(solution)/shard_map/all_to_all | solution.py:424
  261.7 1.1 shard_map.60
  (23 shorter events, 0.1 us)
Async XLA Ops:
  0.6 2.2 copy-start.2
  2.8 1.0 copy-start.3
  3.9 32.7 %copy-start.8 = (s32[256]{0:T(256)S(1)}, s32[256]{0:T(256)}, u32[]{:S(2)}) copy-start(s32[256]{0:T(256)} %param.4) | copy-start | bytes 3076
  6.4 50.7 %copy-start.1 = (f32[1024,256]{1,0:T(8,128)}, f32[1024,256]{1,0:T(8,128)S(1)}, u32[]{:S(2)}) copy-start(f32[1024,256]{1,0:T(8,128)S(1)} %get-tuple-element.30.refs_0_.refs_10_) | copy-start | bytes 3145732
  6.4 79.1 %copy-start = (f32[256,1024]{1,0:T(8,128)}, f32[256,1024]{1,0:T(8,128)S(1)}, u32[]{:S(2)}) copy-start(f32[256,1024]{1,0:T(8,128)S(1)} %get-tuple-element.40.refs_0_.refs_6_) | copy-start | bytes 3145732
  6.5 25.5 %collective-permute-start.4 = (f32[1024,256]{1,0:T(8,128)S(1)}, f32[1024,256]{1,0:T(8,128)}, u32[]{:S(2)}, u32[]{:S(2)}) collective-permute-start(f32[1024,256]{1,0:T(8,128)S(1)} %get-tuple-element.30.refs_0_.refs_10_), channel_id=1, source_target_pairs={{0,192},{64,0},{128,64},{192,128},{1,193},{65,1},{129,65},{193,129... | collective-permute-start | bytes 3145736 | tf_op jit(solution)/shard_map/ppermute | solution.py:305
  10.1 28.3 %collective-permute-start.2 = (f32[1024,256]{1,0:T(8,128)S(1)}, f32[1024,256]{1,0:T(8,128)}, u32[]{:S(2)}, u32[]{:S(2)}) collective-permute-start(f32[1024,256]{1,0:T(8,128)S(1)} %get-tuple-element.30.refs_0_.refs_10_), channel_id=1, source_target_pairs={{0,64},{64,128},{128,192},{192,0},{1,65},{65,129},{129,193},{193,1... | collective-permute-start | bytes 3145736 | tf_op jit(solution)/shard_map/ppermute | solution.py:305
  10.1 45.1 %collective-permute-start.1 = (f32[1024,256]{1,0:T(8,128)S(1)}, f32[1024,256]{1,0:T(8,128)}, u32[]{:S(2)}, u32[]{:S(2)}) collective-permute-start(f32[1024,256]{1,0:T(8,128)S(1)} %get-tuple-element.30.refs_0_.refs_10_), channel_id=1, source_target_pairs={{0,1},{1,0},{2,3},{3,2},{4,5},{5,4},{6,7},{7,6},{8,9},{9,8},{10,11... | collective-permute-start | bytes 3145736 | tf_op jit(solution)/shard_map/ppermute | solution.py:31
  33.0 13.4 %collective-permute-start.7 = (f32[512,256]{1,0:T(8,128)S(1)}, f32[512,256]{1,0:T(8,128)}, u32[]{:S(2)}, u32[]{:S(2)}) collective-permute-start(f32[512,256]{1,0:T(8,128)S(1)} %slice.17), channel_id=1, source_target_pairs={{0,192},{64,0},{128,64},{192,128},{1,193},{65,1},{129,65},{193,129... | collective-permute-start | bytes 1572872 | tf_op jit(solution)/shard_map/ppermute | solution.py:305
  36.6 3.1 %collective-permute-start = (s32[256]{0:T(256)S(1)}, s32[256]{0:T(256)S(1)}, u32[]{:S(2)}, u32[]{:S(2)}) collective-permute-start(s32[256]{0:T(256)S(1)} %copy-done.8), channel_id=1, source_target_pairs={{0,1},{1,0},{2,3},{3,2},{4,5},{5,4},{6,7},{7,6},{8,9},{9,8},{10,11... | collective-permute-start | bytes 3080 | tf_op jit(solution)/shard_map/ppermute | solution.py:31
  39.5 14.9 %collective-permute-start.6 = (f32[512,256]{1,0:T(8,128)S(1)}, f32[512,256]{1,0:T(8,128)}, u32[]{:S(2)}, u32[]{:S(2)}) collective-permute-start(f32[512,256]{1,0:T(8,128)S(1)} %slice.16), channel_id=1, source_target_pairs={{0,64},{64,128},{128,192},{192,0},{1,65},{65,129},{129,193},{193,1... | collective-permute-start | bytes 1572872 | tf_op jit(solution)/shard_map/ppermute | solution.py:305
  39.6 17.1 %collective-permute-start.5 = (f32[1024,256]{1,0:T(8,128)}, f32[1024,256]{1,0:T(8,128)}, u32[]{:S(2)}, u32[]{:S(2)}) collective-permute-start(f32[1024,256]{1,0:T(8,128)} %collective-permute-done.4.refs_4_.refs_14_), channel_id=1, source_target_pairs={{0,1},{1,0},{2,3},{3,2},{4,5},{5,4},{6,7},{7,6},{8,9},{9,8},{10,11... | collective-permute-start | bytes 3145736 | tf_op jit(solution)/shard_map/ppermute | solution.py:31
  39.7 17.4 %collective-permute-start.3 = (f32[1024,256]{1,0:T(8,128)}, f32[1024,256]{1,0:T(8,128)}, u32[]{:S(2)}, u32[]{:S(2)}) collective-permute-start(f32[1024,256]{1,0:T(8,128)} %collective-permute-done.2.refs_2_.refs_12_), channel_id=1, source_target_pairs={{0,1},{1,0},{2,3},{3,2},{4,5},{5,4},{6,7},{7,6},{8,9},{9,8},{10,11... | collective-permute-start | bytes 3145736 | tf_op jit(solution)/shard_map/ppermute | solution.py:31
  46.4 8.9 %collective-permute-start.9 = (f32[512,256]{1,0:T(8,128)}, f32[512,256]{1,0:T(8,128)}, u32[]{:S(2)}, u32[]{:S(2)}) collective-permute-start(f32[512,256]{1,0:T(8,128)} %collective-permute-done.7.refs_7_.refs_17_), channel_id=1, source_target_pairs={{0,1},{1,0},{2,3},{3,2},{4,5},{5,4},{6,7},{7,6},{8,9},{9,8},{10,11... | collective-permute-start | bytes 1572872 | tf_op jit(solution)/shard_map/ppermute | solution.py:31
  54.4 2.7 %collective-permute-start.8 = (f32[512,256]{1,0:T(8,128)}, f32[512,256]{1,0:T(8,128)}, u32[]{:S(2)}, u32[]{:S(2)}) collective-permute-start(f32[512,256]{1,0:T(8,128)} %collective-permute-done.6.refs_6_.refs_16_), channel_id=1, source_target_pairs={{0,1},{1,0},{2,3},{3,2},{4,5},{5,4},{6,7},{7,6},{8,9},{9,8},{10,11... | collective-permute-start | bytes 1572872 | tf_op jit(solution)/shard_map/ppermute | solution.py:31
  55.2 24.8 %collective-permute-start.11 = (f32[256,1024]{1,0:T(8,128)S(1)}, f32[256,1024]{1,0:T(8,128)S(1)}, u32[]{:S(2)}, u32[]{:S(2)}) collective-permute-start(f32[256,1024]{1,0:T(8,128)S(1)} %get-tuple-element.40.refs_0_.refs_6_), channel_id=1, source_target_pairs={{0,192},{64,0},{128,64},{192,128},{1,193},{65,1},{129,65},{193,129... | collective-permute-start | bytes 3145736 | tf_op jit(solution)/shard_map/ppermute | solution.py:305
  55.2 26.1 %collective-permute-start.10 = (f32[256,1024]{1,0:T(8,128)S(1)}, f32[256,1024]{1,0:T(8,128)}, u32[]{:S(2)}, u32[]{:S(2)}) collective-permute-start(f32[256,1024]{1,0:T(8,128)S(1)} %get-tuple-element.40.refs_0_.refs_6_), channel_id=1, source_target_pairs={{0,64},{64,128},{128,192},{192,0},{1,65},{65,129},{129,193},{193,1... | collective-permute-start | bytes 3145736 | tf_op jit(solution)/shard_map/ppermute | solution.py:305
  60.3 25.2 %all-to-all-start = ((f32[32,32,128]{2,1,0:T(8,128)}), f32[32,32,128]{2,1,0:T(8,128)S(1)}, u32[]{:S(2)}, u32[]{:S(2)}) async-start(f32[32,32,128]{2,1,0:T(8,128)} %shard_map.51), calls=%async_computation | async-start | bytes 1048576 | tf_op jit(solution)/shard_map/all_to_all | solution.py:309
  80.1 37.2 %copy-start.4 = (f32[256,1024]{1,0:T(8,128)}, f32[256,1024]{1,0:T(8,128)S(1)}, u32[]{:S(2)}) copy-start(f32[256,1024]{1,0:T(8,128)S(1)} %collective-permute-done.11.refs_4_.refs_10_) | copy-start | bytes 3145732
  85.5 26.9 %collective-permute-start.14 = (f32[256,1024]{1,0:T(8,128)S(1)}, f32[256,1024]{1,0:T(8,128)}, u32[]{:S(2)}, u32[]{:S(2)}) collective-permute-start(f32[256,1024]{1,0:T(8,128)S(1)} %get-tuple-element.40.refs_0_.refs_6_), channel_id=1, source_target_pairs={{0,1},{1,0},{2,3},{3,2},{4,5},{5,4},{6,7},{7,6},{8,9},{9,8},{10,11... | collective-permute-start | bytes 3145736 | tf_op jit(solution)/shard_map/ppermute | solution.py:31
  89.0 23.4 %collective-permute-start.15 = (f32[256,1024]{1,0:T(8,128)}, f32[256,1024]{1,0:T(8,128)}, u32[]{:S(2)}, u32[]{:S(2)}) collective-permute-start(f32[256,1024]{1,0:T(8,128)} %collective-permute-done.10.refs_2_.refs_8_), channel_id=1, source_target_pairs={{0,1},{1,0},{2,3},{3,2},{4,5},{5,4},{6,7},{7,6},{8,9},{9,8},{10,11... | collective-permute-start | bytes 3145736 | tf_op jit(solution)/shard_map/ppermute | solution.py:31
  89.0 23.4 %collective-permute-start.16 = (f32[256,1024]{1,0:T(8,128)S(1)}, f32[256,1024]{1,0:T(8,128)}, u32[]{:S(2)}, u32[]{:S(2)}) collective-permute-start(f32[256,1024]{1,0:T(8,128)S(1)} %collective-permute-done.11.refs_4_.refs_10_), channel_id=1, source_target_pairs={{0,1},{1,0},{2,3},{3,2},{4,5},{5,4},{6,7},{7,6},{8,9},{9,8},{10,11... | collective-permute-start | bytes 3145736 | tf_op jit(solution)/shard_map/ppermute | solution.py:31
  90.4 22.0 %all-to-all-start.1 = ((f32[32,24,128]{2,1,0:T(8,128)}), f32[32,24,128]{2,1,0:T(8,128)S(1)}, u32[]{:S(2)}, u32[]{:S(2)}) async-start(f32[32,24,128]{2,1,0:T(8,128)} %get-tuple-element.35), calls=%async_computation.1 | async-start | bytes 786432 | tf_op jit(solution)/shard_map/all_to_all | solution.py:309
  97.0 13.6 %collective-permute-start.13 = (f32[128,1024]{1,0:T(8,128)S(1)}, f32[128,1024]{1,0:T(8,128)S(1)}, u32[]{:S(2)}, u32[]{:S(2)}) collective-permute-start(f32[128,1024]{1,0:T(8,128)S(1)} %slice.15), channel_id=1, source_target_pairs={{0,192},{64,0},{128,64},{192,128},{1,193},{65,1},{129,65},{193,129... | collective-permute-start | bytes 1572872 | tf_op jit(solution)/shard_map/ppermute | solution.py:305
  98.2 14.2 %collective-permute-start.12 = (f32[128,1024]{1,0:T(8,128)S(1)}, f32[128,1024]{1,0:T(8,128)}, u32[]{:S(2)}, u32[]{:S(2)}) collective-permute-start(f32[128,1024]{1,0:T(8,128)S(1)} %slice.14), channel_id=1, source_target_pairs={{0,64},{64,128},{128,192},{192,0},{1,65},{65,129},{129,193},{193,1... | collective-permute-start | bytes 1572872 | tf_op jit(solution)/shard_map/ppermute | solution.py:305
  110.6 5.9 %copy-start.5 = (f32[128,1024]{1,0:T(8,128)}, f32[128,1024]{1,0:T(8,128)S(1)}, u32[]{:S(2)}) copy-start(f32[128,1024]{1,0:T(8,128)S(1)} %collective-permute-done.13.refs_7_.refs_13_) | copy-start | bytes 1572868
  112.5 3.3 %collective-permute-start.17 = (f32[128,1024]{1,0:T(8,128)}, f32[128,1024]{1,0:T(8,128)S(1)}, u32[]{:S(2)}, u32[]{:S(2)}) collective-permute-start(f32[128,1024]{1,0:T(8,128)} %collective-permute-done.12.refs_6_.refs_12_), channel_id=1, source_target_pairs={{0,1},{1,0},{2,3},{3,2},{4,5},{5,4},{6,7},{7,6},{8,9},{9,8},{10,11... | collective-permute-start | bytes 1572872 | tf_op jit(solution)/shard_map/ppermute | solution.py:31
  114.0 2.5 collective-permute-start.18
  115.7 0.8 copy-start.6
  116.5 0.8 copy-start.7
  142.0 18.5 %all-to-all-start.3 = ((f32[32,24,128]{2,1,0:T(8,128)}), f32[32,24,128]{2,1,0:T(8,128)S(1)}, u32[]{:S(2)}, u32[]{:S(2)}) async-start(f32[32,24,128]{2,1,0:T(8,128)} %shard_map.54), calls=%async_computation.3 | async-start | bytes 786432 | tf_op jit(solution)/shard_map/all_to_all | solution.py:309
  182.4 17.7 %all-to-all-start.5 = ((f32[32,24,128]{2,1,0:T(8,128)}), f32[32,24,128]{2,1,0:T(8,128)S(1)}, u32[]{:S(2)}, u32[]{:S(2)}) async-start(f32[32,24,128]{2,1,0:T(8,128)} %shard_map.56), calls=%async_computation.5 | async-start | bytes 786432 | tf_op jit(solution)/shard_map/all_to_all | solution.py:309
  221.6 16.9 %all-to-all-start.7 = ((f32[32,24,128]{2,1,0:T(8,128)}), f32[32,24,128]{2,1,0:T(8,128)S(1)}, u32[]{:S(2)}, u32[]{:S(2)}) async-start(f32[32,24,128]{2,1,0:T(8,128)} %shard_map.58), calls=%async_computation.7 | async-start | bytes 786432 | tf_op jit(solution)/shard_map/all_to_all | solution.py:309

commit v5 on v4

--- a/solution.py
+++ b/solution.py
@@ -31,39 +31,45 @@
     return lax.ppermute(value, "core", [(0, 1), (1, 0)])
 
 
-def prepare_kernel(gram_ref, x_ref, z_ref, xf_ref):
-    gram = gram_ref[0]
-    high = gram.astype(BF16)
-    rest = gram - high.astype(F32)
-    mid = rest.astype(BF16)
-    low = (rest - mid.astype(F32)).astype(BF16)
-    x = x_ref[...]
-    z_ref[...] = (dot_t(low, x) + dot_t(mid, x)) + dot_t(high, x)
-
-    @pl.when(pl.program_id(0) == 0)
-    def _():
-        xf_ref[...] = x.astype(F32)
-
-
-def prepare(features, inv_gram, tile=256):
+def prepare_kernel(gram_ref, x_ref, z0_ref, z1_ref, xf_ref, gram_land, x_land, sems):
+    tiles, tile, _ = gram_land.shape
+    x_copy = pltpu.make_async_copy(x_ref, x_land, sems.at[tiles])
+    x_copy.start()
+    copies = []
+    for t in range(tiles):
+        source = gram_ref.at[0, pl.ds(t * tile, tile)]
+        copies.append(pltpu.make_async_copy(source, gram_land.at[t], sems.at[t]))
+        copies[t].start()
+    x_copy.wait()
+    x = x_land[...]
+    per_half = tiles // 2
+    for t in range(tiles):
+        copies[t].wait()
+        gram = gram_land[t]
+        high = gram.astype(BF16)
+        rest = gram - high.astype(F32)
+        mid = rest.astype(BF16)
+        low = (rest - mid.astype(F32)).astype(BF16)
+        z_ref = z0_ref if t < per_half else z1_ref
+        at = pl.ds((t % per_half) * tile, tile)
+        z_ref[at, :] = (dot_t(low, x) + dot_t(mid, x)) + dot_t(high, x)
+    xf_ref[...] = x.astype(F32)
+
+
+def prepare(features, inv_gram, tiles=4):
     rows, width = features.shape
     return pl.pallas_call(
         prepare_kernel,
-        grid=(width // tile,),
-        in_specs=[
-            pl.BlockSpec((1, tile, width), lambda i: (0, i, 0)),
-            pl.BlockSpec((rows, width), lambda i: (0, 0)),
+        in_specs=[ANY, ANY],
+        out_specs=[VMEM] * 3,
+        out_shape=[held((width // 2, rows))] * 2 + [held((rows, width))],
+        scratch_shapes=[
+            pltpu.VMEM((tiles, width // tiles, width), F32),
+            pltpu.VMEM((rows, width), BF16),
+            pltpu.SemaphoreType.DMA((tiles + 1,)),
         ],
-        out_specs=[
-            pl.BlockSpec((tile, rows), lambda i: (i, 0)),
-            pl.BlockSpec((rows, width), lambda i: (0, 0)),
-        ],
-        out_shape=[
-            jax.ShapeDtypeStruct((width, rows), F32),
-            jax.ShapeDtypeStruct((rows, width), F32),
-        ],
-        compiler_params=room(24),
-    )(inv_gram, features)
+        compiler_params=room(20),
+    )(far(inv_gram), far(features))
 
 
 def held(shape, dtype=F32):
@@ -78,33 +84,36 @@
     return pltpu.with_memory_space_constraint(value, pltpu.HBM)
 
 
-HELD_BLOCKS = 10
-
-
-def fetch(slot_ref, refs, landing, sems):
-    half = landing.shape[1] // 2
-    for slot, first in ((0, 0), (1, 2), (3, 4)):
+Z_PLACES = tuple(
+    tuple((4 * slot + 2 * k + h, k, h, 2) for k in range(2) for h in range(2)) for slot in range(4)
+)
+X_PLACES = (
+    ((0, 0, 0, 1), (1, 1, 0, 1)),
+    ((2, 0, 0, 1), (3, 1, 0, 1)),
+    tuple((4 + 2 * k + h, k, h, 2) for k in range(2) for h in range(2)),
+    ((8, 0, 0, 1), (9, 1, 0, 1)),
+)
+Z_COUNT, X_COUNT = 16, 10
+
+
+def fetch(slot_ref, places, refs, landing, sems):
+    for slot, parts in enumerate(places):
 
         @pl.when(slot_ref[0] == slot)
         def _():
-            for k in range(2):
-                pltpu.make_async_copy(refs[first + k], landing.at[k], sems.at[k]).start()
-
-    @pl.when(slot_ref[0] == 2)
-    def _():
-        for k in range(2):
-            for h in range(2):
-                target = landing.at[k, pl.ds(h * half, half)]
-                pltpu.make_async_copy(refs[6 + 2 * k + h], target, sems.at[k]).start()
-
-
-def wait_fetch(refs, landing, sems):
+            for index, k, part, count in parts:
+                size = landing.shape[1] // count
+                target = landing.at[k, pl.ds(part * size, size)]
+                pltpu.make_async_copy(refs[index], target, sems.at[k]).start()
+
+
+def wait_fetch(landing, sems):
     for k in range(2):
-        pltpu.make_async_copy(refs[k], landing.at[k], sems.at[k]).wait()
-
-
-def landing_of(blocks):
-    return [pltpu.VMEM((2,) + blocks[0].shape, F32), pltpu.SemaphoreType.DMA((2,))]
+        pltpu.make_async_copy(landing.at[k], landing.at[k], sems.at[k]).wait()
+
+
+def landing_of(shape):
+    return [pltpu.VMEM((2,) + shape, F32), pltpu.SemaphoreType.DMA((2,))]
 
 
 def partial_sum(landing, scaled):
@@ -148,7 +157,7 @@
 
 def first_kernel(slices, padded, slice_ref, slot_ref, lab_ref, *refs):
     z_refs, (out_ref, landing, sems) = refs[:-3], refs[-3:]
-    fetch(slot_ref, z_refs, landing, sems)
+    fetch(slot_ref, Z_PLACES, z_refs, landing, sems)
     lab = lab_ref[...]
     group, low_label = label_parts(lab, slices, C // slices)
     row = lax.broadcasted_iota(jnp.int32, (LANES, lab.shape[1]), 0)
@@ -160,7 +169,7 @@
     chips, deep, _ = out_ref.shape
     chunk = deep - slices
     out_ref[:, chunk:, :] = jnp.broadcast_to(counts[None], (chips, slices, LANES))
-    wait_fetch(z_refs, landing, sems)
+    wait_fetch(landing, sems)
     put_pieces(out_ref, partial_sum(landing, onehot), chunk)
 
 
@@ -210,11 +219,10 @@
     slices, total_rows, groups, slice_ref, x_slot_ref, z_slot_ref, lab_ref, totals_ref,
     everyone_ref, *refs,
 ):
-    x_refs, z_refs = refs[:HELD_BLOCKS], refs[HELD_BLOCKS : 2 * HELD_BLOCKS]
-    solved_ref, residual_ref, weight_ref, out_ref = refs[2 * HELD_BLOCKS : 2 * HELD_BLOCKS + 4]
-    x_land, x_sems, z_land, z_sems = refs[2 * HELD_BLOCKS + 4 :]
-    fetch(x_slot_ref, x_refs, x_land, x_sems)
-    fetch(z_slot_ref, z_refs, z_land, z_sems)
+    x_refs, z_refs, refs = refs[:X_COUNT], refs[X_COUNT:][:Z_COUNT], refs[X_COUNT + Z_COUNT :]
+    solved_ref, residual_ref, weight_ref, out_ref, x_land, x_sems, z_land, z_sems = refs
+    fetch(x_slot_ref, X_PLACES, x_refs, x_land, x_sems)
+    fetch(z_slot_ref, Z_PLACES, z_refs, z_land, z_sems)
     lab = lab_ref[...]
     group, low_label = label_parts(lab, slices, C // slices)
     solved = take_copies(everyone_ref, groups)
@@ -230,26 +238,25 @@
     weight = total_rows / (C * row_count)
     weight_ref[...] = jnp.broadcast_to(weight, weight_ref.shape)
     onehot = jnp.where(hit & (group == slice_ref[0]), 1.0, 0.0)
-    wait_fetch(x_refs, x_land, x_sems)
+    wait_fetch(x_land, x_sems)
     residual = update(solved, x_land, onehot)
     residual_ref[...] = residual
-    wait_fetch(z_refs, z_land, z_sems)
+    wait_fetch(z_land, z_sems)
     put_pieces(out_ref, partial_sum(z_land, (weight * residual).astype(BF16)), out_ref.shape[1])
 
 
 def step_kernel(groups, x_slot_ref, z_slot_ref, everyone_ref, old_ref, weight_ref, *refs):
-    x_refs, z_refs = refs[:HELD_BLOCKS], refs[HELD_BLOCKS : 2 * HELD_BLOCKS]
-    solved_ref, residual_ref, out_ref = refs[2 * HELD_BLOCKS : 2 * HELD_BLOCKS + 3]
-    x_land, x_sems, z_land, z_sems = refs[2 * HELD_BLOCKS + 3 :]
-    fetch(x_slot_ref, x_refs, x_land, x_sems)
-    fetch(z_slot_ref, z_refs, z_land, z_sems)
+    x_refs, z_refs, refs = refs[:X_COUNT], refs[X_COUNT:][:Z_COUNT], refs[X_COUNT + Z_COUNT :]
+    solved_ref, residual_ref, out_ref, x_land, x_sems, z_land, z_sems = refs
+    fetch(x_slot_ref, X_PLACES, x_refs, x_land, x_sems)
+    fetch(z_slot_ref, Z_PLACES, z_refs, z_land, z_sems)
     solved = take_copies(everyone_ref, groups)
     solved_ref[...] = solved
-    wait_fetch(x_refs, x_land, x_sems)
+    wait_fetch(x_land, x_sems)
     residual = update(solved, x_land, old_ref[...])
     residual_ref[...] = residual
     scaled = (weight_ref[0:1, :] * residual).astype(BF16)
-    wait_fetch(z_refs, z_land, z_sems)
+    wait_fetch(z_land, z_sems)
     put_pieces(out_ref, partial_sum(z_land, scaled), out_ref.shape[1])
 
 
@@ -258,8 +265,8 @@
 ):
     solved_refs, refs = refs[: blocks - 1], refs[blocks - 1 :]
     rows_refs, refs = refs[: blocks - 1], refs[blocks - 1 :]
-    x_refs, (out_ref, x_land, x_sems, turned) = refs[:HELD_BLOCKS], refs[HELD_BLOCKS:]
-    fetch(x_slot_ref, x_refs, x_land, x_sems)
+    x_refs, (out_ref, x_land, x_sems, turned) = refs[:X_COUNT], refs[X_COUNT:]
+    fetch(x_slot_ref, X_PLACES, x_refs, x_land, x_sems)
     last_solved = take_copies(everyone_ref, groups)
     rows = x_land.shape[1]
     head = out_ref.shape[1] - width
@@ -278,7 +285,7 @@
                 out_ref[2 * b + k, :head, h * LANES : (h + 1) * LANES] = turned[
                     pl.ds(pl.multiple_of(begin + h * head, ROW_TILE), head), :
                 ]
-    wait_fetch(x_refs, x_land, x_sems)
+    wait_fetch(x_land, x_sems)
     last = update(last_solved, x_land, rows_refs[-1][...])
     for b in range(blocks):
         value = last if b == blocks - 1 else rows_refs[b][...]
@@ -340,25 +347,38 @@
     def slot(b):
         return lax.rem(feat + (blocks - b), blocks)[None]
 
-    z_own, x_own = prepare(features, inv_gram)
+    z0, z1, x_own = prepare(features, inv_gram)
+    z_shape = (block_width, rows_here)
     lab = jnp.concatenate([labels, swap_cores(labels)])[None, :]
 
-    z_up, z_down = shifted(z_own, 1), shifted(z_own, -1)
-    z_pair = [z_own, swap_cores(z_own)]
-    z_far0 = shifted(halves(z_up)[0], 1)
-    z_far1 = shifted(halves(z_down)[1], -1)
-    x_own, _, _ = lax.optimization_barrier((x_own, z_up, z_down))
-    z_all = z_pair + [z_up, swap_cores(z_up), z_down, swap_cores(z_down)]
-    z_all += [z_far0, z_far1, swap_cores(z_far0), swap_cores(z_far1)]
+    def move(value, by):
+        return shifted(value, by)
+
+    def swap(value):
+        return swap_cores(value)
+
+    z_up0, z_down1 = move(z0, 1), move(z1, -1)
+    z_up1, z_down0 = move(z1, 1), move(z0, -1)
+    z_far0, z_far1 = move(z_up0, 1), move(z_down1, -1)
+    x_up, x_down = move(x_own, 1), move(x_own, -1)
+    z_all = [z0, z1, swap(z0), swap(z1)]
+    z_all += [z_up0, z_up1, swap(z_up0), swap(z_up1)]
+    z_all += [z_far0, z_far1, swap(z_far0), swap(z_far1)]
+    z_all += [z_down0, z_down1, swap(z_down0), swap(z_down1)]
     z_all = [far(z) for z in z_all]
-    x_up, x_down = shifted(x_own, 1), shifted(x_own, -1)
+    x_far0 = move(halves(x_up)[0], 1)
+    x_far1 = move(halves(x_down)[1], -1)
+    x_all = [x_own, swap(x_own), x_up, swap(x_up)]
+    x_all += [x_far0, x_far1, swap(x_far0), swap(x_far1)]
+    x_all += [x_down, swap(x_down)]
+    x_all = [far(x) for x in x_all]
 
     pieces = pl.pallas_call(
         functools.partial(first_kernel, slices, padded),
-        in_specs=[SMEM, SMEM, VMEM] + [ANY] * HELD_BLOCKS,
+        in_specs=[SMEM, SMEM, VMEM] + [ANY] * Z_COUNT,
         out_specs=VMEM,
         out_shape=held((chips, chunk + slices, LANES)),
-        scratch_shapes=landing_of(z_all),
+        scratch_shapes=landing_of(z_shape),
         compiler_params=room(12),
     )(slice_index, slot(0), lab, *z_all)
 
@@ -367,43 +387,30 @@
     pieces_shape = held((chips, chunk, LANES))
     kept_rows = []
     kept_solved = []
-    totals = weight = x_all = x_near = None
+    totals = weight = None
     for b in range(blocks):
         arrived = exchange(pieces)
-        if b == 0:
-            arrived, x_up, x_down, x_own = lax.optimization_barrier(
-                (arrived, x_up, x_down, x_own)
-            )
-            x_far0 = shifted(halves(x_up)[0], 1)
-            x_far1 = shifted(halves(x_down)[1], -1)
-            x_near = [x_own, swap_cores(x_own), x_up, swap_cores(x_up)]
-            x_near += [x_down, swap_cores(x_down)]
         result = middle(slices, total_rows, slice_index, part_index, arrived, chunk)
         if b == 0:
             totals = result[1]
         everyone = exchange(result[0])
         if b == 0:
-            everyone, x_far0, x_far1, *x_near = lax.optimization_barrier(
-                (everyone, x_far0, x_far1, *x_near)
-            )
-            x_all = x_near + [x_far0, x_far1, swap_cores(x_far0), swap_cores(x_far1)]
-            x_all = [far(x) for x in x_all]
             solved, residual, weight, pieces = pl.pallas_call(
                 functools.partial(second_kernel, slices, total_rows, groups),
-                in_specs=[SMEM] * 3 + [VMEM] * 3 + [ANY] * 2 * HELD_BLOCKS,
+                in_specs=[SMEM] * 3 + [VMEM] * 3 + [ANY] * (X_COUNT + Z_COUNT),
                 out_specs=[VMEM] * 4,
                 out_shape=[solved_shape, rows_shape, held((ROW_TILE, both)), pieces_shape],
-                scratch_shapes=landing_of(x_all) + landing_of(z_all),
+                scratch_shapes=landing_of(x_own.shape) + landing_of(z_shape),
                 compiler_params=room(16),
             )(slice_index, slot(b), slot(b + 1), lab, near(totals), near(everyone),
               *x_all, *z_all)
         elif b < blocks - 1:
             solved, residual, pieces = pl.pallas_call(
                 functools.partial(step_kernel, groups),
-                in_specs=[SMEM] * 2 + [VMEM] * 3 + [ANY] * 2 * HELD_BLOCKS,
+                in_specs=[SMEM] * 2 + [VMEM] * 3 + [ANY] * (X_COUNT + Z_COUNT),
                 out_specs=[VMEM] * 3,
                 out_shape=[solved_shape, rows_shape, pieces_shape],
-                scratch_shapes=landing_of(x_all) + landing_of(z_all),
+                scratch_shapes=landing_of(x_own.shape) + landing_of(z_shape),
                 compiler_params=room(16),
             )(slot(b), slot(b + 1), near(everyone), near(kept_rows[-1]), near(weight),
               *x_all, *z_all)
@@ -411,10 +418,10 @@
             head = block_width // (chips * cores) // 2
             sends = pl.pallas_call(
                 functools.partial(last_kernel, blocks, groups, width),
-                in_specs=[SMEM] * 2 + [VMEM] * (2 * blocks - 1) + [ANY] * HELD_BLOCKS,
+                in_specs=[SMEM] * 2 + [VMEM] * (2 * blocks - 1) + [ANY] * X_COUNT,
                 out_specs=VMEM,
                 out_shape=held((slices, head + width, rows_here)),
-                scratch_shapes=landing_of(x_all) + [pltpu.VMEM((LANES, LANES), F32)],
+                scratch_shapes=landing_of(x_own.shape) + [pltpu.VMEM((LANES, LANES), F32)],
                 compiler_params=room(14),
             )(place, slot(b), *map(near, (everyone, *kept_solved, *kept_rows)), *x_all)
         if b < blocks - 1:

time: 264 us -> 249 us (0.943)
  waiting for transfers between devices: 94.1 us -> 66.1 us
  starting transfers between devices: 61.4 us -> 75.6 us
  local copies, waits for them, and re-layouts: 7.3 us -> 3.54 us
  Pallas kernels: 22.2 us -> 25.6 us
    ppermute x8 -> x10, waiting for transfers between devices: 55.7 us -> 26.6 us  [shifted(): lax.ppermute(value, 'feat', [(i, (i + by) % count) for i in range(count)])]
    ppermute x8 -> x10, starting transfers between devices: 10.5 us -> 15.6 us  [shifted(): lax.ppermute(value, 'feat', [(i, (i + by) % count) for i in range(count)])]
    all_to_all x5, starting transfers between devices: 38 us -> 42.7 us  [exchange(): return lax.all_to_all(value, XZ, 0, 0, tiled=True)]
    ppermute x11 -> x14, starting transfers between devices: 12.9 us -> 17.4 us  [swap_cores(): return lax.ppermute(value, 'core', [(0, 1), (1, 0)])]
    all_to_all x3, blocking collectives: 56.3 us -> 52.5 us  [exchange(): return lax.all_to_all(value, XZ, 0, 0, tiled=True)]
    unnamed x18 -> x28, local copies, waits for them, and re-layouts: 4.04 us -> 0.72 us
    pallas_call x1, Pallas kernels: 2.56 us -> 5.4 us  [prepare(): pl.pallas_call(prepare_kernel, in_specs=[ANY, ANY], out_specs=[VMEM] * 3,...]
  transfers between devices with their start and end apart: 24 -> 29, of which waited for: 14 -> 11; matrix products, arithmetic and copies ran while one was open for 1% -> 1% of each run, Pallas kernels for 2% -> 2%
where the time goes in v5:
time: 249 us; the launch traced here: 247 us
  starting transfers between devices  75.6 us (30%)
  blocking collectives  75.5 us (30%)
  waiting for transfers between devices  66.1 us (27%)
  Pallas kernels  25.6 us (10%)
  local copies, waits for them, and re-layouts  3.54 us (1%)
    all_to_all x3, blocking collectives, exchange(): return lax.all_to_all(value, XZ, 0, 0, tiled=True)  52.5 us
    all_to_all x5, starting transfers between devices, exchange(): return lax.all_to_all(value, XZ, 0, 0, tiled=True)  42.7 us
    all_to_all x5, waiting for transfers between devices, exchange(): return lax.all_to_all(value, XZ, 0, 0, tiled=True)  36.7 us
    ppermute x10, waiting for transfers between devices, shifted(): lax.ppermute(value, 'feat', [(i, (i + by) % count) for i in range(count)])  26.6 us
    all_to_all x1, blocking collectives, local(): got = near(lax.all_to_all(sends, ('feat', 'core'), 0, 0, tiled=True))  22.9 us
    ppermute x14, starting transfers between devices, swap_cores(): return lax.ppermute(value, 'core', [(0, 1), (1, 0)])  17.4 us
    ppermute x10, starting transfers between devices, shifted(): lax.ppermute(value, 'feat', [(i, (i + by) % count) for i in range(count)])  15.6 us
    pallas_call x2, Pallas kernels, local(): pl.pallas_call(functools.partial(step_kernel, groups), in_specs=[SMEM] *...  6.94 us
  transfers between devices with their start and end apart: 29, of which 11 were waited for; matrix products, arithmetic and copies ran while one was open for 1% of the time, Pallas kernels for 2%

profile of v5, /device:TPU:1, one launch (start us, length us, event | category | flops | bytes accessed | tf_op | source)
XLA Modules:
  0.0 247.4 jit_solution(12806385132057204432)
XLA Ops:
  0.6 5.4 %shard_map.50 = (f32[512,256]{1,0:T(8,128)S(1)}, f32[512,256]{1,0:T(8,128)S(1)}, f32[256,1024]{1,0:T(8,128)S(1)}) custom-call(f32[1,1024,1024]{2,1,0:T(8,128)} %gram_ref.1, bf16[256,1024]{1,0:T(8,128)(2,1)} %x_ref.1), custom_call_target="tpu_custom_call" | custom-call | tf_op jit(solution)/shard_map/pallas_call | solution.py:61
  6.1 0.0 copy-start.1
  6.1 3.6 %collective-permute-start.12 = (f32[512,256]{1,0:T(8,128)S(1)}, f32[512,256]{1,0:T(8,128)S(1)}, u32[]{:S(2)}, u32[]{:S(2)}) collective-permute-start(f32[512,256]{1,0:T(8,128)S(1)} %get-tuple-element.17.refs_0_.refs_10_), channel_id=1, source_target_pairs={{0,192},{64,0},{128,64},{192,128},{1,193},{65,1},{129,65},{193,129... | collective-permute-start | bytes 1572872 | tf_op jit(solution)/shard_map/ppermute | solution.py:312
  9.7 0.0 collective-permute-start.3
  9.7 1.7 collective-permute-start.1
  11.4 2.2 collective-permute-start.8
  13.6 0.3 collective-permute-start
  13.9 0.9 collective-permute-done
  14.8 5.5 %collective-permute-done.12.refs_12_.refs_22_ = f32[512,256]{1,0:T(8,128)S(1)} collective-permute-done((f32[512,256]{1,0:T(8,128)S(1)}, f32[512,256]{1,0:T(8,128)S(1)}, u32[]{:S(2)}, u32[]{:S(2)}) %collective-permute-start.12) | collective-permute-done | bytes 524320 | tf_op jit(solution)/shard_map/ppermute | solution.py:312
  20.3 3.8 %collective-permute-start.2 = (f32[512,256]{1,0:T(8,128)S(1)}, f32[512,256]{1,0:T(8,128)S(1)}, u32[]{:S(2)}, u32[]{:S(2)}) collective-permute-start(f32[512,256]{1,0:T(8,128)S(1)} %get-tuple-element.18.refs_1_.refs_11_), channel_id=1, source_target_pairs={{0,1},{1,0},{2,3},{3,2},{4,5},{5,4},{6,7},{7,6},{8,9},{9,8},{10,11... | collective-permute-start | bytes 1572872 | tf_op jit(solution)/shard_map/ppermute | solution.py:31
  24.2 2.5 %collective-permute-start.13 = (f32[512,256]{1,0:T(8,128)S(1)}, f32[512,256]{1,0:T(8,128)S(1)}, u32[]{:S(2)}, u32[]{:S(2)}) collective-permute-start(f32[512,256]{1,0:T(8,128)S(1)} %collective-permute-done.12.refs_12_.refs_22_), channel_id=1, source_target_pairs={{0,1},{1,0},{2,3},{3,2},{4,5},{5,4},{6,7},{7,6},{8,9},{9,8},{10,11... | collective-permute-start | bytes 1572872 | tf_op jit(solution)/shard_map/ppermute | solution.py:31
  26.7 0.0 collective-permute-done.1.refs_2_.refs_12_
  26.7 0.0 collective-permute-start.7
  26.7 4.9 %collective-permute-done.8.refs_13_.refs_23_ = f32[512,256]{1,0:T(8,128)S(1)} collective-permute-done((f32[512,256]{1,0:T(8,128)S(1)}, f32[512,256]{1,0:T(8,128)S(1)}, u32[]{:S(2)}, u32[]{:S(2)}) %collective-permute-start.8) | collective-permute-done | bytes 524320 | tf_op jit(solution)/shard_map/ppermute | solution.py:312
  31.6 3.4 %collective-permute-start.9 = (f32[512,256]{1,0:T(8,128)S(1)}, f32[512,256]{1,0:T(8,128)}, u32[]{:S(2)}, u32[]{:S(2)}) collective-permute-start(f32[512,256]{1,0:T(8,128)S(1)} %collective-permute-done.8.refs_13_.refs_23_), channel_id=1, source_target_pairs={{0,192},{64,0},{128,64},{192,128},{1,193},{65,1},{129,65},{193,129... | collective-permute-start | bytes 1572872 | tf_op jit(solution)/shard_map/ppermute | solution.py:312
  35.0 3.0 %collective-permute-start.5 = (f32[512,256]{1,0:T(8,128)S(1)}, f32[512,256]{1,0:T(8,128)S(1)}, u32[]{:S(2)}, u32[]{:S(2)}) collective-permute-start(f32[512,256]{1,0:T(8,128)S(1)} %collective-permute-done.3.refs_4_.refs_14_), channel_id=1, source_target_pairs={{0,1},{1,0},{2,3},{3,2},{4,5},{5,4},{6,7},{7,6},{8,9},{9,8},{10,11... | collective-permute-start | bytes 1572872 | tf_op jit(solution)/shard_map/ppermute | solution.py:31
  38.0 0.0 collective-permute-done.2.refs_3_.refs_13_
  38.0 0.1 collective-permute-start.14
  38.1 0.4 collective-permute-start.6
  38.5 7.5 %collective-permute-done.7.refs_8_.refs_18_ = f32[512,256]{1,0:T(8,128)} collective-permute-done((f32[512,256]{1,0:T(8,128)S(1)}, f32[512,256]{1,0:T(8,128)}, u32[]{:S(2)}, u32[]{:S(2)}) %collective-permute-start.7) | collective-permute-done | bytes 524320 | tf_op jit(solution)/shard_map/ppermute | solution.py:312
  46.0 1.8 collective-permute-start.10
  47.8 0.0 collective-permute-done.9.refs_9_.refs_19_
  47.8 0.0 collective-permute-start.11
  47.9 0.0 collective-permute-done.5.refs_6_.refs_16_
  47.9 2.8 %collective-permute-start.19 = (f32[256,1024]{1,0:T(8,128)S(1)}, f32[256,1024]{1,0:T(8,128)S(1)}, u32[]{:S(2)}, u32[]{:S(2)}) collective-permute-start(f32[256,1024]{1,0:T(8,128)S(1)} %get-tuple-element.21.refs_0_.refs_6_), channel_id=1, source_target_pairs={{0,192},{64,0},{128,64},{192,128},{1,193},{65,1},{129,65},{193,129... | collective-permute-start | bytes 3145736 | tf_op jit(solution)/shard_map/ppermute | solution.py:312
  50.6 0.0 collective-permute-done.14.refs_15_.refs_25_
  50.7 0.1 collective-permute-start.16
  50.8 0.7 copy-done.12
  51.5 0.0 collective-permute-done.6.refs_7_.refs_17_
  51.5 3.1 %shard_map.51 = f32[32,32,128]{2,1,0:T(8,128)} custom-call(s32[1]{0:T(128)} %bitcast.4.slice_ref, s32[1]{0:T(128)} %bitcast.8.slot_ref.x_slot_ref, s32[1,512]{1,0:T(1,128)S(1)} %bitcast.10, f32[512,256]{1,0:T(8,128)} %copy-done.1, f32[512,256]{1,0:T(8,128)} %copy-done.2, f32[512,256]{1,0:T(8,128)} %copy-done.7, f32[512,256]{1,0:T(8,128)} %copy-done.9, ...), custom_call_target="tpu_custom_call" | custom-call | tf_op jit(solution)/shard_map/pallas_call | solution.py:376
  54.7 11.1 %all-to-all-start = ((f32[32,32,128]{2,1,0:T(8,128)}), f32[32,32,128]{2,1,0:T(8,128)S(1)}, u32[]{:S(2)}, u32[]{:S(2)}) async-start(f32[32,32,128]{2,1,0:T(8,128)} %shard_map.51), calls=%async_computation | async-start | bytes 1048576 | tf_op jit(solution)/shard_map/all_to_all | solution.py:316
  65.7 0.7 collective-permute-start.15
  66.5 6.6 %collective-permute-done.19.refs_8_.refs_14_ = f32[256,1024]{1,0:T(8,128)S(1)} collective-permute-done((f32[256,1024]{1,0:T(8,128)S(1)}, f32[256,1024]{1,0:T(8,128)S(1)}, u32[]{:S(2)}, u32[]{:S(2)}) %collective-permute-start.19) | collective-permute-done | bytes 1048608 | tf_op jit(solution)/shard_map/ppermute | solution.py:312
  73.1 0.9 slice.9
  74.0 3.4 %collective-permute-start.20 = (f32[128,1024]{1,0:T(8,128)}, f32[128,1024]{1,0:T(8,128)S(1)}, u32[]{:S(2)}, u32[]{:S(2)}) collective-permute-start(f32[128,1024]{1,0:T(8,128)} %slice.9), channel_id=1, source_target_pairs={{0,192},{64,0},{128,64},{192,128},{1,193},{65,1},{129,65},{193,129... | collective-permute-start | bytes 1572872 | tf_op jit(solution)/shard_map/ppermute | solution.py:312
  77.4 1.2 collective-permute-start.23
  78.6 1.9 slice.8
  80.5 0.0 collective-permute-start.17
  80.5 0.9 shard_map.52
  81.5 11.0 %all-to-all-start.1 = ((f32[32,24,128]{2,1,0:T(8,128)}), f32[32,24,128]{2,1,0:T(8,128)S(1)}, u32[]{:S(2)}, u32[]{:S(2)}) async-start(f32[32,24,128]{2,1,0:T(8,128)} %get-tuple-element.20), calls=%async_computation.1 | async-start | bytes 786432 | tf_op jit(solution)/shard_map/all_to_all | solution.py:316
  92.5 0.9 collective-permute-start.22
  93.4 2.1 collective-permute-done.18.refs_4_.refs_10_
  95.5 0.9 collective-permute-start.21
  96.4 1.9 collective-permute-done.21.refs_6_.refs_12_
  98.3 6.0 %all-to-all-done.1.everyone_ref = f32[32,24,128]{2,1,0:T(8,128)S(1)} async-done(((f32[32,24,128]{2,1,0:T(8,128)}), f32[32,24,128]{2,1,0:T(8,128)S(1)}, u32[]{:S(2)}, u32[]{:S(2)}) %all-to-all-start.1) | async-done | bytes 393248 | tf_op jit(solution)/shard_map/all_to_all | solution.py:316
  104.3 3.0 %shard_map.53 = (f32[96,1024]{1,0:T(8,128)S(1)}, f32[96,512]{1,0:T(8,128)S(1)}, f32[8,512]{1,0:T(8,128)S(1)}, f32[32,24,128]{2,1,0:T(8,128)S(1)}) custom-call(s32[1]{0:T(128)} %bitcast.4.slice_ref, s32[1]{0:T(128)} %bitcast.8.slot_ref.x_slot_ref, s32[1]{0:T(128)} %bitcast.7.z_slot_ref.x_slot_ref, s32[1,512]{1,0:T(1,128)S(1)} %bitcast.11, ...), custom_call_target="tpu_custom_call" | custom-call | tf_op jit(solution)/shard_map/pallas_call | solution.py:398
  107.3 18.4 %all_to_all.45.in_ref = f32[32,24,128]{2,1,0:T(8,128)S(1)} all-to-all(f32[32,24,128]{2,1,0:T(8,128)S(1)} %get-tuple-element.22), channel_id=1, replica_groups=mesh['feat'=4,'x'=4,'z'=8,'core'=2] {'x','z'}, dimensions={0} | all-to-all | bytes 786432 | tf_op jit(solution)/shard_map/all_to_all | solution.py:316
  125.6 0.8 shard_map.54
  126.5 7.8 %all-to-all-start.3 = ((f32[32,24,128]{2,1,0:T(8,128)}), f32[32,24,128]{2,1,0:T(8,128)S(1)}, u32[]{:S(2)}, u32[]{:S(2)}) async-start(f32[32,24,128]{2,1,0:T(8,128)} %shard_map.54), calls=%async_computation.3 | async-start | bytes 786432 | tf_op jit(solution)/shard_map/all_to_all | solution.py:316
  134.2 10.5 %all-to-all-done.3.everyone_ref = f32[32,24,128]{2,1,0:T(8,128)S(1)} async-done(((f32[32,24,128]{2,1,0:T(8,128)}), f32[32,24,128]{2,1,0:T(8,128)S(1)}, u32[]{:S(2)}, u32[]{:S(2)}) %all-to-all-start.3) | async-done | bytes 393248 | tf_op jit(solution)/shard_map/all_to_all | solution.py:316
  144.8 3.5 %shard_map.55 = (f32[96,1024]{1,0:T(8,128)S(1)}, f32[96,512]{1,0:T(8,128)S(1)}, f32[32,24,128]{2,1,0:T(8,128)S(1)}) custom-call(s32[1]{0:T(128)} %bitcast.7.z_slot_ref.x_slot_ref, s32[1]{0:T(128)} %bitcast.6.z_slot_ref.x_slot_ref, f32[32,24,128]{2,1,0:T(8,128)S(1)} %all-to-all-done.3.everyone_ref, f32[96,512]{1,0:T(8,128)S(1)} %get-tuple-element.23.old_ref.refs_3_, ...), custom_call_target="tpu_custom_call" | custom-call | tf_op jit(solution)/shard_map/pallas_call | solution.py:408
  148.3 17.5 %all_to_all.46.in_ref = f32[32,24,128]{2,1,0:T(8,128)S(1)} all-to-all(f32[32,24,128]{2,1,0:T(8,128)S(1)} %get-tuple-element.25), channel_id=1, replica_groups=mesh['feat'=4,'x'=4,'z'=8,'core'=2] {'x','z'}, dimensions={0} | all-to-all | bytes 786432 | tf_op jit(solution)/shard_map/all_to_all | solution.py:316
  165.7 0.8 shard_map.56
  166.6 7.5 %all-to-all-start.5 = ((f32[32,24,128]{2,1,0:T(8,128)}), f32[32,24,128]{2,1,0:T(8,128)S(1)}, u32[]{:S(2)}, u32[]{:S(2)}) async-start(f32[32,24,128]{2,1,0:T(8,128)} %shard_map.56), calls=%async_computation.5 | async-start | bytes 786432 | tf_op jit(solution)/shard_map/all_to_all | solution.py:316
  174.1 10.0 %all-to-all-done.5.everyone_ref = f32[32,24,128]{2,1,0:T(8,128)S(1)} async-done(((f32[32,24,128]{2,1,0:T(8,128)}), f32[32,24,128]{2,1,0:T(8,128)S(1)}, u32[]{:S(2)}, u32[]{:S(2)}) %all-to-all-start.5) | async-done | bytes 393248 | tf_op jit(solution)/shard_map/all_to_all | solution.py:316
  184.1 3.4 %shard_map.57 = (f32[96,1024]{1,0:T(8,128)S(1)}, f32[96,512]{1,0:T(8,128)S(1)}, f32[32,24,128]{2,1,0:T(8,128)S(1)}) custom-call(s32[1]{0:T(128)} %bitcast.6.z_slot_ref.x_slot_ref, s32[1]{0:T(128)} %bitcast.3.z_slot_ref.x_slot_ref, f32[32,24,128]{2,1,0:T(8,128)S(1)} %all-to-all-done.5.everyone_ref, f32[96,512]{1,0:T(8,128)S(1)} %get-tuple-element.26.old_ref.refs_4_, ...), custom_call_target="tpu_custom_call" | custom-call | tf_op jit(solution)/shard_map/pallas_call | solution.py:408
  187.5 16.7 %all_to_all.47.in_ref = f32[32,24,128]{2,1,0:T(8,128)S(1)} all-to-all(f32[32,24,128]{2,1,0:T(8,128)S(1)} %get-tuple-element.27), channel_id=1, replica_groups=mesh['feat'=4,'x'=4,'z'=8,'core'=2] {'x','z'}, dimensions={0} | all-to-all | bytes 786432 | tf_op jit(solution)/shard_map/all_to_all | solution.py:316
  204.3 0.8 shard_map.58
  205.1 5.3 %all-to-all-start.7 = ((f32[32,24,128]{2,1,0:T(8,128)}), f32[32,24,128]{2,1,0:T(8,128)S(1)}, u32[]{:S(2)}, u32[]{:S(2)}) async-start(f32[32,24,128]{2,1,0:T(8,128)} %shard_map.58), calls=%async_computation.7 | async-start | bytes 786432 | tf_op jit(solution)/shard_map/all_to_all | solution.py:316
  210.4 0.1 pad_add_fusion.1.place_ref
  210.5 10.1 %all-to-all-done.7.everyone_ref = f32[32,24,128]{2,1,0:T(8,128)S(1)} async-done(((f32[32,24,128]{2,1,0:T(8,128)}), f32[32,24,128]{2,1,0:T(8,128)S(1)}, u32[]{:S(2)}, u32[]{:S(2)}) %all-to-all-start.7) | async-done | bytes 393248 | tf_op jit(solution)/shard_map/all_to_all | solution.py:316
  220.7 2.7 %shard_map.59 = f32[8,88,256]{2,1,0:T(8,128)S(1)} custom-call(s32[3]{0:T(128)S(1)} %pad_add_fusion.1.place_ref, s32[1]{0:T(128)} %bitcast.3.z_slot_ref.x_slot_ref, f32[32,24,128]{2,1,0:T(8,128)S(1)} %all-to-all-done.7.everyone_ref, f32[96,1024]{1,0:T(8,128)S(1)} %get-tuple-element.28.refs_0_, f32[96,1024]{1,0:T(8,128)S(1)} %get-tuple-element.29.refs_1_, ...), custom_call_target="tpu_custom_call" | custom-call | tf_op jit(solution)/shard_map/pallas_call | solution.py:419
  223.3 22.9 %all_to_all.48.in_ref = f32[8,88,256]{2,1,0:T(8,128)S(1)} all-to-all(f32[8,88,256]{2,1,0:T(8,128)S(1)} %shard_map.59), channel_id=1, replica_groups=mesh['feat'=4,'x'=4,'z'=8,'core'=2] {'feat','core'}, dimensions={0} | all-to-all | bytes 1441792 | tf_op jit(solution)/shard_map/all_to_all | solution.py:431
  246.3 1.1 shard_map.60
  (41 shorter events, 0.1 us)
Async XLA Ops:
  0.6 13.0 %copy-start.13 = (s32[256]{0:T(256)S(1)}, s32[256]{0:T(256)}, u32[]{:S(2)}) copy-start(s32[256]{0:T(256)} %param.4) | copy-start | bytes 3076
  6.1 45.4 %copy-start.1 = (f32[512,256]{1,0:T(8,128)}, f32[512,256]{1,0:T(8,128)S(1)}, u32[]{:S(2)}) copy-start(f32[512,256]{1,0:T(8,128)S(1)} %get-tuple-element.17.refs_0_.refs_10_) | copy-start | bytes 1572868
  6.1 45.4 %copy-start.2 = (f32[512,256]{1,0:T(8,128)}, f32[512,256]{1,0:T(8,128)S(1)}, u32[]{:S(2)}) copy-start(f32[512,256]{1,0:T(8,128)S(1)} %get-tuple-element.18.refs_1_.refs_11_) | copy-start | bytes 1572868
  6.1 59.6 %copy-start = (f32[256,1024]{1,0:T(8,128)}, f32[256,1024]{1,0:T(8,128)S(1)}, u32[]{:S(2)}) copy-start(f32[256,1024]{1,0:T(8,128)S(1)} %get-tuple-element.21.refs_0_.refs_6_) | copy-start | bytes 3145732
  6.1 14.2 %collective-permute-start.12 = (f32[512,256]{1,0:T(8,128)S(1)}, f32[512,256]{1,0:T(8,128)S(1)}, u32[]{:S(2)}, u32[]{:S(2)}) collective-permute-start(f32[512,256]{1,0:T(8,128)S(1)} %get-tuple-element.17.refs_0_.refs_10_), channel_id=1, source_target_pairs={{0,192},{64,0},{128,64},{192,128},{1,193},{65,1},{129,65},{193,129... | collective-permute-start | bytes 1572872 | tf_op jit(solution)/shard_map/ppermute | solution.py:312
  9.7 14.5 %collective-permute-start.3 = (f32[512,256]{1,0:T(8,128)S(1)}, f32[512,256]{1,0:T(8,128)S(1)}, u32[]{:S(2)}, u32[]{:S(2)}) collective-permute-start(f32[512,256]{1,0:T(8,128)S(1)} %get-tuple-element.17.refs_0_.refs_10_), channel_id=1, source_target_pairs={{0,64},{64,128},{128,192},{192,0},{1,65},{65,129},{129,193},{193,1... | collective-permute-start | bytes 1572872 | tf_op jit(solution)/shard_map/ppermute | solution.py:312
  9.7 17.0 %collective-permute-start.1 = (f32[512,256]{1,0:T(8,128)S(1)}, f32[512,256]{1,0:T(8,128)S(1)}, u32[]{:S(2)}, u32[]{:S(2)}) collective-permute-start(f32[512,256]{1,0:T(8,128)S(1)} %get-tuple-element.17.refs_0_.refs_10_), channel_id=1, source_target_pairs={{0,1},{1,0},{2,3},{3,2},{4,5},{5,4},{6,7},{7,6},{8,9},{9,8},{10,11... | collective-permute-start | bytes 1572872 | tf_op jit(solution)/shard_map/ppermute | solution.py:31
  11.4 20.2 %collective-permute-start.8 = (f32[512,256]{1,0:T(8,128)S(1)}, f32[512,256]{1,0:T(8,128)S(1)}, u32[]{:S(2)}, u32[]{:S(2)}) collective-permute-start(f32[512,256]{1,0:T(8,128)S(1)} %get-tuple-element.18.refs_1_.refs_11_), channel_id=1, source_target_pairs={{0,192},{64,0},{128,64},{192,128},{1,193},{65,1},{129,65},{193,129... | collective-permute-start | bytes 1572872 | tf_op jit(solution)/shard_map/ppermute | solution.py:312
  13.6 1.2 collective-permute-start
  14.8 20.2 %collective-permute-start.4 = (f32[512,256]{1,0:T(8,128)S(1)}, f32[512,256]{1,0:T(8,128)}, u32[]{:S(2)}, u32[]{:S(2)}) collective-permute-start(f32[512,256]{1,0:T(8,128)S(1)} %get-tuple-element.18.refs_1_.refs_11_), channel_id=1, source_target_pairs={{0,64},{64,128},{128,192},{192,0},{1,65},{65,129},{129,193},{193,1... | collective-permute-start | bytes 1572872 | tf_op jit(solution)/shard_map/ppermute | solution.py:312
  20.3 30.3 %copy-start.5 = (f32[512,256]{1,0:T(8,128)}, f32[512,256]{1,0:T(8,128)S(1)}, u32[]{:S(2)}) copy-start(f32[512,256]{1,0:T(8,128)S(1)} %collective-permute-done.12.refs_12_.refs_22_) | copy-start | bytes 1572868
  20.3 17.7 %collective-permute-start.2 = (f32[512,256]{1,0:T(8,128)S(1)}, f32[512,256]{1,0:T(8,128)S(1)}, u32[]{:S(2)}, u32[]{:S(2)}) collective-permute-start(f32[512,256]{1,0:T(8,128)S(1)} %get-tuple-element.18.refs_1_.refs_11_), channel_id=1, source_target_pairs={{0,1},{1,0},{2,3},{3,2},{4,5},{5,4},{6,7},{7,6},{8,9},{9,8},{10,11... | collective-permute-start | bytes 1572872 | tf_op jit(solution)/shard_map/ppermute | solution.py:31
  24.2 26.5 %copy-start.6 = (f32[512,256]{1,0:T(8,128)}, f32[512,256]{1,0:T(8,128)S(1)}, u32[]{:S(2)}) copy-start(f32[512,256]{1,0:T(8,128)S(1)} %collective-permute-done.3.refs_4_.refs_14_) | copy-start | bytes 1572868
  24.2 13.9 %collective-permute-start.13 = (f32[512,256]{1,0:T(8,128)S(1)}, f32[512,256]{1,0:T(8,128)S(1)}, u32[]{:S(2)}, u32[]{:S(2)}) collective-permute-start(f32[512,256]{1,0:T(8,128)S(1)} %collective-permute-done.12.refs_12_.refs_22_), channel_id=1, source_target_pairs={{0,1},{1,0},{2,3},{3,2},{4,5},{5,4},{6,7},{7,6},{8,9},{9,8},{10,11... | collective-permute-start | bytes 1572872 | tf_op jit(solution)/shard_map/ppermute | solution.py:31
  26.7 24.1 %copy-start.7 = (f32[512,256]{1,0:T(8,128)}, f32[512,256]{1,0:T(8,128)S(1)}, u32[]{:S(2)}) copy-start(f32[512,256]{1,0:T(8,128)S(1)} %collective-permute-done.1.refs_2_.refs_12_) | copy-start | bytes 1572868
  26.7 19.3 %collective-permute-start.7 = (f32[512,256]{1,0:T(8,128)S(1)}, f32[512,256]{1,0:T(8,128)}, u32[]{:S(2)}, u32[]{:S(2)}) collective-permute-start(f32[512,256]{1,0:T(8,128)S(1)} %collective-permute-done.3.refs_4_.refs_14_), channel_id=1, source_target_pairs={{0,64},{64,128},{128,192},{192,0},{1,65},{65,129},{129,193},{193,1... | collective-permute-start | bytes 1572872 | tf_op jit(solution)/shard_map/ppermute | solution.py:312
  31.6 19.2 %copy-start.8 = (f32[512,256]{1,0:T(8,128)}, f32[512,256]{1,0:T(8,128)S(1)}, u32[]{:S(2)}) copy-start(f32[512,256]{1,0:T(8,128)S(1)} %collective-permute-done.8.refs_13_.refs_23_) | copy-start | bytes 1572868
  31.6 16.3 %collective-permute-start.9 = (f32[512,256]{1,0:T(8,128)S(1)}, f32[512,256]{1,0:T(8,128)}, u32[]{:S(2)}, u32[]{:S(2)}) collective-permute-start(f32[512,256]{1,0:T(8,128)S(1)} %collective-permute-done.8.refs_13_.refs_23_), channel_id=1, source_target_pairs={{0,192},{64,0},{128,64},{192,128},{1,193},{65,1},{129,65},{193,129... | collective-permute-start | bytes 1572872 | tf_op jit(solution)/shard_map/ppermute | solution.py:312
  35.0 12.9 %collective-permute-start.5 = (f32[512,256]{1,0:T(8,128)S(1)}, f32[512,256]{1,0:T(8,128)S(1)}, u32[]{:S(2)}, u32[]{:S(2)}) collective-permute-start(f32[512,256]{1,0:T(8,128)S(1)} %collective-permute-done.3.refs_4_.refs_14_), channel_id=1, source_target_pairs={{0,1},{1,0},{2,3},{3,2},{4,5},{5,4},{6,7},{7,6},{8,9},{9,8},{10,11... | collective-permute-start | bytes 1572872 | tf_op jit(solution)/shard_map/ppermute | solution.py:31
  38.0 12.8 %copy-start.9 = (f32[512,256]{1,0:T(8,128)}, f32[512,256]{1,0:T(8,128)S(1)}, u32[]{:S(2)}) copy-start(f32[512,256]{1,0:T(8,128)S(1)} %collective-permute-done.2.refs_3_.refs_13_) | copy-start | bytes 1572868
  38.0 12.6 %collective-permute-start.14 = (f32[512,256]{1,0:T(8,128)S(1)}, f32[512,256]{1,0:T(8,128)S(1)}, u32[]{:S(2)}, u32[]{:S(2)}) collective-permute-start(f32[512,256]{1,0:T(8,128)S(1)} %collective-permute-done.8.refs_13_.refs_23_), channel_id=1, source_target_pairs={{0,1},{1,0},{2,3},{3,2},{4,5},{5,4},{6,7},{7,6},{8,9},{9,8},{10,11... | collective-permute-start | bytes 1572872 | tf_op jit(solution)/shard_map/ppermute | solution.py:31
  38.1 12.7 %copy-start.10 = (f32[512,256]{1,0:T(8,128)}, f32[512,256]{1,0:T(8,128)S(1)}, u32[]{:S(2)}) copy-start(f32[512,256]{1,0:T(8,128)S(1)} %collective-permute-done.13.refs_14_.refs_24_) | copy-start | bytes 1572868
  38.1 13.3 %collective-permute-start.6 = (f32[512,256]{1,0:T(8,128)}, f32[512,256]{1,0:T(8,128)}, u32[]{:S(2)}, u32[]{:S(2)}) collective-permute-start(f32[512,256]{1,0:T(8,128)} %collective-permute-done.4.refs_5_.refs_15_), channel_id=1, source_target_pairs={{0,1},{1,0},{2,3},{3,2},{4,5},{5,4},{6,7},{7,6},{8,9},{9,8},{10,11... | collective-permute-start | bytes 1572872 | tf_op jit(solution)/shard_map/ppermute | solution.py:31
  46.0 5.4 %collective-permute-start.10 = (f32[512,256]{1,0:T(8,128)}, f32[512,256]{1,0:T(8,128)}, u32[]{:S(2)}, u32[]{:S(2)}) collective-permute-start(f32[512,256]{1,0:T(8,128)} %collective-permute-done.7.refs_8_.refs_18_), channel_id=1, source_target_pairs={{0,1},{1,0},{2,3},{3,2},{4,5},{5,4},{6,7},{7,6},{8,9},{9,8},{10,11... | collective-permute-start | bytes 1572872 | tf_op jit(solution)/shard_map/ppermute | solution.py:31
  47.8 3.6 %collective-permute-start.11 = (f32[512,256]{1,0:T(8,128)}, f32[512,256]{1,0:T(8,128)}, u32[]{:S(2)}, u32[]{:S(2)}) collective-permute-start(f32[512,256]{1,0:T(8,128)} %collective-permute-done.9.refs_9_.refs_19_), channel_id=1, source_target_pairs={{0,1},{1,0},{2,3},{3,2},{4,5},{5,4},{6,7},{7,6},{8,9},{9,8},{10,11... | collective-permute-start | bytes 1572872 | tf_op jit(solution)/shard_map/ppermute | solution.py:31
  47.9 2.9 %copy-start.11 = (f32[512,256]{1,0:T(8,128)}, f32[512,256]{1,0:T(8,128)S(1)}, u32[]{:S(2)}) copy-start(f32[512,256]{1,0:T(8,128)S(1)} %collective-permute-done.5.refs_6_.refs_16_) | copy-start | bytes 1572868
  47.9 25.2 %collective-permute-start.19 = (f32[256,1024]{1,0:T(8,128)S(1)}, f32[256,1024]{1,0:T(8,128)S(1)}, u32[]{:S(2)}, u32[]{:S(2)}) collective-permute-start(f32[256,1024]{1,0:T(8,128)S(1)} %get-tuple-element.21.refs_0_.refs_6_), channel_id=1, source_target_pairs={{0,192},{64,0},{128,64},{192,128},{1,193},{65,1},{129,65},{193,129... | collective-permute-start | bytes 3145736 | tf_op jit(solution)/shard_map/ppermute | solution.py:312
  50.6 0.8 copy-start.12
  50.7 28.0 %collective-permute-start.16 = (f32[256,1024]{1,0:T(8,128)S(1)}, f32[256,1024]{1,0:T(8,128)}, u32[]{:S(2)}, u32[]{:S(2)}) collective-permute-start(f32[256,1024]{1,0:T(8,128)S(1)} %get-tuple-element.21.refs_0_.refs_6_), channel_id=1, source_target_pairs={{0,64},{64,128},{128,192},{192,0},{1,65},{65,129},{129,193},{193,1... | collective-permute-start | bytes 3145736 | tf_op jit(solution)/shard_map/ppermute | solution.py:312
  54.7 25.9 %all-to-all-start = ((f32[32,32,128]{2,1,0:T(8,128)}), f32[32,32,128]{2,1,0:T(8,128)S(1)}, u32[]{:S(2)}, u32[]{:S(2)}) async-start(f32[32,32,128]{2,1,0:T(8,128)} %shard_map.51), calls=%async_computation | async-start | bytes 1048576 | tf_op jit(solution)/shard_map/all_to_all | solution.py:316
  65.7 30.7 %collective-permute-start.15 = (f32[256,1024]{1,0:T(8,128)S(1)}, f32[256,1024]{1,0:T(8,128)}, u32[]{:S(2)}, u32[]{:S(2)}) collective-permute-start(f32[256,1024]{1,0:T(8,128)S(1)} %get-tuple-element.21.refs_0_.refs_6_), channel_id=1, source_target_pairs={{0,1},{1,0},{2,3},{3,2},{4,5},{5,4},{6,7},{7,6},{8,9},{9,8},{10,11... | collective-permute-start | bytes 3145736 | tf_op jit(solution)/shard_map/ppermute | solution.py:31
  73.1 31.2 %copy-start.3 = (f32[256,1024]{1,0:T(8,128)}, f32[256,1024]{1,0:T(8,128)S(1)}, u32[]{:S(2)}) copy-start(f32[256,1024]{1,0:T(8,128)S(1)} %collective-permute-done.19.refs_8_.refs_14_) | copy-start | bytes 3145732
  74.0 18.5 %collective-permute-start.20 = (f32[128,1024]{1,0:T(8,128)}, f32[128,1024]{1,0:T(8,128)S(1)}, u32[]{:S(2)}, u32[]{:S(2)}) collective-permute-start(f32[128,1024]{1,0:T(8,128)} %slice.9), channel_id=1, source_target_pairs={{0,192},{64,0},{128,64},{192,128},{1,193},{65,1},{129,65},{193,129... | collective-permute-start | bytes 1572872 | tf_op jit(solution)/shard_map/ppermute | solution.py:312
  77.4 19.0 %collective-permute-start.23 = (f32[256,1024]{1,0:T(8,128)S(1)}, f32[256,1024]{1,0:T(8,128)}, u32[]{:S(2)}, u32[]{:S(2)}) collective-permute-start(f32[256,1024]{1,0:T(8,128)S(1)} %collective-permute-done.19.refs_8_.refs_14_), channel_id=1, source_target_pairs={{0,1},{1,0},{2,3},{3,2},{4,5},{5,4},{6,7},{7,6},{8,9},{9,8},{10,11... | collective-permute-start | bytes 3145736 | tf_op jit(solution)/shard_map/ppermute | solution.py:31
  80.5 15.0 %collective-permute-start.18 = (f32[128,1024]{1,0:T(8,128)}, f32[128,1024]{1,0:T(8,128)}, u32[]{:S(2)}, u32[]{:S(2)}) collective-permute-start(f32[128,1024]{1,0:T(8,128)} %slice.8), channel_id=1, source_target_pairs={{0,64},{64,128},{128,192},{192,0},{1,65},{65,129},{129,193},{193,1... | collective-permute-start | bytes 1572872 | tf_op jit(solution)/shard_map/ppermute | solution.py:312
  80.5 17.7 %collective-permute-start.17 = (f32[256,1024]{1,0:T(8,128)}, f32[256,1024]{1,0:T(8,128)}, u32[]{:S(2)}, u32[]{:S(2)}) collective-permute-start(f32[256,1024]{1,0:T(8,128)} %collective-permute-done.16.refs_2_.refs_8_), channel_id=1, source_target_pairs={{0,1},{1,0},{2,3},{3,2},{4,5},{5,4},{6,7},{7,6},{8,9},{9,8},{10,11... | collective-permute-start | bytes 3145736 | tf_op jit(solution)/shard_map/ppermute | solution.py:31
  81.5 22.8 %all-to-all-start.1 = ((f32[32,24,128]{2,1,0:T(8,128)}), f32[32,24,128]{2,1,0:T(8,128)S(1)}, u32[]{:S(2)}, u32[]{:S(2)}) async-start(f32[32,24,128]{2,1,0:T(8,128)} %get-tuple-element.20), calls=%async_computation.1 | async-start | bytes 786432 | tf_op jit(solution)/shard_map/all_to_all | solution.py:316
  92.5 11.8 %copy-start.4 = (f32[128,1024]{1,0:T(8,128)}, f32[128,1024]{1,0:T(8,128)S(1)}, u32[]{:S(2)}) copy-start(f32[128,1024]{1,0:T(8,128)S(1)} %collective-permute-done.20.refs_5_.refs_11_) | copy-start | bytes 1572868
  92.5 3.9 %collective-permute-start.22 = (f32[128,1024]{1,0:T(8,128)S(1)}, f32[128,1024]{1,0:T(8,128)}, u32[]{:S(2)}, u32[]{:S(2)}) collective-permute-start(f32[128,1024]{1,0:T(8,128)S(1)} %collective-permute-done.20.refs_5_.refs_11_), channel_id=1, source_target_pairs={{0,1},{1,0},{2,3},{3,2},{4,5},{5,4},{6,7},{7,6},{8,9},{9,8},{10,11... | collective-permute-start | bytes 1572872 | tf_op jit(solution)/shard_map/ppermute | solution.py:31
  95.5 2.7 %collective-permute-start.21 = (f32[128,1024]{1,0:T(8,128)}, f32[128,1024]{1,0:T(8,128)}, u32[]{:S(2)}, u32[]{:S(2)}) collective-permute-start(f32[128,1024]{1,0:T(8,128)} %collective-permute-done.18.refs_4_.refs_10_), channel_id=1, source_target_pairs={{0,1},{1,0},{2,3},{3,2},{4,5},{5,4},{6,7},{7,6},{8,9},{9,8},{10,11... | collective-permute-start | bytes 1572872 | tf_op jit(solution)/shard_map/ppermute | solution.py:31
  126.5 18.3 %all-to-all-start.3 = ((f32[32,24,128]{2,1,0:T(8,128)}), f32[32,24,128]{2,1,0:T(8,128)S(1)}, u32[]{:S(2)}, u32[]{:S(2)}) async-start(f32[32,24,128]{2,1,0:T(8,128)} %shard_map.54), calls=%async_computation.3 | async-start | bytes 786432 | tf_op jit(solution)/shard_map/all_to_all | solution.py:316
  166.6 17.5 %all-to-all-start.5 = ((f32[32,24,128]{2,1,0:T(8,128)}), f32[32,24,128]{2,1,0:T(8,128)S(1)}, u32[]{:S(2)}, u32[]{:S(2)}) async-start(f32[32,24,128]{2,1,0:T(8,128)} %shard_map.56), calls=%async_computation.5 | async-start | bytes 786432 | tf_op jit(solution)/shard_map/all_to_all | solution.py:316
  205.1 15.6 %all-to-all-start.7 = ((f32[32,24,128]{2,1,0:T(8,128)}), f32[32,24,128]{2,1,0:T(8,128)S(1)}, u32[]{:S(2)}, u32[]{:S(2)}) async-start(f32[32,24,128]{2,1,0:T(8,128)} %shard_map.58), calls=%async_computation.7 | async-start | bytes 786432 | tf_op jit(solution)/shard_map/all_to_all | solution.py:316

commit v6 on v5

v6 whole, which is shorter than its diff:
```python
import functools

import jax
import jax.numpy as jnp
from jax import lax
from jax.experimental import pallas as pl
from jax.experimental.pallas import tpu as pltpu
from jax.sharding import Mesh, PartitionSpec as P


C = 640
LANES = 128
ROW_TILE = 8
XZ = ("x", "z")
F32 = jnp.float32
BF16 = jnp.bfloat16
VMEM = pl.BlockSpec(memory_space=pltpu.VMEM)
SMEM = pl.BlockSpec(memory_space=pltpu.SMEM)
ANY = pl.BlockSpec(memory_space=pl.ANY)


def room(mib):
    return pltpu.CompilerParams(vmem_limit_bytes=mib << 20)


def dot(left, right):
    return jnp.dot(left, right, preferred_element_type=F32)


def dot_t(left, right):
    return lax.dot_general(left, right, (((1,), (1,)), ((), ())), preferred_element_type=F32)


def swap_cores(value):
    return lax.ppermute(value, "core", [(0, 1), (1, 0)])


def prepare_kernel(feat_ref, gram_ref, x_ref, z_ref, early_ref, xf_ref, gram_land, x_land, sems):
    tiles, tile, _ = gram_land.shape
    x_copy = pltpu.make_async_copy(x_ref, x_land, sems.at[tiles])
    x_copy.start()
    copies = []
    for t in range(tiles):
        source = gram_ref.at[0, pl.ds(t * tile, tile)]
        copies.append(pltpu.make_async_copy(source, gram_land.at[t], sems.at[t]))
        copies[t].start()
    x_copy.wait()
    x = x_land[...]
    wide = x.astype(F32)
    xf_ref[...] = wide
    for t in range(tiles):
        copies[t].wait()
        gram = gram_land[t]
        high = gram.astype(BF16)
        rest = gram - high.astype(F32)
        mid = rest.astype(BF16)
        low = (rest - mid.astype(F32)).astype(BF16)
        z = (dot_t(x, low) + dot_t(x, mid)) + dot_t(x, high)
        at = pl.ds(t * tile, tile)
        z_ref[:, at] = z
        early_ref[:, at] = jnp.where(feat_ref[0] == 0, wide[:, t * tile : (t + 1) * tile], z)


def prepare(features, inv_gram, feat_index, tiles=4):
    rows, width = features.shape
    return pl.pallas_call(
        prepare_kernel,
        in_specs=[SMEM, ANY, ANY],
        out_specs=[VMEM] * 3,
        out_shape=[held((rows, width))] * 3,
        scratch_shapes=[
            pltpu.VMEM((tiles, width // tiles, width), F32),
            pltpu.VMEM((rows, width), BF16),
            pltpu.SemaphoreType.DMA((tiles + 1,)),
        ],
        compiler_params=room(20),
    )(feat_index, far(inv_gram), far(features))


def held(shape, dtype=F32):
    return pltpu.VMEM(shape, dtype)


def near(value):
    return pltpu.with_memory_space_constraint(value, pltpu.VMEM)


def far(value):
    return pltpu.with_memory_space_constraint(value, pltpu.HBM)


PLACES = (
    ((0, 0, 0, 1), (1, 1, 0, 1)),
    ((2, 0, 0, 1), (3, 1, 0, 1)),
    tuple((4 + 2 * k + h, k, h, 2) for k in range(2) for h in range(2)),
    ((8, 0, 0, 1), (9, 1, 0, 1)),
)
COUNT = 10


def fetch(slot_ref, refs, landing, sems):
    for slot, parts in enumerate(PLACES):

        @pl.when(slot_ref[0] == slot)
        def _():
            for index, k, part, count in parts:
                size = landing.shape[1] // count
                target = landing.at[k, pl.ds(part * size, size)]
                pltpu.make_async_copy(refs[index], target, sems.at[k]).start()


def wait_fetch(landing, sems):
    for k in range(2):
        pltpu.make_async_copy(landing.at[k], landing.at[k], sems.at[k]).wait()


def landing_of(shape):
    return [pltpu.VMEM((2,) + shape, F32), pltpu.SemaphoreType.DMA((2,))]


def partial_sum(blocks, scaled):
    half = scaled.shape[1] // 2
    total = None
    for k in range(2):
        value = blocks[k][...]
        high = value.astype(BF16)
        low = (value - high.astype(F32)).astype(BF16)
        left = scaled[:, k * half : (k + 1) * half]
        part = dot(left, low) + dot(left, high)
        total = part if total is None else total + part
    return total


def put_pieces(out_ref, total, chunk):
    tiles = total.shape[1] // LANES
    for g in range(total.shape[0] // chunk):
        for t in range(tiles):
            out_ref[g * tiles + t, :chunk, :] = total[
                g * chunk : (g + 1) * chunk, t * LANES : (t + 1) * LANES
            ]


def take_copies(everyone_ref, groups):
    tiles = everyone_ref.shape[0] // groups
    rows = []
    for g in range(groups):
        rows.append(
            jnp.concatenate([everyone_ref[g * tiles + t] for t in range(tiles)], axis=1)
        )
    return jnp.concatenate(rows, axis=0)


def label_parts(lab, slices, width):
    group = count_steps(lab, width, slices)
    return group, lab - group * width


def count_steps(value, step, steps):
    out = jnp.zeros_like(value)
    for k in range(1, steps):
        out = out + (value >= k * step).astype(jnp.int32)
    return out


def slice_class(row, groups, share):
    chunk = -(-share // ROW_TILE) * ROW_TILE
    group = count_steps(row, chunk, groups)
    inside = row - group * chunk
    return jnp.where(inside < share, group * share + inside, -1)


def first_kernel(slices, groups, core_ref, lab_ref, za_ref, zb_ref, out_ref):
    lab = lab_ref[...]
    width = C // slices
    share = width // groups
    planes = slices // 2
    group, low_label = label_parts(lab, slices, width)
    lane_row = lax.broadcasted_iota(jnp.int32, (LANES, lab.shape[1]), 0)
    low_hot = jnp.where(low_label == lane_row, 1.0, 0.0).astype(BF16)
    group_row = lax.broadcasted_iota(jnp.int32, (slices, lab.shape[1]), 0)
    group_hot = jnp.where(group == group_row, 1.0, 0.0).astype(BF16)
    counts = dot_t(group_hot, low_hot)
    chunk = planes * share
    row = lax.broadcasted_iota(jnp.int32, (groups * chunk, 1), 0)
    part = count_steps(row, chunk, groups)
    rest = row - part * chunk
    plane = count_steps(rest, share, planes)
    wanted = (2 * plane + core_ref[0]) * width + part * share + (rest - plane * share)
    onehot = jnp.where(wanted == lab, 1.0, 0.0).astype(BF16)
    out_ref[:, chunk:, :] = jnp.broadcast_to(counts[None], (out_ref.shape[0], slices, LANES))
    put_pieces(out_ref, partial_sum((za_ref, zb_ref), onehot), chunk)


def first_middle_kernel(total_rows, share, core_ref, part_ref, in_ref, out_ref, totals_ref):
    planes, _, _ = out_ref.shape
    summed = jnp.sum(in_ref[...], axis=0)
    solved = summed[: planes * share]
    totals = summed[planes * share :]
    totals_ref[...] = totals
    slice_row = lax.broadcasted_iota(jnp.int32, totals.shape, 0)
    row = lax.broadcasted_iota(jnp.int32, solved.shape, 0)
    lane = lax.broadcasted_iota(jnp.int32, solved.shape, 1)
    plane = count_steps(row, share, planes)
    counts = jnp.zeros(solved.shape, F32)
    for g in range(planes):
        mine = jnp.where(slice_row == 2 * g + core_ref[0], totals, 0.0)
        counts = jnp.where(plane == g, jnp.sum(mine, axis=0, keepdims=True), counts)
    here = part_ref[0] * share + (row - plane * share)
    counts = jnp.sum(jnp.where(lane == here, counts, 0.0), axis=1, keepdims=True)
    scale = jnp.where(counts > 0.0, total_rows / (C * jnp.maximum(counts, 1.0)), 0.0)
    solved = solved * scale.astype(BF16).astype(F32)
    out_ref[...] = jnp.zeros(out_ref.shape, F32)
    for g in range(planes):
        out_ref[g, :share, :] = solved[g * share : (g + 1) * share]


def spread_kernel(in_ref, copies_ref):
    copies_ref[...] = jnp.broadcast_to(in_ref[0][None], copies_ref.shape)


def middle_kernel(in_ref, copies_ref):
    copies_ref[...] = jnp.broadcast_to(jnp.sum(in_ref[...], axis=0)[None], copies_ref.shape)


def to_copies(kernel, arrived, shape):
    return pl.pallas_call(
        kernel,
        in_specs=[VMEM],
        out_specs=VMEM,
        out_shape=held(shape),
        compiler_params=room(8),
    )(near(arrived))


def update(solved, landing, residual):
    rows = landing.shape[1]
    solved = solved.astype(BF16)
    parts = [
        residual[:, k * rows : (k + 1) * rows] - dot_t(solved, landing[k].astype(BF16))
        for k in range(2)
    ]
    return jnp.concatenate(parts, axis=1)


def second_kernel(
    slices, total_rows, groups, slice_ref, x_slot_ref, z_slot_ref, lab_ref, totals_ref,
    everyone_ref, *refs,
):
    x_refs, z_refs, refs = refs[:COUNT], refs[COUNT:][:COUNT], refs[2 * COUNT :]
    solved_ref, residual_ref, weight_ref, out_ref, x_land, x_sems, z_land, z_sems = refs
    fetch(x_slot_ref, x_refs, x_land, x_sems)
    fetch(z_slot_ref, z_refs, z_land, z_sems)
    lab = lab_ref[...]
    group, low_label = label_parts(lab, slices, C // slices)
    solved = take_copies(everyone_ref, groups)
    solved_ref[...] = solved
    padded = solved.shape[0]
    share = C // slices // groups
    row = lax.broadcasted_iota(jnp.int32, (padded, lab.shape[1]), 0)
    hit = low_label == slice_class(row, groups, share)
    columns = totals_ref[...].T
    empty = jnp.zeros((padded // groups - share, columns.shape[1]), F32)
    columns = jnp.concatenate(
        [v for g in range(groups) for v in (columns[g * share : (g + 1) * share], empty)], axis=0
    )
    spread = jnp.zeros((padded, lab.shape[1]), F32)
    for d in range(slices):
        spread = jnp.where(group == d, columns[:, d : d + 1], spread)
    row_count = jnp.sum(jnp.where(hit, spread, 0.0), axis=0, keepdims=True)
    weight = total_rows / (C * row_count)
    weight_ref[...] = jnp.broadcast_to(weight, weight_ref.shape)
    onehot = jnp.where(hit & (group == slice_ref[0]), 1.0, 0.0)
    wait_fetch(x_land, x_sems)
    residual = update(solved, x_land, onehot)
    residual_ref[...] = residual
    wait_fetch(z_land, z_sems)
    put_pieces(out_ref, partial_sum((z_land.at[0], z_land.at[1]), (weight * residual).astype(BF16)), out_ref.shape[1])


def step_kernel(groups, x_slot_ref, z_slot_ref, everyone_ref, old_ref, weight_ref, *refs):
    x_refs, z_refs, refs = refs[:COUNT], refs[COUNT:][:COUNT], refs[2 * COUNT :]
    solved_ref, residual_ref, out_ref, x_land, x_sems, z_land, z_sems = refs
    fetch(x_slot_ref, x_refs, x_land, x_sems)
    fetch(z_slot_ref, z_refs, z_land, z_sems)
    solved = take_copies(everyone_ref, groups)
    solved_ref[...] = solved
    wait_fetch(x_land, x_sems)
    residual = update(solved, x_land, old_ref[...])
    residual_ref[...] = residual
    scaled = (weight_ref[0:1, :] * residual).astype(BF16)
    wait_fetch(z_land, z_sems)
    put_pieces(out_ref, partial_sum((z_land.at[0], z_land.at[1]), scaled), out_ref.shape[1])


def last_kernel(
    blocks, groups, width, place_ref, x_slot_ref, everyone_ref, *refs,
):
    solved_refs, refs = refs[: blocks - 1], refs[blocks - 1 :]
    rows_refs, refs = refs[: blocks - 1], refs[blocks - 1 :]
    x_refs, (out_ref, x_land, x_sems, turned) = refs[:COUNT], refs[COUNT:]
    fetch(x_slot_ref, x_refs, x_land, x_sems)
    last_solved = take_copies(everyone_ref, groups)
    rows = x_land.shape[1]
    head = out_ref.shape[1] - width
    share = 2 * head
    share_rows = width // groups
    chunk = last_solved.shape[0] // groups
    for b in range(blocks):
        solved = last_solved if b == blocks - 1 else solved_refs[b][...]
        tile = jnp.zeros((solved.shape[0], LANES), F32)
        for t in range(solved.shape[1] // LANES):
            tile = jnp.where(place_ref[1] == t, solved[:, t * LANES : (t + 1) * LANES], tile)
        empty = jnp.zeros((LANES - tile.shape[0], LANES), F32)
        turned[...] = jnp.concatenate([tile, empty], axis=0).T
        for k in range(2):
            begin = place_ref[2] * (2 * share) + k * share
            begin = pl.multiple_of(begin, ROW_TILE)
            for h in range(2):
                out_ref[2 * b + k, :head, h * LANES : (h + 1) * LANES] = turned[
                    pl.ds(pl.multiple_of(begin + h * head, ROW_TILE), head), :
                ]
    wait_fetch(x_land, x_sems)
    last = update(last_solved, x_land, rows_refs[-1][...])
    for b in range(blocks):
        value = last if b == blocks - 1 else rows_refs[b][...]
        for k in range(2):
            mine = jnp.where(place_ref[0] == k, value[:, :rows], value[:, rows:])
            for g in range(groups):
                out_ref[2 * b + k, head + g * share_rows : head + (g + 1) * share_rows, :] = mine[
                    g * chunk : g * chunk + share_rows
                ]


def join_kernel(groups, in_ref, weights_ref, after_ref):
    slices, deep, _ = in_ref.shape
    width = C // slices
    head = deep - width
    share = width // groups
    chunk = -(-share // ROW_TILE) * ROW_TILE
    for d in range(slices):
        for h in range(2):
            for g in range(groups):
                at = d * width + g * share
                come = h * LANES + g * chunk
                weights_ref[h * head : (h + 1) * head, at : at + share] = in_ref[
                    d, :head, come : come + share
                ]
    joined = jnp.concatenate([in_ref[d, head:, :] for d in range(slices)], axis=0)
    after_ref[0] = joined.T


def shifted(value, by):
    count = lax.axis_size("feat")
    return lax.ppermute(value, "feat", [(i, (i + by) % count) for i in range(count)])


def exchange(value):
    return lax.all_to_all(value, XZ, 0, 0, tiled=True)


def deal(value):
    return lax.all_to_all(value, "feat", 0, 0, tiled=True)


def halves(value):
    middle_row = value.shape[0] // 2
    return value[:middle_row], value[middle_row:]


def local(features, labels, inv_gram):
    rows_here, block_width = features.shape
    blocks = lax.axis_size("feat")
    cores = lax.axis_size("core")
    groups = lax.axis_size("x")
    depth = lax.axis_size("z")
    chips = groups * depth
    slices = blocks * cores
    width = C // slices
    share = width // groups
    chunk = -(-share // ROW_TILE) * ROW_TILE
    padded = groups * chunk
    core = lax.axis_index("core").astype(jnp.int32)
    feat = lax.axis_index("feat").astype(jnp.int32)
    x_index = lax.axis_index("x").astype(jnp.int32)
    chip = x_index * depth + lax.axis_index("z").astype(jnp.int32)
    per_tile = LANES * chips // block_width
    place = jnp.stack([core, chip // per_tile, chip % per_tile])
    slice_index = (feat * cores + core)[None]
    part_index = x_index[None]
    core_index = core[None]
    total_rows = float(rows_here * chips * cores)
    both = cores * rows_here

    def slot(b):
        return lax.rem(feat + (blocks - b), blocks)[None]

    z_own, early, late = prepare(features, inv_gram, feat[None])
    lab = jnp.concatenate([labels, swap_cores(labels)])[None, :]

    def move(value, by):
        return shifted(value, by)

    def swap(value):
        return swap_cores(value)

    def gathered(own):
        up, down = move(own, 1), move(own, -1)
        far0 = move(halves(up)[0], 1)
        far1 = move(halves(down)[1], -1)
        blocks_held = [own, swap(own), up, swap(up)]
        blocks_held += [far0, far1, swap(far0), swap(far1)]
        blocks_held += [down, swap(down)]
        return [far(block) for block in blocks_held]

    z_other = swap(z_own)
    early_all = gathered(early)
    late_all = gathered(late)
    block_shape = early.shape

    first_chunk = blocks * share
    pieces = pl.pallas_call(
        functools.partial(first_kernel, slices, groups),
        in_specs=[SMEM] + [VMEM] * 3,
        out_specs=VMEM,
        out_shape=held((chips, first_chunk + slices, LANES)),
        compiler_params=room(16),
    )(core_index, lab, near(z_own), near(z_other))

    rows_shape = held((padded, both))
    solved_shape = held((padded, block_width))
    pieces_shape = held((chips, chunk, LANES))
    kept_rows = []
    kept_solved = []
    totals = weight = None
    for b in range(blocks):
        arrived = exchange(pieces)
        if b == 0:
            parts, totals = pl.pallas_call(
                functools.partial(first_middle_kernel, total_rows, share),
                in_specs=[SMEM, SMEM, VMEM],
                out_specs=[VMEM] * 2,
                out_shape=[held((blocks, chunk, LANES)), held((slices, LANES))],
                compiler_params=room(12),
            )(core_index, part_index, near(arrived))
            parts = deal(parts)
            copies = to_copies(spread_kernel, parts, (chips, chunk, LANES))
        else:
            copies = to_copies(middle_kernel, arrived, (chips, chunk, LANES))
        everyone = exchange(copies)
        x_all = early_all if b == 0 else late_all
        if b == 0:
            solved, residual, weight, pieces = pl.pallas_call(
                functools.partial(second_kernel, slices, total_rows, groups),
                in_specs=[SMEM] * 3 + [VMEM] * 3 + [ANY] * 2 * COUNT,
                out_specs=[VMEM] * 4,
                out_shape=[solved_shape, rows_shape, held((ROW_TILE, both)), pieces_shape],
                scratch_shapes=landing_of(block_shape) * 2,
                compiler_params=room(16),
            )(slice_index, slot(b), slot(b + 1), lab, near(totals), near(everyone),
              *x_all, *early_all)
        elif b < blocks - 1:
            solved, residual, pieces = pl.pallas_call(
                functools.partial(step_kernel, groups),
                in_specs=[SMEM] * 2 + [VMEM] * 3 + [ANY] * 2 * COUNT,
                out_specs=[VMEM] * 3,
                out_shape=[solved_shape, rows_shape, pieces_shape],
                scratch_shapes=landing_of(block_shape) * 2,
                compiler_params=room(16),
            )(slot(b), slot(b + 1), near(everyone), near(kept_rows[-1]), near(weight),
              *x_all, *early_all)
        else:
            head = block_width // (chips * cores) // 2
            sends = pl.pallas_call(
                functools.partial(last_kernel, blocks, groups, width),
                in_specs=[SMEM] * 2 + [VMEM] * (2 * blocks - 1) + [ANY] * COUNT,
                out_specs=VMEM,
                out_shape=held((slices, head + width, rows_here)),
                scratch_shapes=landing_of(block_shape) + [pltpu.VMEM((LANES, LANES), F32)],
                compiler_params=room(14),
            )(place, slot(b), *map(near, (everyone, *kept_solved, *kept_rows)), *x_all)
        if b < blocks - 1:
            kept_solved.append(solved)
            kept_rows.append(residual)

    got = near(lax.all_to_all(sends, ("feat", "core"), 0, 0, tiled=True))
    return pl.pallas_call(
        functools.partial(join_kernel, groups),
        in_specs=[VMEM],
        out_specs=[VMEM, VMEM],
        out_shape=[
            jax.ShapeDtypeStruct((block_width // (chips * cores), C), F32),
            jax.ShapeDtypeStruct((1, rows_here, C), F32),
        ],
        compiler_params=room(12),
    )(got)


def solution(mesh):
    sizes = dict(mesh.shape)
    fine = Mesh(mesh.devices.reshape(sizes["feat"], 4, 8, 2), ("feat", "x", "z", "core"))
    rows = ("x", "z", "core")
    in_specs = (P(rows, "feat"), P(rows), P("feat", None, None))
    out_specs = (P(("feat",) + rows, None), P("feat", rows, None))

    return jax.shard_map(local, mesh=fine, in_specs=in_specs, out_specs=out_specs, check_vma=False)
```

time: 249 us -> 245 us (0.984)
  blocking collectives: 75.5 us -> 66.5 us
  local copies, waits for them, and re-layouts: 3.54 us -> 6.73 us
    all_to_all x3 -> x2, blocking collectives: 52.5 us -> 35.8 us  [exchange(): return lax.all_to_all(value, XZ, 0, 0, tiled=True)]
    all_to_all x0 -> x1, blocking collectives: none -> 8.98 us  [deal(): return lax.all_to_all(value, 'feat', 0, 0, tiled=True)]
    all_to_all x5 -> x6, waiting for transfers between devices: 36.7 us -> 29 us  [exchange(): return lax.all_to_all(value, XZ, 0, 0, tiled=True)]
    all_to_all x5 -> x6, starting transfers between devices: 42.7 us -> 50 us  [exchange(): return lax.all_to_all(value, XZ, 0, 0, tiled=True)]
    ppermute x10 -> x8, starting transfers between devices: 15.6 us -> 9.31 us  [shifted(): lax.ppermute(value, 'feat', [(i, (i + by) % count) for i in range(count)])]
    ppermute x10 -> x8, waiting for transfers between devices: 26.6 us -> 31.1 us  [shifted(): lax.ppermute(value, 'feat', [(i, (i + by) % count) for i in range(count)])]
    slice x2 -> x4, local copies, waits for them, and re-layouts: 2.82 us -> 6.71 us  [halves(): return (value[:middle_row], value[middle_row:])]
    ppermute x14 -> x12, waiting for transfers between devices: 2.78 us -> 5.94 us  [swap_cores(): return lax.ppermute(value, 'core', [(0, 1), (1, 0)])]
  transfers between devices with their start and end apart: 29 -> 26, of which waited for: 11 -> 10; matrix products, arithmetic and copies ran while one was open for 1% -> 3% of each run, Pallas kernels for 2% -> 2%
where the time goes in v6:
time: 245 us; the launch traced here: 244 us
  starting transfers between devices  78 us (32%)
  blocking collectives  66.5 us (27%)
  waiting for transfers between devices  66 us (27%)
  Pallas kernels  25.7 us (10%)
  local copies, waits for them, and re-layouts  6.73 us (3%)
    all_to_all x6, starting transfers between devices, exchange(): return lax.all_to_all(value, XZ, 0, 0, tiled=True)  50 us
    all_to_all x2, blocking collectives, exchange(): return lax.all_to_all(value, XZ, 0, 0, tiled=True)  35.8 us
    ppermute x8, waiting for transfers between devices, shifted(): lax.ppermute(value, 'feat', [(i, (i + by) % count) for i in range(count)])  31.1 us
    all_to_all x6, waiting for transfers between devices, exchange(): return lax.all_to_all(value, XZ, 0, 0, tiled=True)  29 us
    all_to_all x1, blocking collectives, local(): got = near(lax.all_to_all(sends, ('feat', 'core'), 0, 0, tiled=True))  21.7 us
    ppermute x12, starting transfers between devices, swap_cores(): return lax.ppermute(value, 'core', [(0, 1), (1, 0)])  18.7 us
    ppermute x8, starting transfers between devices, shifted(): lax.ppermute(value, 'feat', [(i, (i + by) % count) for i in range(count)])  9.31 us
    all_to_all x1, blocking collectives, deal(): return lax.all_to_all(value, 'feat', 0, 0, tiled=True)  8.98 us
  transfers between devices with their start and end apart: 26, of which 10 were waited for; matrix products, arithmetic and copies ran while one was open for 3% of the time, Pallas kernels for 2%

profile of v6, /device:TPU:1, one launch (start us, length us, event | category | flops | bytes accessed | tf_op | source)
XLA Modules:
  0.0 243.8 jit_solution(6128825172107833654)
XLA Ops:
  0.6 5.4 %shard_map.50 = (f32[256,1024]{1,0:T(8,128)S(1)}, f32[256,1024]{1,0:T(8,128)S(1)}, f32[256,1024]{1,0:T(8,128)S(1)}) custom-call(s32[1]{0:T(128)} %bitcast.10.feat_ref, f32[1,1024,1024]{2,1,0:T(8,128)} %gram_ref.1, bf16[256,1024]{1,0:T(8,128)(2,1)} %x_ref.1), custom_call_target="tpu_custom_call" | custom-call | tf_op jit(solution)/shard_map/pallas_call | solution.py:66
  6.1 3.3 %collective-permute-start.1 = (f32[256,1024]{1,0:T(8,128)S(1)}, f32[256,1024]{1,0:T(8,128)}, u32[]{:S(2)}, u32[]{:S(2)}) collective-permute-start(f32[256,1024]{1,0:T(8,128)S(1)} %get-tuple-element.17.za_ref), channel_id=1, source_target_pairs={{0,1},{1,0},{2,3},{3,2},{4,5},{5,4},{6,7},{7,6},{8,9},{9,8},{10,11... | collective-permute-start | bytes 3145736 | tf_op jit(solution)/shard_map/ppermute | solution.py:35
  9.4 0.1 collective-permute-start
  9.5 2.3 collective-permute-done
  11.8 3.3 %shard_map.51 = f32[32,88,128]{2,1,0:T(8,128)} custom-call(s32[1]{0:T(128)} %bitcast.core_ref, s32[1,512]{1,0:T(1,128)S(1)} %bitcast.11, f32[256,1024]{1,0:T(8,128)S(1)} %get-tuple-element.17.za_ref, f32[256,1024]{1,0:T(8,128)} %collective-permute-done.1.zb_ref), custom_call_target="tpu_custom_call" | custom-call | tf_op jit(solution)/shard_map/pallas_call | solution.py:421
  15.1 9.3 %all-to-all-start = ((f32[32,88,128]{2,1,0:T(8,128)}), f32[32,88,128]{2,1,0:T(8,128)S(1)}, u32[]{:S(2)}, u32[]{:S(2)}) async-start(f32[32,88,128]{2,1,0:T(8,128)} %shard_map.51), calls=%async_computation | async-start | bytes 2883584 | tf_op jit(solution)/shard_map/all_to_all | solution.py:358
  24.4 2.8 %collective-permute-start.6 = (f32[256,1024]{1,0:T(8,128)S(1)}, f32[256,1024]{1,0:T(8,128)}, u32[]{:S(2)}, u32[]{:S(2)}) collective-permute-start(f32[256,1024]{1,0:T(8,128)S(1)} %get-tuple-element.20.refs_0_.refs_10_), channel_id=1, source_target_pairs={{0,192},{64,0},{128,64},{192,128},{1,193},{65,1},{129,65},{193,129... | collective-permute-start | bytes 3145736 | tf_op jit(solution)/shard_map/ppermute | solution.py:354
  27.3 0.9 collective-permute-start.2
  28.2 20.9 %collective-permute-done.6.refs_8_.refs_18_ = f32[256,1024]{1,0:T(8,128)} collective-permute-done((f32[256,1024]{1,0:T(8,128)S(1)}, f32[256,1024]{1,0:T(8,128)}, u32[]{:S(2)}, u32[]{:S(2)}) %collective-permute-start.6) | collective-permute-done | bytes 1048608 | tf_op jit(solution)/shard_map/ppermute | solution.py:354
  49.1 1.1 slice.17
  50.2 3.6 %collective-permute-start.7 = (f32[128,1024]{1,0:T(8,128)S(1)}, f32[128,1024]{1,0:T(8,128)}, u32[]{:S(2)}, u32[]{:S(2)}) collective-permute-start(f32[128,1024]{1,0:T(8,128)S(1)} %slice.17), channel_id=1, source_target_pairs={{0,192},{64,0},{128,64},{192,128},{1,193},{65,1},{129,65},{193,129... | collective-permute-start | bytes 1572872 | tf_op jit(solution)/shard_map/ppermute | solution.py:354
  53.8 0.0 collective-permute-done.3.refs_2_.refs_12_
  53.8 1.9 slice.16
  55.7 0.0 collective-permute-start.5
  55.7 1.8 collective-permute-start.10
  57.5 6.1 %collective-permute-done.7.refs_5_.refs_15_ = f32[128,1024]{1,0:T(8,128)} collective-permute-done((f32[128,1024]{1,0:T(8,128)S(1)}, f32[128,1024]{1,0:T(8,128)}, u32[]{:S(2)}, u32[]{:S(2)}) %collective-permute-start.7) | collective-permute-done | bytes 524320 | tf_op jit(solution)/shard_map/ppermute | solution.py:354
  63.6 2.4 collective-permute-start.9
  65.9 0.0 collective-permute-start.4
  65.9 0.0 all-to-all-done.in_ref
  65.9 0.1 shard_map.52
  66.1 9.0 %all_to_all.50.in_ref = f32[4,24,128]{2,1,0:T(8,128)S(1)} all-to-all(f32[4,24,128]{2,1,0:T(8,128)S(1)} %get-tuple-element.19), channel_id=1, replica_groups=mesh['feat'=4,'x'=4,'z'=8,'core'=2] {'feat'}, dimensions={0} | all-to-all | bytes 98304 | tf_op jit(solution)/shard_map/all_to_all | solution.py:362
  75.1 0.8 shard_map.53
  75.8 8.9 %all-to-all-start.2 = ((f32[32,24,128]{2,1,0:T(8,128)}), f32[32,24,128]{2,1,0:T(8,128)S(1)}, u32[]{:S(2)}, u32[]{:S(2)}) async-start(f32[32,24,128]{2,1,0:T(8,128)} %shard_map.53), calls=%async_computation.2 | async-start | bytes 786432 | tf_op jit(solution)/shard_map/all_to_all | solution.py:358
  84.8 0.0 collective-permute-done.2.refs_1_.refs_11_
  84.8 1.1 collective-permute-start.15
  85.9 0.6 collective-permute-start.12
  86.5 2.8 %collective-permute-start.8 = (f32[128,1024]{1,0:T(8,128)}, f32[128,1024]{1,0:T(8,128)S(1)}, u32[]{:S(2)}, u32[]{:S(2)}) collective-permute-start(f32[128,1024]{1,0:T(8,128)} %collective-permute-done.5.refs_4_.refs_14_), channel_id=1, source_target_pairs={{0,1},{1,0},{2,3},{3,2},{4,5},{5,4},{6,7},{7,6},{8,9},{9,8},{10,11... | collective-permute-start | bytes 1572872 | tf_op jit(solution)/shard_map/ppermute | solution.py:35
  89.3 0.0 collective-permute-done.10.refs_9_.refs_19_
  89.3 1.7 collective-permute-done.8.refs_6_.refs_16_
  91.0 0.0 collective-permute-done.4.refs_3_.refs_13_
  91.0 4.3 %all-to-all-done.2.everyone_ref = f32[32,24,128]{2,1,0:T(8,128)S(1)} async-done(((f32[32,24,128]{2,1,0:T(8,128)}), f32[32,24,128]{2,1,0:T(8,128)S(1)}, u32[]{:S(2)}, u32[]{:S(2)}) %all-to-all-start.2) | async-done | bytes 393248 | tf_op jit(solution)/shard_map/all_to_all | solution.py:358
  95.3 3.5 %shard_map.54 = (f32[96,1024]{1,0:T(8,128)S(1)}, f32[96,512]{1,0:T(8,128)S(1)}, f32[8,512]{1,0:T(8,128)S(1)}, f32[32,24,128]{2,1,0:T(8,128)}) custom-call(s32[1]{0:T(128)} %bitcast.6.slice_ref, s32[1]{0:T(128)} %bitcast.7.x_slot_ref, s32[1]{0:T(128)} %bitcast.5.z_slot_ref.x_slot_ref, s32[1,512]{1,0:T(1,128)S(1)} %bitcast.12, ...), custom_call_target="tpu_custom_call" | custom-call | tf_op jit(solution)/shard_map/pallas_call | solution.py:452
  98.8 7.4 %all-to-all-start.3 = ((f32[32,24,128]{2,1,0:T(8,128)}), f32[32,24,128]{2,1,0:T(8,128)S(1)}, u32[]{:S(2)}, u32[]{:S(2)}) async-start(f32[32,24,128]{2,1,0:T(8,128)} %get-tuple-element.21), calls=%async_computation.3 | async-start | bytes 786432 | tf_op jit(solution)/shard_map/all_to_all | solution.py:358
  106.2 2.8 %collective-permute-start.11 = (f32[256,1024]{1,0:T(8,128)S(1)}, f32[256,1024]{1,0:T(8,128)}, u32[]{:S(2)}, u32[]{:S(2)}) collective-permute-start(f32[256,1024]{1,0:T(8,128)S(1)} %get-tuple-element.24.refs_0_.refs_6_), channel_id=1, source_target_pairs={{0,1},{1,0},{2,3},{3,2},{4,5},{5,4},{6,7},{7,6},{8,9},{9,8},{10,11... | collective-permute-start | bytes 3145736 | tf_op jit(solution)/shard_map/ppermute | solution.py:35
  109.0 1.9 slice.19
  110.9 1.2 collective-permute-start.16
  112.1 2.9 %collective-permute-start.19 = (f32[256,1024]{1,0:T(8,128)}, f32[256,1024]{1,0:T(8,128)}, u32[]{:S(2)}, u32[]{:S(2)}) collective-permute-start(f32[256,1024]{1,0:T(8,128)} %collective-permute-done.15.refs_8_.refs_14_), channel_id=1, source_target_pairs={{0,1},{1,0},{2,3},{3,2},{4,5},{5,4},{6,7},{7,6},{8,9},{9,8},{10,11... | collective-permute-start | bytes 3145736 | tf_op jit(solution)/shard_map/ppermute | solution.py:35
  115.0 0.0 collective-permute-done.12.refs_2_.refs_8_
  115.0 1.9 slice.18
  116.9 0.0 collective-permute-start.13
  116.9 0.0 all-to-all-done.3.in_ref
  116.9 0.8 shard_map.55
  117.7 9.2 %all-to-all-start.4 = ((f32[32,24,128]{2,1,0:T(8,128)}), f32[32,24,128]{2,1,0:T(8,128)S(1)}, u32[]{:S(2)}, u32[]{:S(2)}) async-start(f32[32,24,128]{2,1,0:T(8,128)} %shard_map.55), calls=%async_computation.4 | async-start | bytes 786432 | tf_op jit(solution)/shard_map/all_to_all | solution.py:358
  126.9 0.9 collective-permute-start.18
  127.8 4.1 %collective-permute-done.14.refs_4_.refs_10_ = f32[128,1024]{1,0:T(8,128)} collective-permute-done((f32[128,1024]{1,0:T(8,128)}, f32[128,1024]{1,0:T(8,128)}, u32[]{:S(2)}, u32[]{:S(2)}) %collective-permute-start.14) | collective-permute-done | bytes 524320 | tf_op jit(solution)/shard_map/ppermute | solution.py:354
  131.9 0.9 collective-permute-start.17
  132.7 0.0 collective-permute-done.19.refs_9_.refs_15_
  132.7 1.9 collective-permute-done.17.refs_6_.refs_12_
  134.6 0.0 collective-permute-done.13.refs_3_.refs_9_
  134.6 4.1 %all-to-all-done.4.everyone_ref = f32[32,24,128]{2,1,0:T(8,128)S(1)} async-done(((f32[32,24,128]{2,1,0:T(8,128)}), f32[32,24,128]{2,1,0:T(8,128)S(1)}, u32[]{:S(2)}, u32[]{:S(2)}) %all-to-all-start.4) | async-done | bytes 393248 | tf_op jit(solution)/shard_map/all_to_all | solution.py:358
  138.7 3.2 %shard_map.56 = (f32[96,1024]{1,0:T(8,128)S(1)}, f32[96,512]{1,0:T(8,128)S(1)}, f32[32,24,128]{2,1,0:T(8,128)S(1)}) custom-call(s32[1]{0:T(128)} %bitcast.5.z_slot_ref.x_slot_ref, s32[1]{0:T(128)} %bitcast.4.z_slot_ref.x_slot_ref, f32[32,24,128]{2,1,0:T(8,128)S(1)} %all-to-all-done.4.everyone_ref, f32[96,512]{1,0:T(8,128)S(1)} %get-tuple-element.22.old_ref.refs_3_, ...), custom_call_target="tpu_custom_call" | custom-call | tf_op jit(solution)/shard_map/pallas_call | solution.py:462
  141.9 18.4 %all_to_all.51.in_ref = f32[32,24,128]{2,1,0:T(8,128)S(1)} all-to-all(f32[32,24,128]{2,1,0:T(8,128)S(1)} %get-tuple-element.25), channel_id=1, replica_groups=mesh['feat'=4,'x'=4,'z'=8,'core'=2] {'x','z'}, dimensions={0} | all-to-all | bytes 786432 | tf_op jit(solution)/shard_map/all_to_all | solution.py:358
  160.2 0.8 shard_map.57
  161.0 7.8 %all-to-all-start.6 = ((f32[32,24,128]{2,1,0:T(8,128)}), f32[32,24,128]{2,1,0:T(8,128)S(1)}, u32[]{:S(2)}, u32[]{:S(2)}) async-start(f32[32,24,128]{2,1,0:T(8,128)} %shard_map.57), calls=%async_computation.6 | async-start | bytes 786432 | tf_op jit(solution)/shard_map/all_to_all | solution.py:358
  168.8 10.5 %all-to-all-done.6.everyone_ref = f32[32,24,128]{2,1,0:T(8,128)S(1)} async-done(((f32[32,24,128]{2,1,0:T(8,128)}), f32[32,24,128]{2,1,0:T(8,128)S(1)}, u32[]{:S(2)}, u32[]{:S(2)}) %all-to-all-start.6) | async-done | bytes 393248 | tf_op jit(solution)/shard_map/all_to_all | solution.py:358
  179.3 3.1 %shard_map.58 = (f32[96,1024]{1,0:T(8,128)S(1)}, f32[96,512]{1,0:T(8,128)S(1)}, f32[32,24,128]{2,1,0:T(8,128)S(1)}) custom-call(s32[1]{0:T(128)} %bitcast.4.z_slot_ref.x_slot_ref, s32[1]{0:T(128)} %bitcast.3.z_slot_ref.x_slot_ref, f32[32,24,128]{2,1,0:T(8,128)S(1)} %all-to-all-done.6.everyone_ref, f32[96,512]{1,0:T(8,128)S(1)} %get-tuple-element.26.old_ref.refs_4_, ...), custom_call_target="tpu_custom_call" | custom-call | tf_op jit(solution)/shard_map/pallas_call | solution.py:462
  182.5 17.5 %all_to_all.52.in_ref = f32[32,24,128]{2,1,0:T(8,128)S(1)} all-to-all(f32[32,24,128]{2,1,0:T(8,128)S(1)} %get-tuple-element.27), channel_id=1, replica_groups=mesh['feat'=4,'x'=4,'z'=8,'core'=2] {'x','z'}, dimensions={0} | all-to-all | bytes 786432 | tf_op jit(solution)/shard_map/all_to_all | solution.py:358
  199.9 0.8 shard_map.59
  200.7 7.3 %all-to-all-start.8 = ((f32[32,24,128]{2,1,0:T(8,128)}), f32[32,24,128]{2,1,0:T(8,128)S(1)}, u32[]{:S(2)}, u32[]{:S(2)}) async-start(f32[32,24,128]{2,1,0:T(8,128)} %shard_map.59), calls=%async_computation.8 | async-start | bytes 786432 | tf_op jit(solution)/shard_map/all_to_all | solution.py:358
  208.1 0.1 pad_add_fusion.1.place_ref
  208.1 10.1 %all-to-all-done.8.everyone_ref = f32[32,24,128]{2,1,0:T(8,128)S(1)} async-done(((f32[32,24,128]{2,1,0:T(8,128)}), f32[32,24,128]{2,1,0:T(8,128)S(1)}, u32[]{:S(2)}, u32[]{:S(2)}) %all-to-all-start.8) | async-done | bytes 393248 | tf_op jit(solution)/shard_map/all_to_all | solution.py:358
  218.3 2.6 %shard_map.60 = f32[8,88,256]{2,1,0:T(8,128)S(1)} custom-call(s32[3]{0:T(128)S(1)} %pad_add_fusion.1.place_ref, s32[1]{0:T(128)} %bitcast.3.z_slot_ref.x_slot_ref, f32[32,24,128]{2,1,0:T(8,128)S(1)} %all-to-all-done.8.everyone_ref, f32[96,1024]{1,0:T(8,128)S(1)} %get-tuple-element.28.refs_0_, f32[96,1024]{1,0:T(8,128)S(1)} %get-tuple-element.29.refs_1_, ...), custom_call_target="tpu_custom_call" | custom-call | tf_op jit(solution)/shard_map/pallas_call | solution.py:473
  220.9 21.7 %all_to_all.53.in_ref = f32[8,88,256]{2,1,0:T(8,128)S(1)} all-to-all(f32[8,88,256]{2,1,0:T(8,128)S(1)} %shard_map.60), channel_id=1, replica_groups=mesh['feat'=4,'x'=4,'z'=8,'core'=2] {'feat','core'}, dimensions={0} | all-to-all | bytes 1441792 | tf_op jit(solution)/shard_map/all_to_all | solution.py:485
  242.6 1.2 shard_map.61
  (20 shorter events, 0.1 us)
Async XLA Ops:
  0.6 8.8 %copy-start.4 = (s32[256]{0:T(256)S(1)}, s32[256]{0:T(256)}, u32[]{:S(2)}) copy-start(s32[256]{0:T(256)} %param.4) | copy-start | bytes 3076
  6.1 21.2 %copy-start = (f32[256,1024]{1,0:T(8,128)}, f32[256,1024]{1,0:T(8,128)S(1)}, u32[]{:S(2)}) copy-start(f32[256,1024]{1,0:T(8,128)S(1)} %get-tuple-element.20.refs_0_.refs_10_) | copy-start | bytes 3145732
  6.1 100.1 %copy-start.1 = (f32[256,1024]{1,0:T(8,128)}, f32[256,1024]{1,0:T(8,128)S(1)}, u32[]{:S(2)}) copy-start(f32[256,1024]{1,0:T(8,128)S(1)} %get-tuple-element.24.refs_0_.refs_6_) | copy-start | bytes 3145732
  6.1 5.7 %collective-permute-start.1 = (f32[256,1024]{1,0:T(8,128)S(1)}, f32[256,1024]{1,0:T(8,128)}, u32[]{:S(2)}, u32[]{:S(2)}) collective-permute-start(f32[256,1024]{1,0:T(8,128)S(1)} %get-tuple-element.17.za_ref), channel_id=1, source_target_pairs={{0,1},{1,0},{2,3},{3,2},{4,5},{5,4},{6,7},{7,6},{8,9},{9,8},{10,11... | collective-permute-start | bytes 3145736 | tf_op jit(solution)/shard_map/ppermute | solution.py:35
  9.4 2.4 collective-permute-start
  15.1 50.8 %all-to-all-start = ((f32[32,88,128]{2,1,0:T(8,128)}), f32[32,88,128]{2,1,0:T(8,128)S(1)}, u32[]{:S(2)}, u32[]{:S(2)}) async-start(f32[32,88,128]{2,1,0:T(8,128)} %shard_map.51), calls=%async_computation | async-start | bytes 2883584 | tf_op jit(solution)/shard_map/all_to_all | solution.py:358
  24.4 24.7 %collective-permute-start.6 = (f32[256,1024]{1,0:T(8,128)S(1)}, f32[256,1024]{1,0:T(8,128)}, u32[]{:S(2)}, u32[]{:S(2)}) collective-permute-start(f32[256,1024]{1,0:T(8,128)S(1)} %get-tuple-element.20.refs_0_.refs_10_), channel_id=1, source_target_pairs={{0,192},{64,0},{128,64},{192,128},{1,193},{65,1},{129,65},{193,129... | collective-permute-start | bytes 3145736 | tf_op jit(solution)/shard_map/ppermute | solution.py:354
  27.3 26.5 %collective-permute-start.3 = (f32[256,1024]{1,0:T(8,128)S(1)}, f32[256,1024]{1,0:T(8,128)}, u32[]{:S(2)}, u32[]{:S(2)}) collective-permute-start(f32[256,1024]{1,0:T(8,128)S(1)} %get-tuple-element.20.refs_0_.refs_10_), channel_id=1, source_target_pairs={{0,64},{64,128},{128,192},{192,0},{1,65},{65,129},{129,193},{193,1... | collective-permute-start | bytes 3145736 | tf_op jit(solution)/shard_map/ppermute | solution.py:354
  27.3 57.5 %collective-permute-start.2 = (f32[256,1024]{1,0:T(8,128)S(1)}, f32[256,1024]{1,0:T(8,128)}, u32[]{:S(2)}, u32[]{:S(2)}) collective-permute-start(f32[256,1024]{1,0:T(8,128)S(1)} %get-tuple-element.20.refs_0_.refs_10_), channel_id=1, source_target_pairs={{0,1},{1,0},{2,3},{3,2},{4,5},{5,4},{6,7},{7,6},{8,9},{9,8},{10,11... | collective-permute-start | bytes 3145736 | tf_op jit(solution)/shard_map/ppermute | solution.py:35
  50.2 13.4 %collective-permute-start.7 = (f32[128,1024]{1,0:T(8,128)S(1)}, f32[128,1024]{1,0:T(8,128)}, u32[]{:S(2)}, u32[]{:S(2)}) collective-permute-start(f32[128,1024]{1,0:T(8,128)S(1)} %slice.17), channel_id=1, source_target_pairs={{0,192},{64,0},{128,64},{192,128},{1,193},{65,1},{129,65},{193,129... | collective-permute-start | bytes 1572872 | tf_op jit(solution)/shard_map/ppermute | solution.py:354
  55.7 30.3 %collective-permute-start.5 = (f32[128,1024]{1,0:T(8,128)}, f32[128,1024]{1,0:T(8,128)}, u32[]{:S(2)}, u32[]{:S(2)}) collective-permute-start(f32[128,1024]{1,0:T(8,128)} %slice.16), channel_id=1, source_target_pairs={{0,64},{64,128},{128,192},{192,0},{1,65},{65,129},{129,193},{193,1... | collective-permute-start | bytes 1572872 | tf_op jit(solution)/shard_map/ppermute | solution.py:354
  55.7 33.6 %collective-permute-start.10 = (f32[256,1024]{1,0:T(8,128)}, f32[256,1024]{1,0:T(8,128)}, u32[]{:S(2)}, u32[]{:S(2)}) collective-permute-start(f32[256,1024]{1,0:T(8,128)} %collective-permute-done.6.refs_8_.refs_18_), channel_id=1, source_target_pairs={{0,1},{1,0},{2,3},{3,2},{4,5},{5,4},{6,7},{7,6},{8,9},{9,8},{10,11... | collective-permute-start | bytes 3145736 | tf_op jit(solution)/shard_map/ppermute | solution.py:35
  63.6 23.0 %collective-permute-start.9 = (f32[128,1024]{1,0:T(8,128)}, f32[128,1024]{1,0:T(8,128)}, u32[]{:S(2)}, u32[]{:S(2)}) collective-permute-start(f32[128,1024]{1,0:T(8,128)} %collective-permute-done.7.refs_5_.refs_15_), channel_id=1, source_target_pairs={{0,1},{1,0},{2,3},{3,2},{4,5},{5,4},{6,7},{7,6},{8,9},{9,8},{10,11... | collective-permute-start | bytes 1572872 | tf_op jit(solution)/shard_map/ppermute | solution.py:35
  65.9 25.1 %collective-permute-start.4 = (f32[256,1024]{1,0:T(8,128)}, f32[256,1024]{1,0:T(8,128)}, u32[]{:S(2)}, u32[]{:S(2)}) collective-permute-start(f32[256,1024]{1,0:T(8,128)} %collective-permute-done.3.refs_2_.refs_12_), channel_id=1, source_target_pairs={{0,1},{1,0},{2,3},{3,2},{4,5},{5,4},{6,7},{7,6},{8,9},{9,8},{10,11... | collective-permute-start | bytes 3145736 | tf_op jit(solution)/shard_map/ppermute | solution.py:35
  75.8 19.5 %all-to-all-start.2 = ((f32[32,24,128]{2,1,0:T(8,128)}), f32[32,24,128]{2,1,0:T(8,128)S(1)}, u32[]{:S(2)}, u32[]{:S(2)}) async-start(f32[32,24,128]{2,1,0:T(8,128)} %shard_map.53), calls=%async_computation.2 | async-start | bytes 786432 | tf_op jit(solution)/shard_map/all_to_all | solution.py:358
  84.8 24.2 %collective-permute-start.15 = (f32[256,1024]{1,0:T(8,128)S(1)}, f32[256,1024]{1,0:T(8,128)}, u32[]{:S(2)}, u32[]{:S(2)}) collective-permute-start(f32[256,1024]{1,0:T(8,128)S(1)} %get-tuple-element.24.refs_0_.refs_6_), channel_id=1, source_target_pairs={{0,192},{64,0},{128,64},{192,128},{1,193},{65,1},{129,65},{193,129... | collective-permute-start | bytes 3145736 | tf_op jit(solution)/shard_map/ppermute | solution.py:354
  85.9 29.1 %collective-permute-start.12 = (f32[256,1024]{1,0:T(8,128)S(1)}, f32[256,1024]{1,0:T(8,128)}, u32[]{:S(2)}, u32[]{:S(2)}) collective-permute-start(f32[256,1024]{1,0:T(8,128)S(1)} %get-tuple-element.24.refs_0_.refs_6_), channel_id=1, source_target_pairs={{0,64},{64,128},{128,192},{192,0},{1,65},{65,129},{129,193},{193,1... | collective-permute-start | bytes 3145736 | tf_op jit(solution)/shard_map/ppermute | solution.py:354
  86.5 4.5 %collective-permute-start.8 = (f32[128,1024]{1,0:T(8,128)}, f32[128,1024]{1,0:T(8,128)S(1)}, u32[]{:S(2)}, u32[]{:S(2)}) collective-permute-start(f32[128,1024]{1,0:T(8,128)} %collective-permute-done.5.refs_4_.refs_14_), channel_id=1, source_target_pairs={{0,1},{1,0},{2,3},{3,2},{4,5},{5,4},{6,7},{7,6},{8,9},{9,8},{10,11... | collective-permute-start | bytes 1572872 | tf_op jit(solution)/shard_map/ppermute | solution.py:35
  91.0 4.3 %copy-start.2 = (f32[128,1024]{1,0:T(8,128)}, f32[128,1024]{1,0:T(8,128)S(1)}, u32[]{:S(2)}) copy-start(f32[128,1024]{1,0:T(8,128)S(1)} %collective-permute-done.8.refs_6_.refs_16_) | copy-start | bytes 1572868
  98.8 18.0 %all-to-all-start.3 = ((f32[32,24,128]{2,1,0:T(8,128)}), f32[32,24,128]{2,1,0:T(8,128)S(1)}, u32[]{:S(2)}, u32[]{:S(2)}) async-start(f32[32,24,128]{2,1,0:T(8,128)} %get-tuple-element.21), calls=%async_computation.3 | async-start | bytes 786432 | tf_op jit(solution)/shard_map/all_to_all | solution.py:358
  106.2 26.5 %collective-permute-start.11 = (f32[256,1024]{1,0:T(8,128)S(1)}, f32[256,1024]{1,0:T(8,128)}, u32[]{:S(2)}, u32[]{:S(2)}) collective-permute-start(f32[256,1024]{1,0:T(8,128)S(1)} %get-tuple-element.24.refs_0_.refs_6_), channel_id=1, source_target_pairs={{0,1},{1,0},{2,3},{3,2},{4,5},{5,4},{6,7},{7,6},{8,9},{9,8},{10,11... | collective-permute-start | bytes 3145736 | tf_op jit(solution)/shard_map/ppermute | solution.py:35
  110.9 16.0 %collective-permute-start.16 = (f32[128,1024]{1,0:T(8,128)}, f32[128,1024]{1,0:T(8,128)S(1)}, u32[]{:S(2)}, u32[]{:S(2)}) collective-permute-start(f32[128,1024]{1,0:T(8,128)} %slice.19), channel_id=1, source_target_pairs={{0,192},{64,0},{128,64},{192,128},{1,193},{65,1},{129,65},{193,129... | collective-permute-start | bytes 1572872 | tf_op jit(solution)/shard_map/ppermute | solution.py:354
  112.1 20.6 %collective-permute-start.19 = (f32[256,1024]{1,0:T(8,128)}, f32[256,1024]{1,0:T(8,128)}, u32[]{:S(2)}, u32[]{:S(2)}) collective-permute-start(f32[256,1024]{1,0:T(8,128)} %collective-permute-done.15.refs_8_.refs_14_), channel_id=1, source_target_pairs={{0,1},{1,0},{2,3},{3,2},{4,5},{5,4},{6,7},{7,6},{8,9},{9,8},{10,11... | collective-permute-start | bytes 3145736 | tf_op jit(solution)/shard_map/ppermute | solution.py:35
  116.9 15.0 %collective-permute-start.14 = (f32[128,1024]{1,0:T(8,128)}, f32[128,1024]{1,0:T(8,128)}, u32[]{:S(2)}, u32[]{:S(2)}) collective-permute-start(f32[128,1024]{1,0:T(8,128)} %slice.18), channel_id=1, source_target_pairs={{0,64},{64,128},{128,192},{192,0},{1,65},{65,129},{129,193},{193,1... | collective-permute-start | bytes 1572872 | tf_op jit(solution)/shard_map/ppermute | solution.py:354
  116.9 17.7 %collective-permute-start.13 = (f32[256,1024]{1,0:T(8,128)}, f32[256,1024]{1,0:T(8,128)}, u32[]{:S(2)}, u32[]{:S(2)}) collective-permute-start(f32[256,1024]{1,0:T(8,128)} %collective-permute-done.12.refs_2_.refs_8_), channel_id=1, source_target_pairs={{0,1},{1,0},{2,3},{3,2},{4,5},{5,4},{6,7},{7,6},{8,9},{9,8},{10,11... | collective-permute-start | bytes 3145736 | tf_op jit(solution)/shard_map/ppermute | solution.py:35
  117.7 21.0 %all-to-all-start.4 = ((f32[32,24,128]{2,1,0:T(8,128)}), f32[32,24,128]{2,1,0:T(8,128)S(1)}, u32[]{:S(2)}, u32[]{:S(2)}) async-start(f32[32,24,128]{2,1,0:T(8,128)} %shard_map.55), calls=%async_computation.4 | async-start | bytes 786432 | tf_op jit(solution)/shard_map/all_to_all | solution.py:358
  126.9 11.8 %copy-start.3 = (f32[128,1024]{1,0:T(8,128)}, f32[128,1024]{1,0:T(8,128)S(1)}, u32[]{:S(2)}) copy-start(f32[128,1024]{1,0:T(8,128)S(1)} %collective-permute-done.16.refs_5_.refs_11_) | copy-start | bytes 1572868
  126.9 5.8 %collective-permute-start.18 = (f32[128,1024]{1,0:T(8,128)S(1)}, f32[128,1024]{1,0:T(8,128)}, u32[]{:S(2)}, u32[]{:S(2)}) collective-permute-start(f32[128,1024]{1,0:T(8,128)S(1)} %collective-permute-done.16.refs_5_.refs_11_), channel_id=1, source_target_pairs={{0,1},{1,0},{2,3},{3,2},{4,5},{5,4},{6,7},{7,6},{8,9},{9,8},{10,11... | collective-permute-start | bytes 1572872 | tf_op jit(solution)/shard_map/ppermute | solution.py:35
  131.9 2.7 %collective-permute-start.17 = (f32[128,1024]{1,0:T(8,128)}, f32[128,1024]{1,0:T(8,128)}, u32[]{:S(2)}, u32[]{:S(2)}) collective-permute-start(f32[128,1024]{1,0:T(8,128)} %collective-permute-done.14.refs_4_.refs_10_), channel_id=1, source_target_pairs={{0,1},{1,0},{2,3},{3,2},{4,5},{5,4},{6,7},{7,6},{8,9},{9,8},{10,11... | collective-permute-start | bytes 1572872 | tf_op jit(solution)/shard_map/ppermute | solution.py:35
  161.0 18.3 %all-to-all-start.6 = ((f32[32,24,128]{2,1,0:T(8,128)}), f32[32,24,128]{2,1,0:T(8,128)S(1)}, u32[]{:S(2)}, u32[]{:S(2)}) async-start(f32[32,24,128]{2,1,0:T(8,128)} %shard_map.57), calls=%async_computation.6 | async-start | bytes 786432 | tf_op jit(solution)/shard_map/all_to_all | solution.py:358
  200.7 17.5 %all-to-all-start.8 = ((f32[32,24,128]{2,1,0:T(8,128)}), f32[32,24,128]{2,1,0:T(8,128)S(1)}, u32[]{:S(2)}, u32[]{:S(2)}) async-start(f32[32,24,128]{2,1,0:T(8,128)} %shard_map.59), calls=%async_computation.8 | async-start | bytes 786432 | tf_op jit(solution)/shard_map/all_to_all | solution.py:358

commit v7 on v6

--- a/solution.py
+++ b/solution.py
@@ -169,53 +169,56 @@
     return jnp.where(inside < share, group * share + inside, -1)
 
 
-def first_kernel(slices, groups, core_ref, lab_ref, za_ref, zb_ref, out_ref):
+def first_kernel(slices, groups, core_ref, lab_ref, za_ref, zb_ref, counts_ref, *out_refs):
     lab = lab_ref[...]
     width = C // slices
-    share = width // groups
-    planes = slices // 2
     group, low_label = label_parts(lab, slices, width)
     lane_row = lax.broadcasted_iota(jnp.int32, (LANES, lab.shape[1]), 0)
     low_hot = jnp.where(low_label == lane_row, 1.0, 0.0).astype(BF16)
     group_row = lax.broadcasted_iota(jnp.int32, (slices, lab.shape[1]), 0)
     group_hot = jnp.where(group == group_row, 1.0, 0.0).astype(BF16)
-    counts = dot_t(group_hot, low_hot)
-    chunk = planes * share
-    row = lax.broadcasted_iota(jnp.int32, (groups * chunk, 1), 0)
-    part = count_steps(row, chunk, groups)
-    rest = row - part * chunk
-    plane = count_steps(rest, share, planes)
-    wanted = (2 * plane + core_ref[0]) * width + part * share + (rest - plane * share)
+    counts_ref[...] = dot_t(group_hot, low_hot)
+    chunk = out_refs[0].shape[1]
+    padded = chunk * groups
+    planes = len(out_refs)
+    row = lax.broadcasted_iota(jnp.int32, (planes * padded, 1), 0)
+    plane = count_steps(row, padded, planes)
+    low = slice_class(row - plane * padded, groups, width // groups)
+    wanted = jnp.where(low >= 0, (2 * plane + core_ref[0]) * width + low, -1)
     onehot = jnp.where(wanted == lab, 1.0, 0.0).astype(BF16)
-    out_ref[:, chunk:, :] = jnp.broadcast_to(counts[None], (out_ref.shape[0], slices, LANES))
-    put_pieces(out_ref, partial_sum((za_ref, zb_ref), onehot), chunk)
-
-
-def first_middle_kernel(total_rows, share, core_ref, part_ref, in_ref, out_ref, totals_ref):
-    planes, _, _ = out_ref.shape
+    total = partial_sum((za_ref, zb_ref), onehot)
+    for g in range(planes):
+        put_pieces(out_refs[g], total[g * padded : (g + 1) * padded], chunk)
+
+
+def dealt_kernel(feat_ref, counts_ref, *refs):
+    dealt_refs, out_ref = refs[:-1], refs[-1]
+    chips, deep, _ = out_ref.shape
+    chunk = dealt_refs[0].shape[1]
+    for g, dealt_ref in enumerate(dealt_refs):
+
+        @pl.when(feat_ref[0] == g)
+        def _():
+            out_ref[:, :chunk, :] = dealt_ref[...]
+
+    out_ref[:, chunk:, :] = jnp.broadcast_to(counts_ref[...][None], (chips, deep - chunk, LANES))
+
+
+def first_middle_kernel(total_rows, share, slice_ref, part_ref, in_ref, copies_ref, totals_ref):
+    chunk = copies_ref.shape[1]
     summed = jnp.sum(in_ref[...], axis=0)
-    solved = summed[: planes * share]
-    totals = summed[planes * share :]
+    solved = summed[:chunk]
+    totals = summed[chunk:]
     totals_ref[...] = totals
     slice_row = lax.broadcasted_iota(jnp.int32, totals.shape, 0)
+    mine = jnp.sum(jnp.where(slice_row == slice_ref[0], totals, 0.0), axis=0, keepdims=True)
+    scale = jnp.where(mine > 0.0, total_rows / (C * jnp.maximum(mine, 1.0)), 0.0)
+    scale = scale.astype(BF16).astype(F32)
     row = lax.broadcasted_iota(jnp.int32, solved.shape, 0)
     lane = lax.broadcasted_iota(jnp.int32, solved.shape, 1)
-    plane = count_steps(row, share, planes)
-    counts = jnp.zeros(solved.shape, F32)
-    for g in range(planes):
-        mine = jnp.where(slice_row == 2 * g + core_ref[0], totals, 0.0)
-        counts = jnp.where(plane == g, jnp.sum(mine, axis=0, keepdims=True), counts)
-    here = part_ref[0] * share + (row - plane * share)
-    counts = jnp.sum(jnp.where(lane == here, counts, 0.0), axis=1, keepdims=True)
-    scale = jnp.where(counts > 0.0, total_rows / (C * jnp.maximum(counts, 1.0)), 0.0)
-    solved = solved * scale.astype(BF16).astype(F32)
-    out_ref[...] = jnp.zeros(out_ref.shape, F32)
-    for g in range(planes):
-        out_ref[g, :share, :] = solved[g * share : (g + 1) * share]
-
-
-def spread_kernel(in_ref, copies_ref):
-    copies_ref[...] = jnp.broadcast_to(in_ref[0][None], copies_ref.shape)
+    here = jnp.where(row < share, part_ref[0] * share + row, -1)
+    solved = solved * jnp.sum(jnp.where(lane == here, scale, 0.0), axis=1, keepdims=True)
+    copies_ref[...] = jnp.broadcast_to(solved[None], copies_ref.shape)
 
 
 def middle_kernel(in_ref, copies_ref):
@@ -358,10 +361,6 @@
     return lax.all_to_all(value, XZ, 0, 0, tiled=True)
 
 
-def deal(value):
-    return lax.all_to_all(value, "feat", 0, 0, tiled=True)
-
-
 def halves(value):
     middle_row = value.shape[0] // 2
     return value[:middle_row], value[middle_row:]
@@ -417,14 +416,22 @@
     late_all = gathered(late)
     block_shape = early.shape
 
-    first_chunk = blocks * share
-    pieces = pl.pallas_call(
+    counts, *dealt = pl.pallas_call(
         functools.partial(first_kernel, slices, groups),
         in_specs=[SMEM] + [VMEM] * 3,
-        out_specs=VMEM,
-        out_shape=held((chips, first_chunk + slices, LANES)),
+        out_specs=[VMEM] * (1 + blocks),
+        out_shape=[held((slices, LANES))] + [held((chips, chunk, LANES))] * blocks,
         compiler_params=room(16),
     )(core_index, lab, near(z_own), near(z_other))
+    for g in range(1, blocks):
+        dealt[g] = lax.ppermute(dealt[g], "feat", [(0, g)])
+    pieces = pl.pallas_call(
+        dealt_kernel,
+        in_specs=[SMEM] + [VMEM] * (1 + blocks),
+        out_specs=VMEM,
+        out_shape=held((chips, chunk + slices, LANES)),
+        compiler_params=room(8),
+    )(feat[None], *map(near, (counts, *dealt)))
 
     rows_shape = held((padded, both))
     solved_shape = held((padded, block_width))
@@ -435,15 +442,13 @@
     for b in range(blocks):
         arrived = exchange(pieces)
         if b == 0:
-            parts, totals = pl.pallas_call(
+            copies, totals = pl.pallas_call(
                 functools.partial(first_middle_kernel, total_rows, share),
                 in_specs=[SMEM, SMEM, VMEM],
                 out_specs=[VMEM] * 2,
-                out_shape=[held((blocks, chunk, LANES)), held((slices, LANES))],
-                compiler_params=room(12),
-            )(core_index, part_index, near(arrived))
-            parts = deal(parts)
-            copies = to_copies(spread_kernel, parts, (chips, chunk, LANES))
+                out_shape=[held((chips, chunk, LANES)), held((slices, LANES))],
+                compiler_params=room(8),
+            )(slice_index, part_index, near(arrived))
         else:
             copies = to_copies(middle_kernel, arrived, (chips, chunk, LANES))
         everyone = exchange(copies)

time: 245 us -> 244 us (level)
  blocking collectives: 66.5 us -> 57.5 us
  waiting for transfers between devices: 66 us -> 70.8 us
  starting transfers between devices: 78 us -> 81.8 us
    ppermute x0 -> x3, waiting for transfers between devices: none -> 21.9 us  [local(): dealt[g] = lax.ppermute(dealt[g], 'feat', [(0, g)])]
    ppermute x8, waiting for transfers between devices: 31.1 us -> 14.4 us  [shifted(): lax.ppermute(value, 'feat', [(i, (i + by) % count) for i in range(count)])]
    all_to_all x1 -> x0, blocking collectives: 8.98 us -> none  [deal(): return lax.all_to_all(value, 'feat', 0, 0, tiled=True)]
    ppermute x12, starting transfers between devices: 18.7 us -> 12.3 us  [swap_cores(): return lax.ppermute(value, 'core', [(0, 1), (1, 0)])]
    ppermute x0 -> x3, starting transfers between devices: none -> 5.14 us  [local(): dealt[g] = lax.ppermute(dealt[g], 'feat', [(0, g)])]
    ppermute x8, starting transfers between devices: 9.31 us -> 11.9 us  [shifted(): lax.ppermute(value, 'feat', [(i, (i + by) % count) for i in range(count)])]
    all_to_all x6, starting transfers between devices: 50 us -> 52.4 us  [exchange(): return lax.all_to_all(value, XZ, 0, 0, tiled=True)]
  transfers between devices with their start and end apart: 26 -> 29, of which waited for: 10 -> 13; matrix products, arithmetic and copies ran while one was open for 3% -> 3% of each run, Pallas kernels for 2% -> 3%
where the time goes in v7:
time: 244 us; the launch traced here: 243 us
  starting transfers between devices  81.8 us (34%)
  waiting for transfers between devices  70.8 us (29%)
  blocking collectives  57.5 us (24%)
  Pallas kernels  25.5 us (10%)
  local copies, waits for them, and re-layouts  6.79 us (3%)
    all_to_all x6, starting transfers between devices, exchange(): return lax.all_to_all(value, XZ, 0, 0, tiled=True)  52.4 us
    all_to_all x2, blocking collectives, exchange(): return lax.all_to_all(value, XZ, 0, 0, tiled=True)  35.8 us
    all_to_all x6, waiting for transfers between devices, exchange(): return lax.all_to_all(value, XZ, 0, 0, tiled=True)  29.8 us
    ppermute x3, waiting for transfers between devices, local(): dealt[g] = lax.ppermute(dealt[g], 'feat', [(0, g)])  21.9 us
    all_to_all x1, blocking collectives, local(): got = near(lax.all_to_all(sends, ('feat', 'core'), 0, 0, tiled=True))  21.7 us
    ppermute x8, waiting for transfers between devices, shifted(): lax.ppermute(value, 'feat', [(i, (i + by) % count) for i in range(count)])  14.4 us
    ppermute x12, starting transfers between devices, swap_cores(): return lax.ppermute(value, 'core', [(0, 1), (1, 0)])  12.3 us
    ppermute x8, starting transfers between devices, shifted(): lax.ppermute(value, 'feat', [(i, (i + by) % count) for i in range(count)])  11.9 us
  transfers between devices with their start and end apart: 29, of which 13 were waited for; matrix products, arithmetic and copies ran while one was open for 3% of the time, Pallas kernels for 3%

profile of v7, /device:TPU:1, one launch (start us, length us, event | category | flops | bytes accessed | tf_op | source)
XLA Modules:
  0.0 243.3 jit_solution(2439314326184662553)
XLA Ops:
  0.6 5.4 %shard_map.50 = (f32[256,1024]{1,0:T(8,128)S(1)}, f32[256,1024]{1,0:T(8,128)S(1)}, f32[256,1024]{1,0:T(8,128)S(1)}) custom-call(s32[1]{0:T(128)} %bitcast.10.feat_ref, f32[1,1024,1024]{2,1,0:T(8,128)} %gram_ref.1, bf16[256,1024]{1,0:T(8,128)(2,1)} %x_ref.1), custom_call_target="tpu_custom_call" | custom-call | tf_op jit(solution)/shard_map/pallas_call | solution.py:66
  6.1 3.3 %collective-permute-start.1 = (f32[256,1024]{1,0:T(8,128)S(1)}, f32[256,1024]{1,0:T(8,128)}, u32[]{:S(2)}, u32[]{:S(2)}) collective-permute-start(f32[256,1024]{1,0:T(8,128)S(1)} %get-tuple-element.22.za_ref), channel_id=1, source_target_pairs={{0,1},{1,0},{2,3},{3,2},{4,5},{5,4},{6,7},{7,6},{8,9},{9,8},{10,11... | collective-permute-start | bytes 3145736 | tf_op jit(solution)/shard_map/ppermute | solution.py:35
  9.4 1.0 collective-permute-start.9
  10.4 0.4 collective-permute-start
  10.8 1.0 collective-permute-done
  11.8 0.0 collective-permute-done.1.zb_ref
  11.8 2.3 shard_map.51
  14.1 2.2 collective-permute-start.2
  16.3 1.7 collective-permute-start.3
  17.9 1.3 collective-permute-start.4
  19.2 0.1 collective-permute-start.6
  19.3 5.0 %collective-permute-done.2.refs_1_ = f32[32,24,128]{2,1,0:T(8,128)S(1)} collective-permute-done((f32[32,24,128]{2,1,0:T(8,128)S(1)}, f32[32,24,128]{2,1,0:T(8,128)S(1)}, u32[]{:S(2)}, u32[]{:S(2)}) %collective-permute-start.2) | collective-permute-done | bytes 393248 | tf_op jit(solution)/shard_map/ppermute | solution.py:427
  24.4 8.5 %collective-permute-done.3.refs_2_ = f32[32,24,128]{2,1,0:T(8,128)S(1)} collective-permute-done((f32[32,24,128]{2,1,0:T(8,128)S(1)}, f32[32,24,128]{2,1,0:T(8,128)S(1)}, u32[]{:S(2)}, u32[]{:S(2)}) %collective-permute-start.3) | collective-permute-done | bytes 393248 | tf_op jit(solution)/shard_map/ppermute | solution.py:427
  32.8 8.4 %collective-permute-done.4.refs_3_ = f32[32,24,128]{2,1,0:T(8,128)S(1)} collective-permute-done((f32[32,24,128]{2,1,0:T(8,128)S(1)}, f32[32,24,128]{2,1,0:T(8,128)S(1)}, u32[]{:S(2)}, u32[]{:S(2)}) %collective-permute-start.4) | collective-permute-done | bytes 393248 | tf_op jit(solution)/shard_map/ppermute | solution.py:427
  41.3 0.9 shard_map.52
  42.1 11.0 %all-to-all-start = ((f32[32,32,128]{2,1,0:T(8,128)}), f32[32,32,128]{2,1,0:T(8,128)S(1)}, u32[]{:S(2)}, u32[]{:S(2)}) async-start(f32[32,32,128]{2,1,0:T(8,128)} %shard_map.52), calls=%async_computation | async-start | bytes 1048576 | tf_op jit(solution)/shard_map/all_to_all | solution.py:361
  53.2 1.3 collective-permute-start.5
  54.5 1.1 slice.17
  55.6 3.5 %collective-permute-start.10 = (f32[128,1024]{1,0:T(8,128)S(1)}, f32[128,1024]{1,0:T(8,128)}, u32[]{:S(2)}, u32[]{:S(2)}) collective-permute-start(f32[128,1024]{1,0:T(8,128)S(1)} %slice.17), channel_id=1, source_target_pairs={{0,192},{64,0},{128,64},{192,128},{1,193},{65,1},{129,65},{193,129... | collective-permute-start | bytes 1572872 | tf_op jit(solution)/shard_map/ppermute | solution.py:357
  59.0 0.0 collective-permute-done.6.refs_2_.refs_12_
  59.0 1.9 slice.16
  60.9 0.3 collective-permute-start.13
  61.2 9.1 %collective-permute-done.10.refs_5_.refs_15_ = f32[128,1024]{1,0:T(8,128)} collective-permute-done((f32[128,1024]{1,0:T(8,128)S(1)}, f32[128,1024]{1,0:T(8,128)}, u32[]{:S(2)}, u32[]{:S(2)}) %collective-permute-start.10) | collective-permute-done | bytes 524320 | tf_op jit(solution)/shard_map/ppermute | solution.py:357
  70.3 0.9 collective-permute-start.12
  71.2 0.0 collective-permute-start.7
  71.2 0.0 all-to-all-done.in_ref
  71.2 0.9 shard_map.53
  72.1 9.5 %all-to-all-start.1 = ((f32[32,24,128]{2,1,0:T(8,128)}), f32[32,24,128]{2,1,0:T(8,128)S(1)}, u32[]{:S(2)}, u32[]{:S(2)}) async-start(f32[32,24,128]{2,1,0:T(8,128)} %get-tuple-element.29), calls=%async_computation.1 | async-start | bytes 786432 | tf_op jit(solution)/shard_map/all_to_all | solution.py:361
  81.6 0.0 collective-permute-done.5.refs_1_.refs_11_
  81.6 3.8 %collective-permute-start.18 = (f32[256,1024]{1,0:T(8,128)S(1)}, f32[256,1024]{1,0:T(8,128)}, u32[]{:S(2)}, u32[]{:S(2)}) collective-permute-start(f32[256,1024]{1,0:T(8,128)S(1)} %get-tuple-element.34.refs_0_.refs_6_), channel_id=1, source_target_pairs={{0,192},{64,0},{128,64},{192,128},{1,193},{65,1},{129,65},{193,129... | collective-permute-start | bytes 3145736 | tf_op jit(solution)/shard_map/ppermute | solution.py:357
  85.4 1.2 collective-permute-start.11
  86.5 1.7 collective-permute-done.11.refs_6_.refs_16_
  88.3 5.1 %all-to-all-done.1.everyone_ref = f32[32,24,128]{2,1,0:T(8,128)S(1)} async-done(((f32[32,24,128]{2,1,0:T(8,128)}), f32[32,24,128]{2,1,0:T(8,128)S(1)}, u32[]{:S(2)}, u32[]{:S(2)}) %all-to-all-start.1) | async-done | bytes 393248 | tf_op jit(solution)/shard_map/all_to_all | solution.py:361
  93.4 3.5 %shard_map.54 = (f32[96,1024]{1,0:T(8,128)S(1)}, f32[96,512]{1,0:T(8,128)S(1)}, f32[8,512]{1,0:T(8,128)S(1)}, f32[32,24,128]{2,1,0:T(8,128)}) custom-call(s32[1]{0:T(128)} %bitcast.6.slice_ref, s32[1]{0:T(128)} %bitcast.7.x_slot_ref, s32[1]{0:T(128)} %bitcast.5.z_slot_ref.x_slot_ref, s32[1,512]{1,0:T(1,128)S(1)} %bitcast.12, ...), custom_call_target="tpu_custom_call" | custom-call | tf_op jit(solution)/shard_map/pallas_call | solution.py:457
  96.9 7.6 %all-to-all-start.2 = ((f32[32,24,128]{2,1,0:T(8,128)}), f32[32,24,128]{2,1,0:T(8,128)S(1)}, u32[]{:S(2)}, u32[]{:S(2)}) async-start(f32[32,24,128]{2,1,0:T(8,128)} %get-tuple-element.31), calls=%async_computation.2 | async-start | bytes 786432 | tf_op jit(solution)/shard_map/all_to_all | solution.py:361
  104.5 1.3 collective-permute-start.14
  105.8 1.3 collective-permute-done.18.refs_8_.refs_14_
  107.1 1.9 slice.19
  109.0 3.5 %collective-permute-start.19 = (f32[128,1024]{1,0:T(8,128)}, f32[128,1024]{1,0:T(8,128)S(1)}, u32[]{:S(2)}, u32[]{:S(2)}) collective-permute-start(f32[128,1024]{1,0:T(8,128)} %slice.19), channel_id=1, source_target_pairs={{0,192},{64,0},{128,64},{192,128},{1,193},{65,1},{129,65},{193,129... | collective-permute-start | bytes 1572872 | tf_op jit(solution)/shard_map/ppermute | solution.py:357
  112.5 1.9 collective-permute-start.22
  114.5 1.9 slice.18
  116.4 0.0 collective-permute-start.17
  116.4 0.0 collective-permute-start.16
  116.4 0.8 shard_map.55
  117.2 9.2 %all-to-all-start.3 = ((f32[32,24,128]{2,1,0:T(8,128)}), f32[32,24,128]{2,1,0:T(8,128)S(1)}, u32[]{:S(2)}, u32[]{:S(2)}) async-start(f32[32,24,128]{2,1,0:T(8,128)} %shard_map.55), calls=%async_computation.3 | async-start | bytes 786432 | tf_op jit(solution)/shard_map/all_to_all | solution.py:361
  126.4 0.9 collective-permute-start.21
  127.3 4.1 %collective-permute-done.17.refs_4_.refs_10_ = f32[128,1024]{1,0:T(8,128)} collective-permute-done((f32[128,1024]{1,0:T(8,128)}, f32[128,1024]{1,0:T(8,128)}, u32[]{:S(2)}, u32[]{:S(2)}) %collective-permute-start.17) | collective-permute-done | bytes 524320 | tf_op jit(solution)/shard_map/ppermute | solution.py:357
  131.4 0.9 collective-permute-start.20
  132.2 1.9 collective-permute-done.20.refs_6_.refs_12_
  134.1 4.1 %all-to-all-done.3.everyone_ref = f32[32,24,128]{2,1,0:T(8,128)S(1)} async-done(((f32[32,24,128]{2,1,0:T(8,128)}), f32[32,24,128]{2,1,0:T(8,128)S(1)}, u32[]{:S(2)}, u32[]{:S(2)}) %all-to-all-start.3) | async-done | bytes 393248 | tf_op jit(solution)/shard_map/all_to_all | solution.py:361
  138.2 3.2 %shard_map.56 = (f32[96,1024]{1,0:T(8,128)S(1)}, f32[96,512]{1,0:T(8,128)S(1)}, f32[32,24,128]{2,1,0:T(8,128)S(1)}) custom-call(s32[1]{0:T(128)} %bitcast.5.z_slot_ref.x_slot_ref, s32[1]{0:T(128)} %bitcast.4.z_slot_ref.x_slot_ref, f32[32,24,128]{2,1,0:T(8,128)S(1)} %all-to-all-done.3.everyone_ref, f32[96,512]{1,0:T(8,128)S(1)} %get-tuple-element.32.old_ref.refs_3_, ...), custom_call_target="tpu_custom_call" | custom-call | tf_op jit(solution)/shard_map/pallas_call | solution.py:467
  141.4 18.4 %all_to_all.45.in_ref = f32[32,24,128]{2,1,0:T(8,128)S(1)} all-to-all(f32[32,24,128]{2,1,0:T(8,128)S(1)} %get-tuple-element.35), channel_id=1, replica_groups=mesh['feat'=4,'x'=4,'z'=8,'core'=2] {'x','z'}, dimensions={0} | all-to-all | bytes 786432 | tf_op jit(solution)/shard_map/all_to_all | solution.py:361
  159.7 0.8 shard_map.57
  160.5 7.8 %all-to-all-start.5 = ((f32[32,24,128]{2,1,0:T(8,128)}), f32[32,24,128]{2,1,0:T(8,128)S(1)}, u32[]{:S(2)}, u32[]{:S(2)}) async-start(f32[32,24,128]{2,1,0:T(8,128)} %shard_map.57), calls=%async_computation.5 | async-start | bytes 786432 | tf_op jit(solution)/shard_map/all_to_all | solution.py:361
  168.3 10.5 %all-to-all-done.5.everyone_ref = f32[32,24,128]{2,1,0:T(8,128)S(1)} async-done(((f32[32,24,128]{2,1,0:T(8,128)}), f32[32,24,128]{2,1,0:T(8,128)S(1)}, u32[]{:S(2)}, u32[]{:S(2)}) %all-to-all-start.5) | async-done | bytes 393248 | tf_op jit(solution)/shard_map/all_to_all | solution.py:361
  178.8 3.1 %shard_map.58 = (f32[96,1024]{1,0:T(8,128)S(1)}, f32[96,512]{1,0:T(8,128)S(1)}, f32[32,24,128]{2,1,0:T(8,128)S(1)}) custom-call(s32[1]{0:T(128)} %bitcast.4.z_slot_ref.x_slot_ref, s32[1]{0:T(128)} %bitcast.3.z_slot_ref.x_slot_ref, f32[32,24,128]{2,1,0:T(8,128)S(1)} %all-to-all-done.5.everyone_ref, f32[96,512]{1,0:T(8,128)S(1)} %get-tuple-element.36.old_ref.refs_4_, ...), custom_call_target="tpu_custom_call" | custom-call | tf_op jit(solution)/shard_map/pallas_call | solution.py:467
  182.0 17.5 %all_to_all.46.in_ref = f32[32,24,128]{2,1,0:T(8,128)S(1)} all-to-all(f32[32,24,128]{2,1,0:T(8,128)S(1)} %get-tuple-element.37), channel_id=1, replica_groups=mesh['feat'=4,'x'=4,'z'=8,'core'=2] {'x','z'}, dimensions={0} | all-to-all | bytes 786432 | tf_op jit(solution)/shard_map/all_to_all | solution.py:361
  199.4 0.8 shard_map.59
  200.2 7.3 %all-to-all-start.7 = ((f32[32,24,128]{2,1,0:T(8,128)}), f32[32,24,128]{2,1,0:T(8,128)S(1)}, u32[]{:S(2)}, u32[]{:S(2)}) async-start(f32[32,24,128]{2,1,0:T(8,128)} %shard_map.59), calls=%async_computation.7 | async-start | bytes 786432 | tf_op jit(solution)/shard_map/all_to_all | solution.py:361
  207.6 0.1 pad_add_fusion.1.place_ref
  207.6 10.1 %all-to-all-done.7.everyone_ref = f32[32,24,128]{2,1,0:T(8,128)S(1)} async-done(((f32[32,24,128]{2,1,0:T(8,128)}), f32[32,24,128]{2,1,0:T(8,128)S(1)}, u32[]{:S(2)}, u32[]{:S(2)}) %all-to-all-start.7) | async-done | bytes 393248 | tf_op jit(solution)/shard_map/all_to_all | solution.py:361
  217.8 2.6 %shard_map.60 = f32[8,88,256]{2,1,0:T(8,128)S(1)} custom-call(s32[3]{0:T(128)S(1)} %pad_add_fusion.1.place_ref, s32[1]{0:T(128)} %bitcast.3.z_slot_ref.x_slot_ref, f32[32,24,128]{2,1,0:T(8,128)S(1)} %all-to-all-done.7.everyone_ref, f32[96,1024]{1,0:T(8,128)S(1)} %get-tuple-element.38.refs_0_, f32[96,1024]{1,0:T(8,128)S(1)} %get-tuple-element.39.refs_1_, ...), custom_call_target="tpu_custom_call" | custom-call | tf_op jit(solution)/shard_map/pallas_call | solution.py:478
  220.4 21.7 %all_to_all.47.in_ref = f32[8,88,256]{2,1,0:T(8,128)S(1)} all-to-all(f32[8,88,256]{2,1,0:T(8,128)S(1)} %shard_map.60), channel_id=1, replica_groups=mesh['feat'=4,'x'=4,'z'=8,'core'=2] {'feat','core'}, dimensions={0} | all-to-all | bytes 1441792 | tf_op jit(solution)/shard_map/all_to_all | solution.py:490
  242.1 1.2 shard_map.61
  (25 shorter events, 0.1 us)
Async XLA Ops:
  0.6 9.8 %copy-start.4 = (s32[256]{0:T(256)S(1)}, s32[256]{0:T(256)}, u32[]{:S(2)}) copy-start(s32[256]{0:T(256)} %param.4) | copy-start | bytes 3076
  6.1 66.0 %copy-start = (f32[256,1024]{1,0:T(8,128)}, f32[256,1024]{1,0:T(8,128)S(1)}, u32[]{:S(2)}) copy-start(f32[256,1024]{1,0:T(8,128)S(1)} %get-tuple-element.30.refs_0_.refs_10_) | copy-start | bytes 3145732
  6.1 98.4 %copy-start.1 = (f32[256,1024]{1,0:T(8,128)}, f32[256,1024]{1,0:T(8,128)S(1)}, u32[]{:S(2)}) copy-start(f32[256,1024]{1,0:T(8,128)S(1)} %get-tuple-element.34.refs_0_.refs_6_) | copy-start | bytes 3145732
  6.1 5.7 %collective-permute-start.1 = (f32[256,1024]{1,0:T(8,128)S(1)}, f32[256,1024]{1,0:T(8,128)}, u32[]{:S(2)}, u32[]{:S(2)}) collective-permute-start(f32[256,1024]{1,0:T(8,128)S(1)} %get-tuple-element.22.za_ref), channel_id=1, source_target_pairs={{0,1},{1,0},{2,3},{3,2},{4,5},{5,4},{6,7},{7,6},{8,9},{9,8},{10,11... | collective-permute-start | bytes 3145736 | tf_op jit(solution)/shard_map/ppermute | solution.py:35
  9.4 45.1 %collective-permute-start.9 = (f32[256,1024]{1,0:T(8,128)S(1)}, f32[256,1024]{1,0:T(8,128)}, u32[]{:S(2)}, u32[]{:S(2)}) collective-permute-start(f32[256,1024]{1,0:T(8,128)S(1)} %get-tuple-element.30.refs_0_.refs_10_), channel_id=1, source_target_pairs={{0,192},{64,0},{128,64},{192,128},{1,193},{65,1},{129,65},{193,129... | collective-permute-start | bytes 3145736 | tf_op jit(solution)/shard_map/ppermute | solution.py:357
  10.4 1.4 collective-permute-start
  14.1 10.3 %collective-permute-start.2 = (f32[32,24,128]{2,1,0:T(8,128)S(1)}, f32[32,24,128]{2,1,0:T(8,128)S(1)}, u32[]{:S(2)}, u32[]{:S(2)}) collective-permute-start(f32[32,24,128]{2,1,0:T(8,128)S(1)} %get-tuple-element.25), channel_id=1, source_target_pairs={{0,64},{1,65},{2,66},{3,67},{4,68},{5,69},{6,70},{7,71},{8,72},{9,... | collective-permute-start | bytes 1179656 | tf_op jit(solution)/shard_map/ppermute | solution.py:427
  16.3 16.6 %collective-permute-start.3 = (f32[32,24,128]{2,1,0:T(8,128)S(1)}, f32[32,24,128]{2,1,0:T(8,128)S(1)}, u32[]{:S(2)}, u32[]{:S(2)}) collective-permute-start(f32[32,24,128]{2,1,0:T(8,128)S(1)} %get-tuple-element.26), channel_id=1, source_target_pairs={{0,128},{1,129},{2,130},{3,131},{4,132},{5,133},{6,134},{7,135},{8... | collective-permute-start | bytes 1179656 | tf_op jit(solution)/shard_map/ppermute | solution.py:427
  17.9 23.3 %collective-permute-start.4 = (f32[32,24,128]{2,1,0:T(8,128)S(1)}, f32[32,24,128]{2,1,0:T(8,128)S(1)}, u32[]{:S(2)}, u32[]{:S(2)}) collective-permute-start(f32[32,24,128]{2,1,0:T(8,128)S(1)} %get-tuple-element.27), channel_id=1, source_target_pairs={{0,192},{1,193},{2,194},{3,195},{4,196},{5,197},{6,198},{7,199},{8... | collective-permute-start | bytes 1179656 | tf_op jit(solution)/shard_map/ppermute | solution.py:427
  19.2 39.8 %collective-permute-start.6 = (f32[256,1024]{1,0:T(8,128)S(1)}, f32[256,1024]{1,0:T(8,128)}, u32[]{:S(2)}, u32[]{:S(2)}) collective-permute-start(f32[256,1024]{1,0:T(8,128)S(1)} %get-tuple-element.30.refs_0_.refs_10_), channel_id=1, source_target_pairs={{0,64},{64,128},{128,192},{192,0},{1,65},{65,129},{129,193},{193,1... | collective-permute-start | bytes 3145736 | tf_op jit(solution)/shard_map/ppermute | solution.py:357
  42.1 29.1 %all-to-all-start = ((f32[32,32,128]{2,1,0:T(8,128)}), f32[32,32,128]{2,1,0:T(8,128)S(1)}, u32[]{:S(2)}, u32[]{:S(2)}) async-start(f32[32,32,128]{2,1,0:T(8,128)} %shard_map.52), calls=%async_computation | async-start | bytes 1048576 | tf_op jit(solution)/shard_map/all_to_all | solution.py:361
  53.2 28.4 %collective-permute-start.5 = (f32[256,1024]{1,0:T(8,128)S(1)}, f32[256,1024]{1,0:T(8,128)}, u32[]{:S(2)}, u32[]{:S(2)}) collective-permute-start(f32[256,1024]{1,0:T(8,128)S(1)} %get-tuple-element.30.refs_0_.refs_10_), channel_id=1, source_target_pairs={{0,1},{1,0},{2,3},{3,2},{4,5},{5,4},{6,7},{7,6},{8,9},{9,8},{10,11... | collective-permute-start | bytes 3145736 | tf_op jit(solution)/shard_map/ppermute | solution.py:35
  55.6 14.7 %collective-permute-start.10 = (f32[128,1024]{1,0:T(8,128)S(1)}, f32[128,1024]{1,0:T(8,128)}, u32[]{:S(2)}, u32[]{:S(2)}) collective-permute-start(f32[128,1024]{1,0:T(8,128)S(1)} %slice.17), channel_id=1, source_target_pairs={{0,192},{64,0},{128,64},{192,128},{1,193},{65,1},{129,65},{193,129... | collective-permute-start | bytes 1572872 | tf_op jit(solution)/shard_map/ppermute | solution.py:357
  60.9 24.5 %collective-permute-start.8 = (f32[128,1024]{1,0:T(8,128)}, f32[128,1024]{1,0:T(8,128)}, u32[]{:S(2)}, u32[]{:S(2)}) collective-permute-start(f32[128,1024]{1,0:T(8,128)} %slice.16), channel_id=1, source_target_pairs={{0,64},{64,128},{128,192},{192,0},{1,65},{65,129},{129,193},{193,1... | collective-permute-start | bytes 1572872 | tf_op jit(solution)/shard_map/ppermute | solution.py:357
  60.9 25.6 %collective-permute-start.13 = (f32[256,1024]{1,0:T(8,128)}, f32[256,1024]{1,0:T(8,128)}, u32[]{:S(2)}, u32[]{:S(2)}) collective-permute-start(f32[256,1024]{1,0:T(8,128)} %collective-permute-done.9.refs_8_.refs_18_), channel_id=1, source_target_pairs={{0,1},{1,0},{2,3},{3,2},{4,5},{5,4},{6,7},{7,6},{8,9},{9,8},{10,11... | collective-permute-start | bytes 3145736 | tf_op jit(solution)/shard_map/ppermute | solution.py:35
  70.3 15.1 %collective-permute-start.12 = (f32[128,1024]{1,0:T(8,128)}, f32[128,1024]{1,0:T(8,128)}, u32[]{:S(2)}, u32[]{:S(2)}) collective-permute-start(f32[128,1024]{1,0:T(8,128)} %collective-permute-done.10.refs_5_.refs_15_), channel_id=1, source_target_pairs={{0,1},{1,0},{2,3},{3,2},{4,5},{5,4},{6,7},{7,6},{8,9},{9,8},{10,11... | collective-permute-start | bytes 1572872 | tf_op jit(solution)/shard_map/ppermute | solution.py:35
  71.2 17.1 %collective-permute-start.7 = (f32[256,1024]{1,0:T(8,128)}, f32[256,1024]{1,0:T(8,128)}, u32[]{:S(2)}, u32[]{:S(2)}) collective-permute-start(f32[256,1024]{1,0:T(8,128)} %collective-permute-done.6.refs_2_.refs_12_), channel_id=1, source_target_pairs={{0,1},{1,0},{2,3},{3,2},{4,5},{5,4},{6,7},{7,6},{8,9},{9,8},{10,11... | collective-permute-start | bytes 3145736 | tf_op jit(solution)/shard_map/ppermute | solution.py:35
  72.1 21.3 %all-to-all-start.1 = ((f32[32,24,128]{2,1,0:T(8,128)}), f32[32,24,128]{2,1,0:T(8,128)S(1)}, u32[]{:S(2)}, u32[]{:S(2)}) async-start(f32[32,24,128]{2,1,0:T(8,128)} %get-tuple-element.29), calls=%async_computation.1 | async-start | bytes 786432 | tf_op jit(solution)/shard_map/all_to_all | solution.py:361
  81.6 25.5 %collective-permute-start.18 = (f32[256,1024]{1,0:T(8,128)S(1)}, f32[256,1024]{1,0:T(8,128)}, u32[]{:S(2)}, u32[]{:S(2)}) collective-permute-start(f32[256,1024]{1,0:T(8,128)S(1)} %get-tuple-element.34.refs_0_.refs_6_), channel_id=1, source_target_pairs={{0,192},{64,0},{128,64},{192,128},{1,193},{65,1},{129,65},{193,129... | collective-permute-start | bytes 3145736 | tf_op jit(solution)/shard_map/ppermute | solution.py:357
  85.4 29.1 %collective-permute-start.15 = (f32[256,1024]{1,0:T(8,128)S(1)}, f32[256,1024]{1,0:T(8,128)}, u32[]{:S(2)}, u32[]{:S(2)}) collective-permute-start(f32[256,1024]{1,0:T(8,128)S(1)} %get-tuple-element.34.refs_0_.refs_6_), channel_id=1, source_target_pairs={{0,64},{64,128},{128,192},{192,0},{1,65},{65,129},{129,193},{193,1... | collective-permute-start | bytes 3145736 | tf_op jit(solution)/shard_map/ppermute | solution.py:357
  85.4 2.9 %collective-permute-start.11 = (f32[128,1024]{1,0:T(8,128)}, f32[128,1024]{1,0:T(8,128)S(1)}, u32[]{:S(2)}, u32[]{:S(2)}) collective-permute-start(f32[128,1024]{1,0:T(8,128)} %collective-permute-done.8.refs_4_.refs_14_), channel_id=1, source_target_pairs={{0,1},{1,0},{2,3},{3,2},{4,5},{5,4},{6,7},{7,6},{8,9},{9,8},{10,11... | collective-permute-start | bytes 1572872 | tf_op jit(solution)/shard_map/ppermute | solution.py:35
  88.3 5.1 %copy-start.2 = (f32[128,1024]{1,0:T(8,128)}, f32[128,1024]{1,0:T(8,128)S(1)}, u32[]{:S(2)}) copy-start(f32[128,1024]{1,0:T(8,128)S(1)} %collective-permute-done.11.refs_6_.refs_16_) | copy-start | bytes 1572868
  96.9 19.5 %all-to-all-start.2 = ((f32[32,24,128]{2,1,0:T(8,128)}), f32[32,24,128]{2,1,0:T(8,128)S(1)}, u32[]{:S(2)}, u32[]{:S(2)}) async-start(f32[32,24,128]{2,1,0:T(8,128)} %get-tuple-element.31), calls=%async_computation.2 | async-start | bytes 786432 | tf_op jit(solution)/shard_map/all_to_all | solution.py:361
  104.5 27.7 %collective-permute-start.14 = (f32[256,1024]{1,0:T(8,128)S(1)}, f32[256,1024]{1,0:T(8,128)}, u32[]{:S(2)}, u32[]{:S(2)}) collective-permute-start(f32[256,1024]{1,0:T(8,128)S(1)} %get-tuple-element.34.refs_0_.refs_6_), channel_id=1, source_target_pairs={{0,1},{1,0},{2,3},{3,2},{4,5},{5,4},{6,7},{7,6},{8,9},{9,8},{10,11... | collective-permute-start | bytes 3145736 | tf_op jit(solution)/shard_map/ppermute | solution.py:35
  109.0 17.4 %collective-permute-start.19 = (f32[128,1024]{1,0:T(8,128)}, f32[128,1024]{1,0:T(8,128)S(1)}, u32[]{:S(2)}, u32[]{:S(2)}) collective-permute-start(f32[128,1024]{1,0:T(8,128)} %slice.19), channel_id=1, source_target_pairs={{0,192},{64,0},{128,64},{192,128},{1,193},{65,1},{129,65},{193,129... | collective-permute-start | bytes 1572872 | tf_op jit(solution)/shard_map/ppermute | solution.py:357
  112.5 19.7 %collective-permute-start.22 = (f32[256,1024]{1,0:T(8,128)}, f32[256,1024]{1,0:T(8,128)}, u32[]{:S(2)}, u32[]{:S(2)}) collective-permute-start(f32[256,1024]{1,0:T(8,128)} %collective-permute-done.18.refs_8_.refs_14_), channel_id=1, source_target_pairs={{0,1},{1,0},{2,3},{3,2},{4,5},{5,4},{6,7},{7,6},{8,9},{9,8},{10,11... | collective-permute-start | bytes 3145736 | tf_op jit(solution)/shard_map/ppermute | solution.py:35
  116.4 15.0 %collective-permute-start.17 = (f32[128,1024]{1,0:T(8,128)}, f32[128,1024]{1,0:T(8,128)}, u32[]{:S(2)}, u32[]{:S(2)}) collective-permute-start(f32[128,1024]{1,0:T(8,128)} %slice.18), channel_id=1, source_target_pairs={{0,64},{64,128},{128,192},{192,0},{1,65},{65,129},{129,193},{193,1... | collective-permute-start | bytes 1572872 | tf_op jit(solution)/shard_map/ppermute | solution.py:357
  116.4 17.7 %collective-permute-start.16 = (f32[256,1024]{1,0:T(8,128)}, f32[256,1024]{1,0:T(8,128)}, u32[]{:S(2)}, u32[]{:S(2)}) collective-permute-start(f32[256,1024]{1,0:T(8,128)} %collective-permute-done.15.refs_2_.refs_8_), channel_id=1, source_target_pairs={{0,1},{1,0},{2,3},{3,2},{4,5},{5,4},{6,7},{7,6},{8,9},{9,8},{10,11... | collective-permute-start | bytes 3145736 | tf_op jit(solution)/shard_map/ppermute | solution.py:35
  117.2 21.0 %all-to-all-start.3 = ((f32[32,24,128]{2,1,0:T(8,128)}), f32[32,24,128]{2,1,0:T(8,128)S(1)}, u32[]{:S(2)}, u32[]{:S(2)}) async-start(f32[32,24,128]{2,1,0:T(8,128)} %shard_map.55), calls=%async_computation.3 | async-start | bytes 786432 | tf_op jit(solution)/shard_map/all_to_all | solution.py:361
  126.4 11.8 %copy-start.3 = (f32[128,1024]{1,0:T(8,128)}, f32[128,1024]{1,0:T(8,128)S(1)}, u32[]{:S(2)}) copy-start(f32[128,1024]{1,0:T(8,128)S(1)} %collective-permute-done.19.refs_5_.refs_11_) | copy-start | bytes 1572868
  126.4 5.8 %collective-permute-start.21 = (f32[128,1024]{1,0:T(8,128)S(1)}, f32[128,1024]{1,0:T(8,128)}, u32[]{:S(2)}, u32[]{:S(2)}) collective-permute-start(f32[128,1024]{1,0:T(8,128)S(1)} %collective-permute-done.19.refs_5_.refs_11_), channel_id=1, source_target_pairs={{0,1},{1,0},{2,3},{3,2},{4,5},{5,4},{6,7},{7,6},{8,9},{9,8},{10,11... | collective-permute-start | bytes 1572872 | tf_op jit(solution)/shard_map/ppermute | solution.py:35
  131.4 2.7 %collective-permute-start.20 = (f32[128,1024]{1,0:T(8,128)}, f32[128,1024]{1,0:T(8,128)}, u32[]{:S(2)}, u32[]{:S(2)}) collective-permute-start(f32[128,1024]{1,0:T(8,128)} %collective-permute-done.17.refs_4_.refs_10_), channel_id=1, source_target_pairs={{0,1},{1,0},{2,3},{3,2},{4,5},{5,4},{6,7},{7,6},{8,9},{9,8},{10,11... | collective-permute-start | bytes 1572872 | tf_op jit(solution)/shard_map/ppermute | solution.py:35
  160.5 18.3 %all-to-all-start.5 = ((f32[32,24,128]{2,1,0:T(8,128)}), f32[32,24,128]{2,1,0:T(8,128)S(1)}, u32[]{:S(2)}, u32[]{:S(2)}) async-start(f32[32,24,128]{2,1,0:T(8,128)} %shard_map.57), calls=%async_computation.5 | async-start | bytes 786432 | tf_op jit(solution)/shard_map/all_to_all | solution.py:361
  200.2 17.5 %all-to-all-start.7 = ((f32[32,24,128]{2,1,0:T(8,128)}), f32[32,24,128]{2,1,0:T(8,128)S(1)}, u32[]{:S(2)}, u32[]{:S(2)}) async-start(f32[32,24,128]{2,1,0:T(8,128)} %shard_map.59), calls=%async_computation.7 | async-start | bytes 786432 | tf_op jit(solution)/shard_map/all_to_all | solution.py:361
